TPU v7x, 512 devices: a whole 4x8x8 slice. The times are simulated.
512 devices in a mesh: seq: 64 (over z, x, core), fsdp: 8 (over y).
Axes of the slice: x: 4, y: 8, z: 8, core: 2. Of those that a mesh axis runs over, the one named last changes fastest.
Arguments:
- queries: bfloat16 [8, 8192, 1536], P('fsdp', 'seq'), may hold values from -6 to 6
- keys: bfloat16 [8, 8192, 1536], P('fsdp', 'seq'), may hold values from -6 to 6
- values: bfloat16 [8, 8192, 1536], P('fsdp', 'seq'), may hold values from -27.2 to 27.2
- lengths: int32 [8, 16], P('fsdp'), may hold values from 1 to 1024, 8192 in all within a row
- gain: float32 [1536], replicated, may hold values from 0.5 to 2
- out_weight: bfloat16 [1536, 2048], P('fsdp'), may hold values from -0.15625 to 0.15625
- cotangent: bfloat16 [8, 8192, 2048], P('fsdp', 'seq'), may hold values from -6 to 6
Outputs:
- output: bfloat16 [8, 8192, 2048], P('fsdp', 'seq')
- grad_queries: bfloat16 [8, 8192, 1536], P('fsdp', 'seq')
- grad_keys: bfloat16 [8, 8192, 1536], P('fsdp', 'seq')
- grad_values: bfloat16 [8, 8192, 1536], P('fsdp', 'seq')
Inputs may be any that keep to these rules, and one draw needn't show every extreme that they name: Each row holds the lengths of the documents packed into one sequence, in order; a row sums to 8192 and its longest document has exactly 1024 positions.
All inputs are finite; a program needn't handle non-finite values.
Results may differ from a plain program's by a relative error of at most 0.012.
Values may be sent and summed in bfloat16 or wider, within the bound.
No kernel may reach another device: no remote copies, remote signals or barrier semaphores. Data moves between devices by JAX's collectives and lax.ppermute only.
A program may use at most 128 MiB of HBM per device.

v0:
```python
import jax
import jax.numpy as jnp
from jax import lax
from jax.sharding import PartitionSpec as P

HEADS = 12
HEAD_DIM = 128


epsilon = 1.0


def from_behind(block, axis, distance):
    devices = range(lax.axis_size(axis))
    route = [(i - distance, i) for i in devices if i - distance in devices]
    return lax.ppermute(block, axis, route)


def shortened(value):
    return jax.tree.map(lambda a: a.astype(jnp.bfloat16) if a.dtype == jnp.float32 else a, value)


def doc_index(doc_ends, positions):
    return jnp.sum((doc_ends[None, :] <= positions[:, None]).astype(jnp.int32), axis=1)


def combine_pair(earlier, later):
    return (jnp.maximum(earlier[0], later[0]), later[1] + (1.0 - later[0]) * earlier[1])


def window_forward(element, span_blocks):
    levels = (span_blocks - 1).bit_length()
    amounts = [1] + [2**level for level in range(levels)]
    current = element
    for number, amount in enumerate(amounts):
        shifted = from_behind((current[0], current[1]), "seq", amount)
        current = shifted if number == 0 else combine_pair(shifted, current)
    return current


def window_backward(element, span_blocks):
    levels = (span_blocks - 1).bit_length()
    amounts = [1] + [2**level for level in range(levels)]
    current = element
    for number, amount in enumerate(amounts):
        shifted = from_behind((shortened(current[0]), shortened(current[1])), "seq", -amount)
        current = shifted if number == 0 else combine_pair(shifted, current)
    return current


def on_device(queries, keys, values, lengths, gain, out_weight, cotangent):
    tokens = queries.shape[1]
    inner = queries.shape[2]
    query_heads = queries[0].reshape(tokens, HEADS, HEAD_DIM)
    key_heads = keys[0].reshape(tokens, HEADS, HEAD_DIM)
    value_heads = values[0].reshape(tokens, HEADS, HEAD_DIM)
    cotangent_rows = cotangent[0]
    block_start = lax.axis_index("seq") * tokens
    offsets = jnp.arange(tokens, dtype=jnp.int32)
    doc_ends = jnp.cumsum(lengths[0])
    doc_ids = doc_index(doc_ends, block_start + offsets)
    border = doc_index(doc_ends, jnp.stack([block_start - 1, block_start + tokens]))
    doc_before = border[0]
    doc_after = border[1]
    doc_first = doc_ids[0]
    doc_last = doc_ids[tokens - 1]
    causal = offsets[:, None] >= offsets[None, :]
    same_doc = causal & (doc_ids[:, None] == doc_ids[None, :])
    longest = 2 * lax.axis_size("seq") * tokens // lengths.shape[1]
    chain_span = longest // tokens + 1
    scores = jnp.einsum("thd,shd->hts", query_heads, key_heads, preferred_element_type=jnp.float32)
    attn_low = jnp.where(same_doc[None], scores, 0.0).astype(jnp.bfloat16)
    tail_values = jnp.where((doc_ids == doc_last)[:, None, None], value_heads, 0)
    local_fwd = jnp.einsum(
        "shd,she->hde", key_heads, tail_values, preferred_element_type=jnp.float32
    )
    reset_fwd = jnp.where(doc_last != doc_before, 1.0, 0.0).astype(jnp.float32)
    state_in = window_forward((reset_fwd, local_fwd), chain_span)[1]
    inside = jnp.einsum("hts,shd->thd", attn_low, value_heads, preferred_element_type=jnp.float32)
    state_low = state_in.astype(jnp.bfloat16)
    carry_rows = (doc_ids == doc_before)[:, None, None]
    after_rows = (doc_ids == doc_after)[:, None, None]
    carried = jnp.einsum("thd,hde->the", query_heads, state_low, preferred_element_type=jnp.float32)
    mixed = inside + jnp.where(carry_rows, carried, 0.0)
    inv_rms = lax.rsqrt(jnp.mean(mixed * mixed, axis=-1, keepdims=True) + epsilon)
    normed = mixed * inv_rms
    gain_heads = gain.reshape(HEADS, HEAD_DIM)
    scaled = (normed * gain_heads).astype(jnp.bfloat16).reshape(tokens, inner)
    contract_last = (((1,), (1,)), ((), ()))
    full_weight = lax.all_gather(out_weight, "fsdp", axis=0, tiled=True)
    output_sum = jnp.dot(scaled, full_weight, preferred_element_type=jnp.float32)
    grad_scaled = lax.dot_general(
        cotangent_rows, full_weight, contract_last, preferred_element_type=jnp.float32
    )
    output = output_sum.astype(jnp.bfloat16)
    grad_norm = grad_scaled.reshape(tokens, HEADS, HEAD_DIM) * gain_heads
    grad_mixed = inv_rms * (
        grad_norm - normed * jnp.mean(grad_norm * normed, axis=-1, keepdims=True)
    )
    grad_low = grad_mixed.astype(jnp.bfloat16)
    head_queries = jnp.where((doc_ids == doc_first)[:, None, None], query_heads, 0)
    local_back = jnp.einsum(
        "thd,the->hde", head_queries, grad_low, preferred_element_type=jnp.float32
    )
    reset_back = jnp.where(doc_first != doc_after, 1.0, 0.0).astype(jnp.float32)
    back_in = window_backward((reset_back, local_back), chain_span)[1]
    grad_scores = jnp.einsum(
        "thd,shd->hts", grad_low, value_heads, preferred_element_type=jnp.float32
    )
    grad_attn = jnp.where(same_doc[None], grad_scores, 0.0).astype(jnp.bfloat16)
    back_low = back_in.astype(jnp.bfloat16)
    grad_query = jnp.einsum(
        "hts,shd->thd", grad_attn, key_heads, preferred_element_type=jnp.float32
    )
    grad_query = grad_query + jnp.where(
        carry_rows,
        jnp.einsum("the,hde->thd", grad_low, state_low, preferred_element_type=jnp.float32),
        0.0,
    )
    grad_key = jnp.einsum(
        "hts,thd->shd", grad_attn, query_heads, preferred_element_type=jnp.float32
    )
    grad_key = grad_key + jnp.where(
        after_rows,
        jnp.einsum("she,hde->shd", value_heads, back_low, preferred_element_type=jnp.float32),
        0.0,
    )
    grad_value = jnp.einsum("hts,thd->shd", attn_low, grad_low, preferred_element_type=jnp.float32)
    grad_value = grad_value + jnp.where(
        after_rows,
        jnp.einsum("shd,hde->she", key_heads, back_low, preferred_element_type=jnp.float32),
        0.0,
    )
    grad_queries = grad_query.astype(jnp.bfloat16).reshape(1, tokens, inner)
    grad_keys = grad_key.astype(jnp.bfloat16).reshape(1, tokens, inner)
    grad_values = grad_value.astype(jnp.bfloat16).reshape(1, tokens, inner)
    return (output.reshape(1, tokens, output.shape[1]), grad_queries, grad_keys, grad_values)


def solution(mesh):
    placed = (
        P("fsdp", "seq", None),
        P("fsdp", "seq", None),
        P("fsdp", "seq", None),
        P("fsdp", None),
        P(),
        P("fsdp", None),
        P("fsdp", "seq", None),
    )
    return jax.shard_map(
        on_device,
        mesh=mesh,
        in_specs=placed,
        out_specs=(
            P("fsdp", "seq", None),
            P("fsdp", "seq", None),
            P("fsdp", "seq", None),
            P("fsdp", "seq", None),
        ),
        check_vma=False,
    )
```

profile of v0, /device:TPU:223, one launch (start us, length us, event | category | flops | bytes accessed | tf_op | source)
XLA Modules:
  0.0 230.6 jit_solution(9101523186275680919)
XLA Ops:
  7.9 1.2 copy.53
  10.0 1.2 copy.56
  12.8 2.6 %broadcast_compare_fusion = (pred[128]{0:T(512)(128)(4,1)S(1)}, pred[128]{0:T(512)(128)(4,1)S(1)}, pred[128]{0:T(512)(128)(4,1)S(1)}, pred[128]{0:T(512)(128)(4,1)S(1)}) fusion(s32[128]{0:T(128)S(1)} %convert_reduce_fusion, s32[]{:T(128)} %bitcast.22, s32[]{:T(128)} %bitcast.21, s32[]{:T(128)} %bitcast.8, s32[]{:T(128)} %bitcast.7), kind=kLoop, calls=%fused_computation.54 | loop fusion | flops 512 | bytes 1040 | tf_op jit(solution)/shard_map/eq | solution.py:101
  15.8 5.7 %collective-permute-start = (f32[12,128,128]{1,2,0:T(8,128)S(1)}, f32[12,128,128]{1,2,0:T(8,128)S(1)}, u32[]{:S(2)}, u32[]{:S(2)}) collective-permute-start(f32[12,128,128]{1,2,0:T(8,128)S(1)} %convolution_bitcast_fusion.2), channel_id=1, source_target_pairs={{0,8},{8,16},{16,24},{24,32},{32,40},{40,48},{48,56},{56,64},{64,7... | collective-permute-start | bytes 2359304 | tf_op jit(solution)/shard_map/ppermute | solution.py:16
  21.5 8.9 %collective-permute-done = f32[12,128,128]{1,2,0:T(8,128)S(1)} collective-permute-done((f32[12,128,128]{1,2,0:T(8,128)S(1)}, f32[12,128,128]{1,2,0:T(8,128)S(1)}, u32[]{:S(2)}, u32[]{:S(2)}) %collective-permute-start) | collective-permute-done | bytes 786464 | tf_op jit(solution)/shard_map/ppermute | solution.py:16
  30.4 7.7 %collective-permute-start.2 = (f32[12,128,128]{1,2,0:T(8,128)S(1)}, f32[12,128,128]{1,2,0:T(8,128)}, u32[]{:S(2)}, u32[]{:S(2)}) collective-permute-start(f32[12,128,128]{1,2,0:T(8,128)S(1)} %collective-permute-done), channel_id=1, source_target_pairs={{0,8},{8,16},{16,24},{24,32},{32,40},{40,48},{48,56},{56,64},{64,7... | collective-permute-start | bytes 2359304 | tf_op jit(solution)/shard_map/ppermute | solution.py:16
  39.4 7.7 %collective-permute-start.1 = (f32[]{:T(128)}, f32[]{:T(128)}, u32[]{:S(2)}, u32[]{:S(2)}) collective-permute-start(f32[]{:T(128)} %select_n.46), channel_id=1, source_target_pairs={{0,8},{8,16},{16,24},{24,32},{32,40},{40,48},{48,56},{56,64},{64,7... | collective-permute-start | bytes 20 | tf_op jit(solution)/shard_map/ppermute | solution.py:16
  47.7 1.2 multiply_add_fusion.2
  48.9 1.9 collective-permute-start.4
  50.8 7.9 %collective-permute-start.3 = (f32[]{:T(128)}, f32[]{:T(128)}, u32[]{:S(2)}, u32[]{:S(2)}) collective-permute-start(f32[]{:T(128)} %collective-permute-done.1), channel_id=1, source_target_pairs={{0,8},{8,16},{16,24},{24,32},{32,40},{40,48},{48,56},{56,64},{64,7... | collective-permute-start | bytes 20 | tf_op jit(solution)/shard_map/ppermute | solution.py:16
  58.7 3.0 %collective-permute-done.3 = f32[]{:T(128)} collective-permute-done((f32[]{:T(128)}, f32[]{:T(128)}, u32[]{:S(2)}, u32[]{:S(2)}) %collective-permute-start.3) | collective-permute-done | bytes 36 | tf_op jit(solution)/shard_map/ppermute | solution.py:16
  62.9 4.3 %collective-permute-done.4 = f32[12,128,128]{1,2,0:T(8,128)} collective-permute-done((f32[12,128,128]{1,2,0:T(8,128)S(1)}, f32[12,128,128]{1,2,0:T(8,128)}, u32[]{:S(2)}, u32[]{:S(2)}) %collective-permute-start.4) | collective-permute-done | bytes 786464 | tf_op jit(solution)/shard_map/ppermute | solution.py:16
  67.2 1.2 multiply_add_fusion.1
  68.4 1.9 collective-permute-start.6
  70.3 14.4 %collective-permute-start.5 = (f32[]{:T(128)}, f32[]{:T(128)}, u32[]{:S(2)}, u32[]{:S(2)}) collective-permute-start(f32[]{:T(128)} %max.18), channel_id=1, source_target_pairs={{0,16},{8,24},{16,32},{24,40},{32,48},{40,56},{48,64},{56,72},{64,... | collective-permute-start | bytes 20 | tf_op jit(solution)/shard_map/ppermute | solution.py:16
  85.4 3.9 %collective-permute-done.6 = f32[12,128,128]{1,2,0:T(8,128)S(1)} collective-permute-done((f32[12,128,128]{1,2,0:T(8,128)S(1)}, f32[12,128,128]{1,2,0:T(8,128)S(1)}, u32[]{:S(2)}, u32[]{:S(2)}) %collective-permute-start.6) | collective-permute-done | bytes 786464 | tf_op jit(solution)/shard_map/ppermute | solution.py:16
  89.3 1.0 multiply_add_fusion
  90.2 5.2 %collective-permute-start.8 = (f32[12,128,128]{1,2,0:T(8,128)}, f32[12,128,128]{1,2,0:T(8,128)S(1)}, u32[]{:S(2)}, u32[]{:S(2)}) collective-permute-start(f32[12,128,128]{1,2,0:T(8,128)} %multiply_add_fusion), channel_id=1, source_target_pairs={{0,64},{8,72},{16,80},{24,88},{32,96},{40,104},{48,112},{56,120},{... | collective-permute-start | bytes 2359304 | tf_op jit(solution)/shard_map/ppermute | solution.py:16
  95.5 1.2 copy.52
  97.1 1.3 convolution_bitcast_fusion.3
  98.4 11.8 %collective-permute-start.7 = (f32[]{:T(128)}, f32[]{:T(128)}, u32[]{:S(2)}, u32[]{:S(2)}) collective-permute-start(f32[]{:T(128)} %max.19), channel_id=1, source_target_pairs={{0,32},{8,40},{16,48},{24,56},{32,64},{40,72},{48,80},{56,88},{64,... | collective-permute-start | bytes 20 | tf_op jit(solution)/shard_map/ppermute | solution.py:16
  110.8 1.2 add_convert_fusion
  112.0 1.6 multiply_reduce_fusion.1
  113.7 4.6 %multiply_reduce_fusion = (f32[128,12]{0,1:T(8,128)S(1)}, f32[128,12,128]{0,2,1:T(8,128)S(1)}) fusion(f32[128,12,128]{0,2,1:T(8,128)S(1)} %get-tuple-element.27, f32[128,12]{0,1:T(8,128)S(1)} %add_rsqrt_fusion, f32[12,128]{1,0:T(8,128)S(1)} %bitcast.90, bf16[12,128,2048]{2,1,0:T(8,128)(2,1)} %bitcast.73, bf16[1,128,2048]{2,1,0:T(8,128)(2,1)S(1)} %copy-done), kind=kOutput, calls=%fused_computation.27 | convolution fusion | flops 806091264 | bytes 8407040 | tf_op jit(solution)/shard_map/dot_general | solution.py:92
  118.3 1.1 multiply_convert_fusion
  119.8 5.2 %collective-permute-start.9 = (bf16[12,128,128]{2,1,0:T(8,128)(2,1)S(1)}, bf16[12,128,128]{2,1,0:T(8,128)(2,1)S(1)}, u32[]{:S(2)}, u32[]{:S(2)}) collective-permute-start(bf16[12,128,128]{2,1,0:T(8,128)(2,1)S(1)} %convolution_convert_fusion.1), channel_id=1, source_target_pairs={{8,0},{16,8},{24,16},{32,24},{40,32},{48,40},{56,48},{64,56},{72,6... | collective-permute-start | bytes 1179656 | tf_op jit(solution)/shard_map/ppermute | solution.py:16
  125.0 11.6 %collective-permute-done.9 = bf16[12,128,128]{2,1,0:T(8,128)(2,1)S(1)} collective-permute-done((bf16[12,128,128]{2,1,0:T(8,128)(2,1)S(1)}, bf16[12,128,128]{2,1,0:T(8,128)(2,1)S(1)}, u32[]{:S(2)}, u32[]{:S(2)}) %collective-permute-start.9) | collective-permute-done | bytes 393248 | tf_op jit(solution)/shard_map/ppermute | solution.py:16
  136.6 1.9 collective-permute-start.11
  139.8 2.7 %collective-permute-start.10 = (bf16[]{:T(256)}, bf16[]{:T(256)}, u32[]{:S(2)}, u32[]{:S(2)}) collective-permute-start(bf16[]{:T(256)} %select_n.53), channel_id=1, source_target_pairs={{8,0},{16,8},{24,16},{32,24},{40,32},{48,40},{56,48},{64,56},{72,6... | collective-permute-start | bytes 14 | tf_op jit(solution)/shard_map/ppermute | solution.py:16
  142.6 6.6 %collective-permute-done.10 = bf16[]{:T(256)} collective-permute-done((bf16[]{:T(256)}, bf16[]{:T(256)}, u32[]{:S(2)}, u32[]{:S(2)}) %collective-permute-start.10) | collective-permute-done | bytes 34 | tf_op jit(solution)/shard_map/ppermute | solution.py:16
  149.1 1.9 collective-permute-start.12
  151.8 5.6 %collective-permute-done.12 = bf16[]{:T(256)} collective-permute-done((bf16[]{:T(256)}, bf16[]{:T(256)}, u32[]{:S(2)}, u32[]{:S(2)}) %collective-permute-start.12) | collective-permute-done | bytes 34 | tf_op jit(solution)/shard_map/ppermute | solution.py:16
  158.6 2.6 %collective-permute-start.14 = (bf16[]{:T(256)}, bf16[]{:T(256)}, u32[]{:S(2)}, u32[]{:S(2)}) collective-permute-start(bf16[]{:T(256)} %max.21), channel_id=1, source_target_pairs={{16,0},{24,8},{32,16},{40,24},{48,32},{56,40},{64,48},{72,56},{80,... | collective-permute-start | bytes 14 | tf_op jit(solution)/shard_map/ppermute | solution.py:16
  161.3 5.1 %collective-permute-done.14 = bf16[]{:T(256)} collective-permute-done((bf16[]{:T(256)}, bf16[]{:T(256)}, u32[]{:S(2)}, u32[]{:S(2)}) %collective-permute-start.14) | collective-permute-done | bytes 34 | tf_op jit(solution)/shard_map/ppermute | solution.py:16
  167.1 2.6 %collective-permute-start.16 = (bf16[]{:T(256)}, bf16[]{:T(256)}, u32[]{:S(2)}, u32[]{:S(2)}) collective-permute-start(bf16[]{:T(256)} %max.22), channel_id=1, source_target_pairs={{32,0},{40,8},{48,16},{56,24},{64,32},{72,40},{80,48},{88,56},{96,... | collective-permute-start | bytes 14 | tf_op jit(solution)/shard_map/ppermute | solution.py:16
  169.7 5.4 %collective-permute-done.16 = bf16[]{:T(256)} collective-permute-done((bf16[]{:T(256)}, bf16[]{:T(256)}, u32[]{:S(2)}, u32[]{:S(2)}) %collective-permute-start.16) | collective-permute-done | bytes 34 | tf_op jit(solution)/shard_map/ppermute | solution.py:16
  176.2 1.9 collective-permute-start.13
  178.5 1.3 fusion.12
  179.9 10.0 %collective-permute-done.13 = bf16[12,128,128]{2,1,0:T(8,128)(2,1)S(1)} collective-permute-done((bf16[12,128,128]{2,1,0:T(8,128)(2,1)S(1)}, bf16[12,128,128]{2,1,0:T(8,128)(2,1)S(1)}, u32[]{:S(2)}, u32[]{:S(2)}) %collective-permute-start.13) | collective-permute-done | bytes 393248 | tf_op jit(solution)/shard_map/ppermute | solution.py:16
  190.7 1.9 collective-permute-start.15
  192.6 1.2 convolution_bitcast_fusion
  194.9 11.1 %collective-permute-done.15 = bf16[12,128,128]{2,1,0:T(8,128)(2,1)} collective-permute-done((bf16[12,128,128]{2,1,0:T(8,128)(2,1)}, bf16[12,128,128]{2,1,0:T(8,128)(2,1)}, u32[]{:S(2)}, u32[]{:S(2)}) %collective-permute-start.15) | collective-permute-done | bytes 393248 | tf_op jit(solution)/shard_map/ppermute | solution.py:16
  206.1 1.2 multiply_add_fusion.4
  207.2 1.9 collective-permute-start.17
  209.2 4.7 %fusion = bf16[1,128,2048]{2,1,0:T(8,128)(2,1)} fusion(bf16[128,1536]{0,1:T(8,128)(2,1)} %bitcast.86, bf16[1536,2048]{1,0:T(8,128)(2,1)} %all-gather.2.cloned.1.call-done), kind=kOutput, calls=%fused_computation.1 | convolution fusion | flops 805568512 | bytes 7208960 | tf_op jit(solution)/shard_map/dot_general | solution.py:91
  213.9 7.4 %collective-permute-done.17 = bf16[12,128,128]{2,1,0:T(8,128)(2,1)S(1)} collective-permute-done((bf16[12,128,128]{2,1,0:T(8,128)(2,1)S(1)}, bf16[12,128,128]{2,1,0:T(8,128)(2,1)S(1)}, u32[]{:S(2)}, u32[]{:S(2)}) %collective-permute-start.17) | collective-permute-done | bytes 393248 | tf_op jit(solution)/shard_map/ppermute | solution.py:16
  221.5 0.9 copy.68
  222.8 0.9 copy.69
  (40 shorter events, 7.7 us)
Async XLA Ops:
  7.2 106.5 %copy-start = (bf16[1,128,2048]{2,1,0:T(8,128)(2,1)S(1)}, bf16[1,128,2048]{2,1,0:T(8,128)(2,1)}, u32[]{:S(2)}) copy-start(bf16[1,128,2048]{2,1,0:T(8,128)(2,1)} %param.13) | copy-start | bytes 1572868
  7.2 106.5 %all-gather.2.cloned.1.call-start = ((), (), s32[]{:S(2)}) async-start(), calls=%async_computation | async-start | bytes 7077888 | tf_op jit(solution)/shard_map/all_gather | solution.py:90
  15.8 14.6 %collective-permute-start = (f32[12,128,128]{1,2,0:T(8,128)S(1)}, f32[12,128,128]{1,2,0:T(8,128)S(1)}, u32[]{:S(2)}, u32[]{:S(2)}) collective-permute-start(f32[12,128,128]{1,2,0:T(8,128)S(1)} %convolution_bitcast_fusion.2), channel_id=1, source_target_pairs={{0,8},{8,16},{16,24},{24,32},{32,40},{40,48},{48,56},{56,64},{64,7... | collective-permute-start | bytes 2359304 | tf_op jit(solution)/shard_map/ppermute | solution.py:16
  30.4 17.3 %collective-permute-start.2 = (f32[12,128,128]{1,2,0:T(8,128)S(1)}, f32[12,128,128]{1,2,0:T(8,128)}, u32[]{:S(2)}, u32[]{:S(2)}) collective-permute-start(f32[12,128,128]{1,2,0:T(8,128)S(1)} %collective-permute-done), channel_id=1, source_target_pairs={{0,8},{8,16},{16,24},{24,32},{32,40},{40,48},{48,56},{56,64},{64,7... | collective-permute-start | bytes 2359304 | tf_op jit(solution)/shard_map/ppermute | solution.py:16
  39.4 7.7 %collective-permute-start.1 = (f32[]{:T(128)}, f32[]{:T(128)}, u32[]{:S(2)}, u32[]{:S(2)}) collective-permute-start(f32[]{:T(128)} %select_n.46), channel_id=1, source_target_pairs={{0,8},{8,16},{16,24},{24,32},{32,40},{40,48},{48,56},{56,64},{64,7... | collective-permute-start | bytes 20 | tf_op jit(solution)/shard_map/ppermute | solution.py:16
  48.9 18.2 %collective-permute-start.4 = (f32[12,128,128]{1,2,0:T(8,128)S(1)}, f32[12,128,128]{1,2,0:T(8,128)}, u32[]{:S(2)}, u32[]{:S(2)}) collective-permute-start(f32[12,128,128]{1,2,0:T(8,128)S(1)} %multiply_add_fusion.2), channel_id=1, source_target_pairs={{0,16},{8,24},{16,32},{24,40},{32,48},{40,56},{48,64},{56,72},{64,... | collective-permute-start | bytes 2359304 | tf_op jit(solution)/shard_map/ppermute | solution.py:16
  50.8 10.9 %collective-permute-start.3 = (f32[]{:T(128)}, f32[]{:T(128)}, u32[]{:S(2)}, u32[]{:S(2)}) collective-permute-start(f32[]{:T(128)} %collective-permute-done.1), channel_id=1, source_target_pairs={{0,8},{8,16},{16,24},{24,32},{32,40},{40,48},{48,56},{56,64},{64,7... | collective-permute-start | bytes 20 | tf_op jit(solution)/shard_map/ppermute | solution.py:16
  62.9 50.8 %copy-start.3 = (f32[1536]{0:T(1024)S(1)}, f32[1536]{0:T(1024)}, u32[]{:S(2)}) copy-start(f32[1536]{0:T(1024)} %param.11) | copy-start | bytes 18436
  68.4 20.9 %collective-permute-start.6 = (f32[12,128,128]{1,2,0:T(8,128)S(1)}, f32[12,128,128]{1,2,0:T(8,128)S(1)}, u32[]{:S(2)}, u32[]{:S(2)}) collective-permute-start(f32[12,128,128]{1,2,0:T(8,128)S(1)} %multiply_add_fusion.1), channel_id=1, source_target_pairs={{0,32},{8,40},{16,48},{24,56},{32,64},{40,72},{48,80},{56,88},{64,... | collective-permute-start | bytes 2359304 | tf_op jit(solution)/shard_map/ppermute | solution.py:16
  70.3 14.4 %collective-permute-start.5 = (f32[]{:T(128)}, f32[]{:T(128)}, u32[]{:S(2)}, u32[]{:S(2)}) collective-permute-start(f32[]{:T(128)} %max.18), channel_id=1, source_target_pairs={{0,16},{8,24},{16,32},{24,40},{32,48},{40,56},{48,64},{56,72},{64,... | collective-permute-start | bytes 20 | tf_op jit(solution)/shard_map/ppermute | solution.py:16
  90.2 20.6 %collective-permute-start.8 = (f32[12,128,128]{1,2,0:T(8,128)}, f32[12,128,128]{1,2,0:T(8,128)S(1)}, u32[]{:S(2)}, u32[]{:S(2)}) collective-permute-start(f32[12,128,128]{1,2,0:T(8,128)} %multiply_add_fusion), channel_id=1, source_target_pairs={{0,64},{8,72},{16,80},{24,88},{32,96},{40,104},{48,112},{56,120},{... | collective-permute-start | bytes 2359304 | tf_op jit(solution)/shard_map/ppermute | solution.py:16
  98.4 11.8 %collective-permute-start.7 = (f32[]{:T(128)}, f32[]{:T(128)}, u32[]{:S(2)}, u32[]{:S(2)}) collective-permute-start(f32[]{:T(128)} %max.19), channel_id=1, source_target_pairs={{0,32},{8,40},{16,48},{24,56},{32,64},{40,72},{48,80},{56,88},{64,... | collective-permute-start | bytes 20 | tf_op jit(solution)/shard_map/ppermute | solution.py:16
  112.0 6.3 %copy-start.1 = (bf16[12,128,128]{1,2,0:T(8,128)(2,1)}, bf16[12,128,128]{1,2,0:T(8,128)(2,1)S(1)}, u32[]{:S(2)}) copy-start(bf16[12,128,128]{1,2,0:T(8,128)(2,1)S(1)} %add_convert_fusion) | copy-start | bytes 1179652
  119.8 16.8 %collective-permute-start.9 = (bf16[12,128,128]{2,1,0:T(8,128)(2,1)S(1)}, bf16[12,128,128]{2,1,0:T(8,128)(2,1)S(1)}, u32[]{:S(2)}, u32[]{:S(2)}) collective-permute-start(bf16[12,128,128]{2,1,0:T(8,128)(2,1)S(1)} %convolution_convert_fusion.1), channel_id=1, source_target_pairs={{8,0},{16,8},{24,16},{32,24},{40,32},{48,40},{56,48},{64,56},{72,6... | collective-permute-start | bytes 1179656 | tf_op jit(solution)/shard_map/ppermute | solution.py:16
  136.6 39.5 %collective-permute-start.11 = (bf16[12,128,128]{2,1,0:T(8,128)(2,1)S(1)}, bf16[12,128,128]{2,1,0:T(8,128)(2,1)S(1)}, u32[]{:S(2)}, u32[]{:S(2)}) collective-permute-start(bf16[12,128,128]{2,1,0:T(8,128)(2,1)S(1)} %collective-permute-done.9), channel_id=1, source_target_pairs={{8,0},{16,8},{24,16},{32,24},{40,32},{48,40},{56,48},{64,56},{72,6... | collective-permute-start | bytes 1179656 | tf_op jit(solution)/shard_map/ppermute | solution.py:16
  139.8 9.3 %collective-permute-start.10 = (bf16[]{:T(256)}, bf16[]{:T(256)}, u32[]{:S(2)}, u32[]{:S(2)}) collective-permute-start(bf16[]{:T(256)} %select_n.53), channel_id=1, source_target_pairs={{8,0},{16,8},{24,16},{32,24},{40,32},{48,40},{56,48},{64,56},{72,6... | collective-permute-start | bytes 14 | tf_op jit(solution)/shard_map/ppermute | solution.py:16
  149.1 8.2 %collective-permute-start.12 = (bf16[]{:T(256)}, bf16[]{:T(256)}, u32[]{:S(2)}, u32[]{:S(2)}) collective-permute-start(bf16[]{:T(256)} %collective-permute-done.10), channel_id=1, source_target_pairs={{8,0},{16,8},{24,16},{32,24},{40,32},{48,40},{56,48},{64,56},{72,6... | collective-permute-start | bytes 14 | tf_op jit(solution)/shard_map/ppermute | solution.py:16
  158.6 7.7 %collective-permute-start.14 = (bf16[]{:T(256)}, bf16[]{:T(256)}, u32[]{:S(2)}, u32[]{:S(2)}) collective-permute-start(bf16[]{:T(256)} %max.21), channel_id=1, source_target_pairs={{16,0},{24,8},{32,16},{40,24},{48,32},{56,40},{64,48},{72,56},{80,... | collective-permute-start | bytes 14 | tf_op jit(solution)/shard_map/ppermute | solution.py:16
  167.1 8.0 %collective-permute-start.16 = (bf16[]{:T(256)}, bf16[]{:T(256)}, u32[]{:S(2)}, u32[]{:S(2)}) collective-permute-start(bf16[]{:T(256)} %max.22), channel_id=1, source_target_pairs={{32,0},{40,8},{48,16},{56,24},{64,32},{72,40},{80,48},{88,56},{96,... | collective-permute-start | bytes 14 | tf_op jit(solution)/shard_map/ppermute | solution.py:16
  176.2 13.7 %collective-permute-start.13 = (bf16[12,128,128]{2,1,0:T(8,128)(2,1)S(1)}, bf16[12,128,128]{2,1,0:T(8,128)(2,1)S(1)}, u32[]{:S(2)}, u32[]{:S(2)}) collective-permute-start(bf16[12,128,128]{2,1,0:T(8,128)(2,1)S(1)} %multiply_add_fusion.6), channel_id=1, source_target_pairs={{16,0},{24,8},{32,16},{40,24},{48,32},{56,40},{64,48},{72,56},{80,... | collective-permute-start | bytes 1179656 | tf_op jit(solution)/shard_map/ppermute | solution.py:16
  190.7 15.4 %collective-permute-start.15 = (bf16[12,128,128]{2,1,0:T(8,128)(2,1)}, bf16[12,128,128]{2,1,0:T(8,128)(2,1)}, u32[]{:S(2)}, u32[]{:S(2)}) collective-permute-start(bf16[12,128,128]{2,1,0:T(8,128)(2,1)} %multiply_add_fusion.5), channel_id=1, source_target_pairs={{32,0},{40,8},{48,16},{56,24},{64,32},{72,40},{80,48},{88,56},{96,... | collective-permute-start | bytes 1179656 | tf_op jit(solution)/shard_map/ppermute | solution.py:16
  194.7 26.6 %copy-start.2 = (f32[128,12,128]{0,2,1:T(8,128)S(1)}, f32[128,12,128]{0,2,1:T(8,128)}, u32[]{:S(2)}) copy-start(f32[128,12,128]{0,2,1:T(8,128)} %convolution_bitcast_fusion) | copy-start | bytes 2359300
  207.2 14.0 %collective-permute-start.17 = (bf16[12,128,128]{2,1,0:T(8,128)(2,1)S(1)}, bf16[12,128,128]{2,1,0:T(8,128)(2,1)S(1)}, u32[]{:S(2)}, u32[]{:S(2)}) collective-permute-start(bf16[12,128,128]{2,1,0:T(8,128)(2,1)S(1)} %multiply_add_fusion.4), channel_id=1, source_target_pairs={{64,0},{72,8},{80,16},{88,24},{96,32},{104,40},{112,48},{120,56},{... | collective-permute-start | bytes 1179656 | tf_op jit(solution)/shard_map/ppermute | solution.py:16
Sparse Core Ops, SparseCore 0:
  10.1 78.5 all-gather.1
where the time goes:
time: 232 us; the launch traced here: 231 us
  starting transfers between devices  87 us (38%)
  waiting for transfers between devices  83.6 us (36%)
  between operations  23.5 us (10%)
  matrix products  17.3 us (7%)
  other arithmetic  10.9 us (5%)
  local copies, waits for them, and re-layouts  8.36 us (4%)
    ppermute x18, starting transfers between devices, from_behind(): return lax.ppermute(block, axis, route)  86.9 us
    ppermute x18, waiting for transfers between devices, from_behind(): return lax.ppermute(block, axis, route)  82.9 us
    unnamed x14, local copies, waits for them, and re-layouts  6.45 us
    add x6, other arithmetic, combine_pair(): later[1] + (1.0 - later[0]) * earlier[1]  5.4 us
    dot_general x1, matrix products, on_device(): jnp.dot(scaled, full_weight, preferred_element_type=jnp.float32)  4.74 us
  transfers between devices with their start and end apart: 19, of which 12 were waited for; matrix products, arithmetic and copies ran while one was open for 11% of the time, Pallas kernels for 0%

commit v1 on v0

v1 whole, which is shorter than its diff:
```python
import jax
import jax.numpy as jnp
from jax import lax
from jax.experimental import pallas as pl
from jax.experimental.pallas import tpu as pltpu
from jax.sharding import Mesh, PartitionSpec as P


HEADS = 12
HALF = 6
HEAD_DIM = 128
NDOCS = 16
TOK = 128
DI = HEADS * HEAD_DIM
D = 2048
CHIPS = 32
EPSILON = 1.0
F32 = jnp.float32
BF16 = jnp.bfloat16

CA, CB, MP, ME1, ME3, CS, ES, CR, ER = range(9)
BACK = 9
ROWS = 24

VMEM = pl.BlockSpec(memory_space=pltpu.VMEM)
SMEM = pl.BlockSpec(memory_space=pltpu.SMEM)


def params(mib=24):
    return pltpu.CompilerParams(vmem_limit_bytes=mib << 20)


def cost(flops, moved):
    return pl.CostEstimate(flops=flops, bytes_accessed=moved, transcendentals=0)


def chip_and_core():
    return lax.axis_index("z") * 4 + lax.axis_index("x"), lax.axis_index("core")


def running_ends(lengths_ref):
    ends, total = [], jnp.int32(0)
    for j in range(NDOCS):
        total = total + lengths_ref[0, j]
        ends.append(total)
    return ends


def last_end(ends, position):
    best = jnp.int32(-(1 << 30))
    for end in ends:
        best = jnp.where(end <= position, end, best)
    return best


def next_end(ends, position):
    best = jnp.int32(1 << 30)
    for end in reversed(ends):
        best = jnp.where(end > position, end, best)
    return best


def same(ends, early, late):
    return last_end(ends, late) <= early


def lanes(head):
    start = head * HEAD_DIM
    return pl.ds(start if isinstance(head, int) else pl.multiple_of(start, HEAD_DIM), HEAD_DIM)


def dot(a, b, contract):
    return lax.dot_general(a, b, ((contract[0], contract[1]), ((), ())), preferred_element_type=F32)


NN = ((1,), (0,))
NT = ((1,), (1,))
TN = ((0,), (0,))


def rows_of(start, width=HEAD_DIM):
    return start + lax.broadcasted_iota(jnp.int32, (TOK, width), 0)


def same_doc_mask(ends, start):
    rows = rows_of(start)
    columns = start + lax.broadcasted_iota(jnp.int32, (TOK, TOK), 1)
    first = jnp.full((TOK, TOK), -(1 << 30), jnp.int32)
    for end in ends:
        first = jnp.where(end <= rows, end, first)
    return (columns <= rows) & (columns >= first)


def local_state_kernel(lengths_ref, keys_ref, values_ref, keep_ref, give_ref, coef_ref):
    chip, core = chip_and_core()
    ends = running_ends(lengths_ref)
    start = (chip * 2 + core) * TOK
    tail = rows_of(start) >= last_end(ends, start + TOK - 1)
    for part, ref in ((0, keep_ref), (1, give_ref)):
        first = HALF * core if part == 0 else HALF * (1 - core)
        for j in range(HALF):
            span = lanes(first + j)
            tail_values = jnp.where(tail, values_ref[:, span], 0)
            ref[j] = dot(keys_ref[:, span], tail_values, TN).astype(BF16)
    base = chip * 2 * TOK
    one, zero = jnp.float32(1), jnp.float32(0)

    def flag(condition):
        return jnp.where(condition, one, zero)

    def put(row, value):
        coef_ref[row : row + 1, :] = jnp.full((1, 128), value, F32)

    low = core == 0
    inner = flag(same(ends, base + 127, base + 255))
    across = flag(same(ends, base - 1, base + 127))
    put(CA, jnp.where(low, inner, one))
    put(CB, jnp.where(low, one, inner))
    put(MP, flag((chip >= 1) & same(ends, base - 1, base + 255)))
    put(ME1, flag(chip >= 1))
    put(ME3, flag((chip >= 3) & same(ends, base - 513, base - 1)))
    put(CS, jnp.where(low, one, zero))
    put(ES, jnp.where(low, across, one))
    put(CR, jnp.where(low, zero, one))
    put(ER, jnp.where(low, one, across))
    inner = flag(same(ends, base, base + 128))
    across = flag(same(ends, base + 128, base + 256))
    put(BACK + CA, jnp.where(low, one, inner))
    put(BACK + CB, jnp.where(low, inner, one))
    put(BACK + MP, flag((chip <= CHIPS - 2) & same(ends, base, base + 256)))
    put(BACK + ME1, flag(chip <= CHIPS - 2))
    put(BACK + ME3, flag((chip <= CHIPS - 4) & same(ends, base + 256, base + 768)))
    put(BACK + CS, jnp.where(low, zero, one))
    put(BACK + ES, jnp.where(low, one, across))
    put(BACK + CR, jnp.where(low, one, zero))
    put(BACK + ER, jnp.where(low, across, one))
    for row in range(2 * BACK, ROWS):
        put(row, zero)


def local_state(lengths, keys, values):
    half = jax.ShapeDtypeStruct((HALF, HEAD_DIM, HEAD_DIM), BF16)
    return pl.pallas_call(
        local_state_kernel,
        out_shape=(half, half, jax.ShapeDtypeStruct((ROWS, 128), F32)),
        in_specs=[SMEM, VMEM, VMEM],
        out_specs=(VMEM, VMEM, VMEM),
        compiler_params=params(),
        cost_estimate=cost(50_000_000, 1_200_000),
        name="local_state",
    )(lengths, keys, values)


def inside_kernel(lengths_ref, queries_ref, keys_ref, values_ref, attn_ref, inside_ref):
    chip, core = chip_and_core()
    ends = running_ends(lengths_ref)
    start = (chip * 2 + core) * TOK
    mask = same_doc_mask(ends, start)
    for h in range(HEADS):
        span = lanes(h)
        scores = dot(queries_ref[:, span], keys_ref[:, span], NT)
        attn = jnp.where(mask, scores, 0.0).astype(BF16)
        attn_ref[h] = attn
        inside_ref[:, span] = dot(attn, values_ref[:, span], NN)


def inside_part(lengths, queries, keys, values):
    return pl.pallas_call(
        inside_kernel,
        out_shape=(
            jax.ShapeDtypeStruct((HEADS, TOK, TOK), BF16),
            jax.ShapeDtypeStruct((TOK, DI), F32),
        ),
        in_specs=[SMEM, VMEM, VMEM, VMEM],
        out_specs=(VMEM, VMEM),
        compiler_params=params(),
        cost_estimate=cost(100_000_000, 2_400_000),
        name="inside_part",
    )(lengths, queries, keys, values)


def mixed_kernel(lengths_ref, queries_ref, inside_ref, mine_ref, other_ref, gain_ref, mixed_ref, scaled_ref):
    chip, core = chip_and_core()
    ends = running_ends(lengths_ref)
    start = (chip * 2 + core) * TOK
    carry = rows_of(start) < next_end(ends, start - 1)
    for part, ref in ((0, mine_ref), (1, other_ref)):
        first = HALF * core if part == 0 else HALF * (1 - core)
        for j in range(HALF):
            span = lanes(first + j)
            carried = dot(queries_ref[:, span], ref[j], NN)
            mixed = inside_ref[:, span] + jnp.where(carry, carried, 0.0)
            mixed_ref[:, span] = mixed
            inv_rms = lax.rsqrt(jnp.mean(mixed * mixed, axis=-1, keepdims=True) + EPSILON)
            scaled_ref[:, span] = (mixed * inv_rms * gain_ref[:, span]).astype(BF16)


def mixed_part(lengths, queries, inside, mine, other, gain):
    return pl.pallas_call(
        mixed_kernel,
        out_shape=(jax.ShapeDtypeStruct((TOK, DI), F32), jax.ShapeDtypeStruct((TOK, DI), BF16)),
        in_specs=[SMEM, VMEM, VMEM, VMEM, VMEM, VMEM],
        out_specs=(VMEM, VMEM),
        compiler_params=params(),
        cost_estimate=cost(50_000_000, 2_700_000),
        name="mixed_part",
    )(lengths, queries, inside, mine, other, gain)


PAIR = 2 * HEAD_DIM


def grad_mixed_kernel(
    core_ref, lengths_ref, cot_ref, weight_ref, mixed_ref, gain_ref, queries_ref, low_ref, give_ref, keep_ref
):
    step = pl.program_id(0)
    chip, core = chip_and_core()
    ends = running_ends(lengths_ref)
    start = (chip * 2 + core) * TOK
    head_rows = rows_of(start) < next_end(ends, start)
    grad_scaled = dot(cot_ref[:, : D // 2], weight_ref[0], NT) + dot(cot_ref[:, D // 2 :], weight_ref[1], NT)
    states = []
    for j in range(2):
        span = lanes(j)
        mixed = mixed_ref[:, span]
        inv_rms = lax.rsqrt(jnp.mean(mixed * mixed, axis=-1, keepdims=True) + EPSILON)
        normed = mixed * inv_rms
        g = grad_scaled[:, j * HEAD_DIM : (j + 1) * HEAD_DIM] * gain_ref[:, span]
        low = (inv_rms * (g - normed * jnp.mean(g * normed, axis=-1, keepdims=True))).astype(BF16)
        low_ref[:, span] = low
        head_queries = jnp.where(head_rows, queries_ref[:, span], 0)
        states.append(dot(head_queries, low, TN).astype(BF16))

    @pl.when(step < 3)
    def _():
        give_ref[0] = states[0]
        give_ref[1] = states[1]

    @pl.when(step >= 3)
    def _():
        keep_ref[0] = states[0]
        keep_ref[1] = states[1]


def grad_mixed_part(core_index, lengths, cotangent, weight, mixed, gain, queries):
    def pair(i, core_ref):
        return lax.rem(i + 3 * (1 - core_ref[0]), 6)

    half = jax.ShapeDtypeStruct((HALF, HEAD_DIM, HEAD_DIM), BF16)
    return pl.pallas_call(
        grad_mixed_kernel,
        out_shape=(jax.ShapeDtypeStruct((TOK, DI), BF16), half, half),
        grid_spec=pltpu.PrefetchScalarGridSpec(
            num_scalar_prefetch=1,
            grid=(6,),
            in_specs=[
                SMEM,
                pl.BlockSpec((TOK, D), lambda i, c: (0, 0)),
                pl.BlockSpec((2, PAIR, D // 2), lambda i, c: (0, pair(i, c), 0)),
                pl.BlockSpec((TOK, PAIR), lambda i, c: (0, pair(i, c))),
                pl.BlockSpec((1, PAIR), lambda i, c: (0, pair(i, c))),
                pl.BlockSpec((TOK, PAIR), lambda i, c: (0, pair(i, c))),
            ],
            out_specs=(
                pl.BlockSpec((TOK, PAIR), lambda i, c: (0, pair(i, c))),
                pl.BlockSpec((2, HEAD_DIM, HEAD_DIM), lambda i, c: (jnp.minimum(i, 2), 0, 0)),
                pl.BlockSpec((2, HEAD_DIM, HEAD_DIM), lambda i, c: (jnp.maximum(i - 3, 0), 0, 0)),
            ),
        ),
        compiler_params=params(58),
        cost_estimate=cost(860_000_000, 9_000_000),
        name="grad_mixed_part",
    )(core_index, lengths, cotangent, weight, mixed, gain, queries)


def output_kernel(scaled_ref, weight_ref, output_ref):
    output_ref[...] = dot(scaled_ref[...], weight_ref[0], NN).astype(BF16)


def output_part(scaled, weight):
    width = 512
    per = D // 2 // width
    return pl.pallas_call(
        output_kernel,
        out_shape=jax.ShapeDtypeStruct((TOK, D), BF16),
        grid=(D // width,),
        in_specs=[
            pl.BlockSpec((TOK, DI), lambda i: (0, 0)),
            pl.BlockSpec((1, DI, width), lambda i: (i // per, 0, i % per)),
        ],
        out_specs=pl.BlockSpec((TOK, width), lambda i: (0, i)),
        compiler_params=params(58),
        cost_estimate=cost(810_000_000, 7_500_000),
        name="output_part",
    )(scaled, weight)


def grads_kernel(
    lengths_ref, queries_ref, keys_ref, values_ref, low_ref, attn_ref, mine_ref, other_ref,
    dq_ref, dk_ref, dv_ref,
):
    chip, core = chip_and_core()
    ends = running_ends(lengths_ref)
    start = (chip * 2 + core) * TOK
    mask = same_doc_mask(ends, start)
    carry = rows_of(start) < next_end(ends, start - 1)
    for part, ref in ((0, mine_ref), (1, other_ref)):
        first = HALF * core if part == 0 else HALF * (1 - core)
        for j in range(HALF):
            span = lanes(first + j)
            low = low_ref[:, span]
            queries = queries_ref[:, span]
            grad_attn = jnp.where(mask, dot(low, values_ref[:, span], NT), 0.0).astype(BF16)
            from_state = jnp.where(carry, dot(low, ref[j], NT), 0.0)
            dq_ref[:, span] = (dot(grad_attn, keys_ref[:, span], NN) + from_state).astype(BF16)
            dk_ref[:, span] = dot(grad_attn, queries, TN)
            dv_ref[:, span] = dot(attn_ref[first + j], low, TN)


def grads_part(lengths, queries, keys, values, low, attn, mine, other):
    full = jax.ShapeDtypeStruct((TOK, DI), F32)
    return pl.pallas_call(
        grads_kernel,
        out_shape=(jax.ShapeDtypeStruct((TOK, DI), BF16), full, full),
        in_specs=[SMEM] + [VMEM] * 7,
        out_specs=(VMEM,) * 3,
        compiler_params=params(),
        cost_estimate=cost(250_000_000, 5_000_000),
        name="grads_part",
    )(lengths, queries, keys, values, low, attn, mine, other)


def last_kernel(lengths_ref, keys_ref, values_ref, dk_part_ref, dv_part_ref, mine_ref, other_ref, dk_ref, dv_ref):
    chip, core = chip_and_core()
    ends = running_ends(lengths_ref)
    start = (chip * 2 + core) * TOK
    after = rows_of(start) >= last_end(ends, start + TOK)
    for part, ref in ((0, mine_ref), (1, other_ref)):
        first = HALF * core if part == 0 else HALF * (1 - core)
        for j in range(HALF):
            span = lanes(first + j)
            state = ref[j]
            from_keys = jnp.where(after, dot(values_ref[:, span], state, NT), 0.0)
            dk_ref[:, span] = (dk_part_ref[:, span] + from_keys).astype(BF16)
            from_values = jnp.where(after, dot(keys_ref[:, span], state, NN), 0.0)
            dv_ref[:, span] = (dv_part_ref[:, span] + from_values).astype(BF16)


def last_part(lengths, keys, values, dk, dv, mine, other):
    full = jax.ShapeDtypeStruct((TOK, DI), BF16)
    return pl.pallas_call(
        last_kernel,
        out_shape=(full, full),
        in_specs=[SMEM] + [VMEM] * 6,
        out_specs=(VMEM,) * 2,
        compiler_params=params(),
        cost_estimate=cost(100_000_000, 3_500_000),
        name="last_part",
    )(lengths, keys, values, dk, dv, mine, other)


def swap_cores(block):
    return lax.ppermute(block, "core", [(0, 1), (1, 0)])


def from_chip(block, distance):
    chips = range(CHIPS)
    pairs = [(2 * (i - distance) + c, 2 * i + c) for i in chips for c in range(2) if i - distance in chips]
    return lax.ppermute(block, ("z", "x", "core"), pairs)


def window(keep, give, coef, sign):
    def row(index):
        return coef[index + (0 if sign > 0 else BACK)]

    got = swap_cores(give).astype(F32)
    own = keep.astype(F32)
    chip_sum = (row(CA) * own + row(CB) * got).astype(BF16)
    before = from_chip(chip_sum, sign)
    pair_sum = (chip_sum.astype(F32) + row(MP) * before.astype(F32)).astype(BF16)
    near = from_chip(pair_sum, sign)
    far = from_chip(pair_sum, 3 * sign)
    enter = row(ME1) * near.astype(F32) + row(ME3) * far.astype(F32)
    other = swap_cores((row(CS) * own + row(ES) * enter).astype(BF16))
    mine = (row(CR) * got + row(ER) * enter).astype(BF16)
    return mine, other


def layer(queries, keys, values, lengths, gain, out_weight, cotangent):
    queries, keys, values, cotangent = queries[0], keys[0], values[0], cotangent[0]
    core = lax.axis_index("core")
    part = lax.dynamic_slice(out_weight, (0, core * (D // 2)), (out_weight.shape[0], D // 2))
    gathered = lax.all_gather(part, ("core", "fsdp"), axis=0, tiled=True)
    weight = gathered.reshape(2, DI, D // 2)
    gain_row = gain.reshape(1, DI)
    core_index = jnp.full((1,), core, jnp.int32)

    keep, give, coef = local_state(lengths, keys, values)
    mine, other = window(keep, give, coef, 1)
    attn, inside = inside_part(lengths, queries, keys, values)
    mixed, scaled = mixed_part(lengths, queries, inside, mine, other, gain_row)
    low, give_back, keep_back = grad_mixed_part(core_index, lengths, cotangent, weight, mixed, gain_row, queries)
    back_mine, back_other = window(keep_back, give_back, coef, -1)
    output = output_part(scaled, weight)
    dq, dk_part, dv_part = grads_part(lengths, queries, keys, values, low, attn, mine, other)
    dk, dv = last_part(lengths, keys, values, dk_part, dv_part, back_mine, back_other)
    return output[None], dq[None], dk[None], dv[None]


def solution(mesh):
    split = Mesh(mesh.devices.reshape(8, 4, 2, 8), ("z", "x", "core", "fsdp"))
    tokens = P("fsdp", ("z", "x", "core"), None)
    return jax.shard_map(
        layer,
        mesh=split,
        in_specs=(tokens, tokens, tokens, P("fsdp", None), P(), P("fsdp", None), tokens),
        out_specs=(tokens,) * 4,
        check_vma=False,
    )
```

time: 232 us -> 123 us (0.53)
  the two profiles are of different devices: /device:TPU:223 before, /device:TPU:199 now
where the time goes in v1:
time: 123 us; the launch traced here: 122 us
  waiting for transfers between devices  37.8 us (31%)
  starting transfers between devices  33.6 us (27%)
  Pallas kernels  23.4 us (19%)
  between operations  14.3 us (12%)
  local copies, waits for them, and re-layouts  10.9 us (9%)
  other arithmetic  2.55 us (2%)
    ppermute x6, waiting for transfers between devices, from_chip(): return lax.ppermute(block, ('z', 'x', 'core'), pairs)  24.3 us
    ppermute x6, starting transfers between devices, from_chip(): return lax.ppermute(block, ('z', 'x', 'core'), pairs)  20.9 us
    ppermute x4, starting transfers between devices, swap_cores(): return lax.ppermute(block, 'core', [(0, 1), (1, 0)])  12.7 us
    all_gather x1, waiting for transfers between devices, layer(): gathered = lax.all_gather(part, ('core', 'fsdp'), axis=0, tiled=True)  11 us
    unnamed x30, local copies, waits for them, and re-layouts  9.43 us
    pallas_call x1, Pallas kernels, grad_mixed_part(): pl.pallas_call(grad_mixed_kernel, out_shape=(jax.ShapeDtypeStruct((TOK, D...  8.02 us
    pallas_call x1, Pallas kernels, output_part(): pl.pallas_call(output_kernel, out_shape=jax.ShapeDtypeStruct((TOK, D), BF...  5.05 us
    pallas_call x1, Pallas kernels, grads_part(): pl.pallas_call(grads_kernel, out_shape=(jax.ShapeDtypeStruct((TOK, DI), B...  3.96 us
  transfers between devices with their start and end apart: 11, of which 8 were waited for; matrix products, arithmetic and copies ran while one was open for 1% of the time, Pallas kernels for 11%

profile of v1, /device:TPU:199, one launch (start us, length us, event | category | flops | bytes accessed | tf_op | source)
XLA Modules:
  0.0 122.4 jit_solution(8182795917746861295)
XLA Ops:
  7.2 0.0 copy-start
  7.2 0.0 all-gather.2.cloned.1.call-start
  7.2 1.1 copy-done
  8.3 0.8 constant_dynamic-slice_fusion
  9.1 0.0 all-gather.2.cloned.1.call-update
  9.1 0.0 copy-start.3
  9.1 1.0 copy-done.3
  10.1 1.0 copy-done.6
  11.1 0.7 copy-done.13
  11.8 0.9 local_state.1
  12.7 2.6 %collective-permute-start = (bf16[6,128,128]{2,1,0:T(8,128)(2,1)S(1)}, bf16[6,128,128]{2,1,0:T(8,128)(2,1)S(1)}, u32[]{:S(2)}, u32[]{:S(2)}) collective-permute-start(bf16[6,128,128]{2,1,0:T(8,128)(2,1)S(1)} %get-tuple-element.21), channel_id=1, source_target_pairs={{0,8},{8,0},{1,9},{9,1},{2,10},{10,2},{3,11},{11,3},{4,12},{12,4},... | collective-permute-start | bytes 589832 | tf_op jit(solution)/shard_map/ppermute | solution.py:363
  15.3 1.0 collective-permute-done
  16.4 0.1 fusion.3
  16.4 5.1 %collective-permute-start.1 = (bf16[6,128,128]{2,1,0:T(8,128)(2,1)S(1)}, bf16[6,128,128]{2,1,0:T(8,128)(2,1)S(1)}, u32[]{:S(2)}, u32[]{:S(2)}) collective-permute-start(bf16[6,128,128]{2,1,0:T(8,128)(2,1)S(1)} %fusion.3), channel_id=1, source_target_pairs={{0,16},{8,24},{16,32},{24,40},{32,48},{40,56},{48,64},{56,72},{64,... | collective-permute-start | bytes 589832 | tf_op jit(solution)/shard_map/ppermute | solution.py:369
  21.6 3.9 %collective-permute-done.1 = bf16[6,128,128]{2,1,0:T(8,128)(2,1)S(1)} collective-permute-done((bf16[6,128,128]{2,1,0:T(8,128)(2,1)S(1)}, bf16[6,128,128]{2,1,0:T(8,128)(2,1)S(1)}, u32[]{:S(2)}, u32[]{:S(2)}) %collective-permute-start.1) | collective-permute-done | bytes 196640 | tf_op jit(solution)/shard_map/ppermute | solution.py:369
  25.4 0.1 add_convert_fusion.1
  25.5 4.5 %collective-permute-start.3 = (bf16[6,128,128]{2,1,0:T(8,128)(2,1)S(1)}, bf16[6,128,128]{2,1,0:T(8,128)(2,1)S(1)}, u32[]{:S(2)}, u32[]{:S(2)}) collective-permute-start(bf16[6,128,128]{2,1,0:T(8,128)(2,1)S(1)} %add_convert_fusion.1), channel_id=1, source_target_pairs={{0,48},{8,56},{16,64},{24,72},{32,80},{40,88},{48,96},{56,104},{64... | collective-permute-start | bytes 589832 | tf_op jit(solution)/shard_map/ppermute | solution.py:369
  30.0 4.9 %collective-permute-start.2 = (bf16[6,128,128]{2,1,0:T(8,128)(2,1)S(1)}, bf16[6,128,128]{2,1,0:T(8,128)(2,1)S(1)}, u32[]{:S(2)}, u32[]{:S(2)}) collective-permute-start(bf16[6,128,128]{2,1,0:T(8,128)(2,1)S(1)} %add_convert_fusion.1), channel_id=1, source_target_pairs={{0,16},{8,24},{16,32},{24,40},{32,48},{40,56},{48,64},{56,72},{64,... | collective-permute-start | bytes 589832 | tf_op jit(solution)/shard_map/ppermute | solution.py:369
  34.9 3.0 %collective-permute-done.2 = bf16[6,128,128]{2,1,0:T(8,128)(2,1)S(1)} collective-permute-done((bf16[6,128,128]{2,1,0:T(8,128)(2,1)S(1)}, bf16[6,128,128]{2,1,0:T(8,128)(2,1)S(1)}, u32[]{:S(2)}, u32[]{:S(2)}) %collective-permute-start.2) | collective-permute-done | bytes 196640 | tf_op jit(solution)/shard_map/ppermute | solution.py:369
  37.9 0.2 fusion.5
  38.1 4.0 %collective-permute-start.4 = (bf16[6,128,128]{2,1,0:T(8,128)(2,1)S(1)}, bf16[6,128,128]{2,1,0:T(8,128)(2,1)S(1)}, u32[]{:S(2)}, u32[]{:S(2)}) collective-permute-start(bf16[6,128,128]{2,1,0:T(8,128)(2,1)S(1)} %get-tuple-element.36), channel_id=1, source_target_pairs={{0,8},{8,0},{1,9},{9,1},{2,10},{10,2},{3,11},{11,3},{4,12},{12,4},... | collective-permute-start | bytes 589832 | tf_op jit(solution)/shard_map/ppermute | solution.py:363
  42.1 0.7 reshape.32.gain_ref
  42.8 1.0 copy-done.1
  43.8 1.0 copy-done.4
  44.9 1.0 copy-done.7
  45.9 2.5 %inside_part.1 = (bf16[12,128,128]{2,1,0:T(8,128)(2,1)S(1)}, f32[128,1536]{1,0:T(8,128)S(1)}) custom-call(s32[1,16]{1,0:T(1,128)S(1)} %copy-done.13, bf16[128,1536]{1,0:T(8,128)(2,1)S(1)} %bitcast.47, bf16[128,1536]{1,0:T(8,128)(2,1)S(1)} %bitcast.51, bf16[128,1536]{1,0:T(8,128)(2,1)S(1)} %bitcast.55), custom_call_target="tpu_custom_call" | custom-call | flops 100000000 | bytes 2400000 | tf_op jit(solution)/shard_map/inside_part/pallas_call | solution.py:168
  48.4 1.0 mixed_part.1
  49.4 0.9 copy-done.9
  50.3 0.7 copy-done.10
  51.0 11.0 %all-gather.2.cloned.1.call-done = bf16[3072,1024]{1,0:T(8,128)(2,1)} async-done(((bf16[192,1024]{1,0:T(8,128)(2,1)}), bf16[3072,1024]{1,0:T(8,128)(2,1)}) %all-gather.2.cloned.1.call-update) | async-done | bytes 6291472 | tf_op jit(solution)/shard_map/all_gather | solution.py:393
  62.1 8.0 %grad_mixed_part.1 = (bf16[128,1536]{1,0:T(8,128)(2,1)}, bf16[6,128,128]{2,1,0:T(8,128)(2,1)}, bf16[6,128,128]{2,1,0:T(8,128)(2,1)}) custom-call(s32[1]{0:T(128)} %bitcast.14.core_ref, s32[1,16]{1,0:T(1,128)} %lengths_ref.11, bf16[128,2048]{1,0:T(8,128)(2,1)} %bitcast.60, bf16[2,1536,1024]{2,1,0:T(8,128)(2,1)} %bitcast.58, f32[128,1536]{1,0:T(8,128)} %copy-done.9, ...), custom_call_target="tpu_custom_call" | custom-call | flops 860000000 | bytes 9000000 | tf_op jit(solution)/shard_map/grad_mixed_part/pallas_call | solution.py:250
  70.1 2.2 %collective-permute-start.5 = (bf16[6,128,128]{2,1,0:T(8,128)(2,1)}, bf16[6,128,128]{2,1,0:T(8,128)(2,1)S(1)}, u32[]{:S(2)}, u32[]{:S(2)}) collective-permute-start(bf16[6,128,128]{2,1,0:T(8,128)(2,1)} %get-tuple-element.30), channel_id=1, source_target_pairs={{0,8},{8,0},{1,9},{9,1},{2,10},{10,2},{3,11},{11,3},{4,12},{12,4},... | collective-permute-start | bytes 589832 | tf_op jit(solution)/shard_map/ppermute | solution.py:363
  72.3 1.4 %collective-permute-done.5 = bf16[6,128,128]{2,1,0:T(8,128)(2,1)S(1)} collective-permute-done((bf16[6,128,128]{2,1,0:T(8,128)(2,1)}, bf16[6,128,128]{2,1,0:T(8,128)(2,1)S(1)}, u32[]{:S(2)}, u32[]{:S(2)}) %collective-permute-start.5) | collective-permute-done | bytes 196640 | tf_op jit(solution)/shard_map/ppermute | solution.py:363
  73.6 1.0 fusion.9
  74.7 2.5 %collective-permute-start.6 = (bf16[6,128,128]{2,1,0:T(8,128)(2,1)S(1)}, bf16[6,128,128]{2,1,0:T(8,128)(2,1)S(1)}, u32[]{:S(2)}, u32[]{:S(2)}) collective-permute-start(bf16[6,128,128]{2,1,0:T(8,128)(2,1)S(1)} %fusion.9), channel_id=1, source_target_pairs={{16,0},{24,8},{32,16},{40,24},{48,32},{56,40},{64,48},{72,56},{80,... | collective-permute-start | bytes 589832 | tf_op jit(solution)/shard_map/ppermute | solution.py:369
  77.1 8.9 %collective-permute-done.6 = bf16[6,128,128]{2,1,0:T(8,128)(2,1)S(1)} collective-permute-done((bf16[6,128,128]{2,1,0:T(8,128)(2,1)S(1)}, bf16[6,128,128]{2,1,0:T(8,128)(2,1)S(1)}, u32[]{:S(2)}, u32[]{:S(2)}) %collective-permute-start.6) | collective-permute-done | bytes 196640 | tf_op jit(solution)/shard_map/ppermute | solution.py:369
  86.0 0.1 add_convert_fusion
  86.1 1.9 %collective-permute-start.8 = (bf16[6,128,128]{2,1,0:T(8,128)(2,1)S(1)}, bf16[6,128,128]{2,1,0:T(8,128)(2,1)S(1)}, u32[]{:S(2)}, u32[]{:S(2)}) collective-permute-start(bf16[6,128,128]{2,1,0:T(8,128)(2,1)S(1)} %add_convert_fusion), channel_id=1, source_target_pairs={{48,0},{56,8},{64,16},{72,24},{80,32},{88,40},{96,48},{104,56},{11... | collective-permute-start | bytes 589832 | tf_op jit(solution)/shard_map/ppermute | solution.py:369
  88.0 2.0 %collective-permute-start.7 = (bf16[6,128,128]{2,1,0:T(8,128)(2,1)S(1)}, bf16[6,128,128]{2,1,0:T(8,128)(2,1)S(1)}, u32[]{:S(2)}, u32[]{:S(2)}) collective-permute-start(bf16[6,128,128]{2,1,0:T(8,128)(2,1)S(1)} %add_convert_fusion), channel_id=1, source_target_pairs={{16,0},{24,8},{32,16},{40,24},{48,32},{56,40},{64,48},{72,56},{80,... | collective-permute-start | bytes 589832 | tf_op jit(solution)/shard_map/ppermute | solution.py:369
  90.0 5.4 %collective-permute-done.8 = bf16[6,128,128]{2,1,0:T(8,128)(2,1)S(1)} collective-permute-done((bf16[6,128,128]{2,1,0:T(8,128)(2,1)S(1)}, bf16[6,128,128]{2,1,0:T(8,128)(2,1)S(1)}, u32[]{:S(2)}, u32[]{:S(2)}) %collective-permute-start.8) | collective-permute-done | bytes 196640 | tf_op jit(solution)/shard_map/ppermute | solution.py:369
  95.5 3.1 %collective-permute-done.7 = bf16[6,128,128]{2,1,0:T(8,128)(2,1)S(1)} collective-permute-done((bf16[6,128,128]{2,1,0:T(8,128)(2,1)S(1)}, bf16[6,128,128]{2,1,0:T(8,128)(2,1)S(1)}, u32[]{:S(2)}, u32[]{:S(2)}) %collective-permute-start.7) | collective-permute-done | bytes 196640 | tf_op jit(solution)/shard_map/ppermute | solution.py:369
  98.6 1.1 fusion.11
  99.7 3.9 %collective-permute-start.9 = (bf16[6,128,128]{2,1,0:T(8,128)(2,1)S(1)}, bf16[6,128,128]{2,1,0:T(8,128)(2,1)S(1)}, u32[]{:S(2)}, u32[]{:S(2)}) collective-permute-start(bf16[6,128,128]{2,1,0:T(8,128)(2,1)S(1)} %get-tuple-element.34), channel_id=1, source_target_pairs={{0,8},{8,0},{1,9},{9,1},{2,10},{10,2},{3,11},{11,3},{4,12},{12,4},... | collective-permute-start | bytes 589832 | tf_op jit(solution)/shard_map/ppermute | solution.py:363
  103.7 0.0 copy-start.11
  103.7 1.0 copy-done.11
  104.7 4.0 %grads_part.1 = (bf16[128,1536]{1,0:T(8,128)(2,1)}, f32[128,1536]{1,0:T(8,128)S(1)}, f32[128,1536]{1,0:T(8,128)S(1)}) custom-call(s32[1,16]{1,0:T(1,128)S(1)} %copy-done.14, bf16[128,1536]{1,0:T(8,128)(2,1)S(1)} %bitcast.49, bf16[128,1536]{1,0:T(8,128)(2,1)S(1)} %bitcast.52, bf16[128,1536]{1,0:T(8,128)(2,1)S(1)} %bitcast.56, ...), custom_call_target="tpu_custom_call" | custom-call | flops 250000000 | bytes 5000000 | tf_op jit(solution)/shard_map/grads_part/pallas_call | solution.py:322
  108.6 5.1 %output_part.1 = bf16[128,2048]{1,0:T(8,128)(2,1)} custom-call(bf16[128,1536]{1,0:T(8,128)(2,1)} %copy-done.10, bf16[2,1536,1024]{2,1,0:T(8,128)(2,1)} %bitcast.59), custom_call_target="tpu_custom_call" | custom-call | flops 810000000 | bytes 7500000 | tf_op jit(solution)/shard_map/output_part/pallas_call | solution.py:283
  113.7 1.9 %last_part.1 = (bf16[128,1536]{1,0:T(8,128)(2,1)}, bf16[128,1536]{1,0:T(8,128)(2,1)}) custom-call(s32[1,16]{1,0:T(1,128)S(1)} %copy-done.14, bf16[128,1536]{1,0:T(8,128)(2,1)S(1)} %bitcast.53, bf16[128,1536]{1,0:T(8,128)(2,1)S(1)} %bitcast.57, f32[128,1536]{1,0:T(8,128)S(1)} %get-tuple-element.28.dk_part_ref, f32[128,1536]{1,0:T(8,128)S(1)} %get-tuple-element.29.dv_part_ref, ...), custom_call_target="tpu_custom_call" | custom-call | flops 100000000 | bytes 3500000 | tf_op jit(solution)/shard_map/last_part/pallas_call | solution.py:351
  (21 shorter events, 0.1 us)
Async XLA Ops:
  7.2 1.1 copy-start
  7.2 54.9 %all-gather.2.cloned.1.call-start = ((), (), s32[]{:S(2)}) async-start(), calls=%async_computation | async-start | bytes 6684672 | tf_op jit(solution)/shard_map/all_gather | solution.py:393
  9.1 1.0 copy-start.3
  10.1 1.0 copy-start.6
  11.1 0.7 copy-start.13
  12.7 3.6 %collective-permute-start = (bf16[6,128,128]{2,1,0:T(8,128)(2,1)S(1)}, bf16[6,128,128]{2,1,0:T(8,128)(2,1)S(1)}, u32[]{:S(2)}, u32[]{:S(2)}) collective-permute-start(bf16[6,128,128]{2,1,0:T(8,128)(2,1)S(1)} %get-tuple-element.21), channel_id=1, source_target_pairs={{0,8},{8,0},{1,9},{9,1},{2,10},{10,2},{3,11},{11,3},{4,12},{12,4},... | collective-permute-start | bytes 589832 | tf_op jit(solution)/shard_map/ppermute | solution.py:363
  16.4 9.0 %collective-permute-start.1 = (bf16[6,128,128]{2,1,0:T(8,128)(2,1)S(1)}, bf16[6,128,128]{2,1,0:T(8,128)(2,1)S(1)}, u32[]{:S(2)}, u32[]{:S(2)}) collective-permute-start(bf16[6,128,128]{2,1,0:T(8,128)(2,1)S(1)} %fusion.3), channel_id=1, source_target_pairs={{0,16},{8,24},{16,32},{24,40},{32,48},{40,56},{48,64},{56,72},{64,... | collective-permute-start | bytes 589832 | tf_op jit(solution)/shard_map/ppermute | solution.py:369
  25.5 9.4 %collective-permute-start.3 = (bf16[6,128,128]{2,1,0:T(8,128)(2,1)S(1)}, bf16[6,128,128]{2,1,0:T(8,128)(2,1)S(1)}, u32[]{:S(2)}, u32[]{:S(2)}) collective-permute-start(bf16[6,128,128]{2,1,0:T(8,128)(2,1)S(1)} %add_convert_fusion.1), channel_id=1, source_target_pairs={{0,48},{8,56},{16,64},{24,72},{32,80},{40,88},{48,96},{56,104},{64... | collective-permute-start | bytes 589832 | tf_op jit(solution)/shard_map/ppermute | solution.py:369
  30.0 7.9 %collective-permute-start.2 = (bf16[6,128,128]{2,1,0:T(8,128)(2,1)S(1)}, bf16[6,128,128]{2,1,0:T(8,128)(2,1)S(1)}, u32[]{:S(2)}, u32[]{:S(2)}) collective-permute-start(bf16[6,128,128]{2,1,0:T(8,128)(2,1)S(1)} %add_convert_fusion.1), channel_id=1, source_target_pairs={{0,16},{8,24},{16,32},{24,40},{32,48},{40,56},{48,64},{56,72},{64,... | collective-permute-start | bytes 589832 | tf_op jit(solution)/shard_map/ppermute | solution.py:369
  38.1 10.3 %collective-permute-start.4 = (bf16[6,128,128]{2,1,0:T(8,128)(2,1)S(1)}, bf16[6,128,128]{2,1,0:T(8,128)(2,1)S(1)}, u32[]{:S(2)}, u32[]{:S(2)}) collective-permute-start(bf16[6,128,128]{2,1,0:T(8,128)(2,1)S(1)} %get-tuple-element.36), channel_id=1, source_target_pairs={{0,8},{8,0},{1,9},{9,1},{2,10},{10,2},{3,11},{11,3},{4,12},{12,4},... | collective-permute-start | bytes 589832 | tf_op jit(solution)/shard_map/ppermute | solution.py:363
  42.8 19.3 %copy-start.12 = (f32[1,1536]{1,0:T(1,128)}, f32[1,1536]{1,0:T(1,128)S(1)}, u32[]{:S(2)}) copy-start(f32[1,1536]{1,0:T(1,128)S(1)} %reshape.32.gain_ref) | copy-start | bytes 18436
  42.8 1.0 copy-start.1
  43.8 1.0 copy-start.4
  44.9 1.0 copy-start.7
  45.9 57.7 %copy-start.2 = (bf16[1,128,1536]{2,1,0:T(8,128)(2,1)S(1)}, bf16[1,128,1536]{2,1,0:T(8,128)(2,1)}, u32[]{:S(2)}) copy-start(bf16[1,128,1536]{2,1,0:T(8,128)(2,1)} %param.7) | copy-start | bytes 1179652
  45.9 57.8 %copy-start.5 = (bf16[1,128,1536]{2,1,0:T(8,128)(2,1)S(1)}, bf16[1,128,1536]{2,1,0:T(8,128)(2,1)}, u32[]{:S(2)}) copy-start(bf16[1,128,1536]{2,1,0:T(8,128)(2,1)} %param.8) | copy-start | bytes 1179652
  45.9 57.8 %copy-start.8 = (bf16[1,128,1536]{2,1,0:T(8,128)(2,1)S(1)}, bf16[1,128,1536]{2,1,0:T(8,128)(2,1)}, u32[]{:S(2)}) copy-start(bf16[1,128,1536]{2,1,0:T(8,128)(2,1)} %param.9) | copy-start | bytes 1179652
  45.9 57.8 %copy-start.14 = (s32[1,16]{1,0:T(1,128)S(1)}, s32[1,16]{1,0:T(1,128)}, u32[]{:S(2)}) copy-start(s32[1,16]{1,0:T(1,128)} %lengths_ref.11) | copy-start | bytes 196
  49.4 0.9 copy-start.9
  50.3 0.7 copy-start.10
  70.1 3.5 %collective-permute-start.5 = (bf16[6,128,128]{2,1,0:T(8,128)(2,1)}, bf16[6,128,128]{2,1,0:T(8,128)(2,1)S(1)}, u32[]{:S(2)}, u32[]{:S(2)}) collective-permute-start(bf16[6,128,128]{2,1,0:T(8,128)(2,1)} %get-tuple-element.30), channel_id=1, source_target_pairs={{0,8},{8,0},{1,9},{9,1},{2,10},{10,2},{3,11},{11,3},{4,12},{12,4},... | collective-permute-start | bytes 589832 | tf_op jit(solution)/shard_map/ppermute | solution.py:363
  74.7 11.4 %collective-permute-start.6 = (bf16[6,128,128]{2,1,0:T(8,128)(2,1)S(1)}, bf16[6,128,128]{2,1,0:T(8,128)(2,1)S(1)}, u32[]{:S(2)}, u32[]{:S(2)}) collective-permute-start(bf16[6,128,128]{2,1,0:T(8,128)(2,1)S(1)} %fusion.9), channel_id=1, source_target_pairs={{16,0},{24,8},{32,16},{40,24},{48,32},{56,40},{64,48},{72,56},{80,... | collective-permute-start | bytes 589832 | tf_op jit(solution)/shard_map/ppermute | solution.py:369
  86.1 9.3 %collective-permute-start.8 = (bf16[6,128,128]{2,1,0:T(8,128)(2,1)S(1)}, bf16[6,128,128]{2,1,0:T(8,128)(2,1)S(1)}, u32[]{:S(2)}, u32[]{:S(2)}) collective-permute-start(bf16[6,128,128]{2,1,0:T(8,128)(2,1)S(1)} %add_convert_fusion), channel_id=1, source_target_pairs={{48,0},{56,8},{64,16},{72,24},{80,32},{88,40},{96,48},{104,56},{11... | collective-permute-start | bytes 589832 | tf_op jit(solution)/shard_map/ppermute | solution.py:369
  88.0 10.5 %collective-permute-start.7 = (bf16[6,128,128]{2,1,0:T(8,128)(2,1)S(1)}, bf16[6,128,128]{2,1,0:T(8,128)(2,1)S(1)}, u32[]{:S(2)}, u32[]{:S(2)}) collective-permute-start(bf16[6,128,128]{2,1,0:T(8,128)(2,1)S(1)} %add_convert_fusion), channel_id=1, source_target_pairs={{16,0},{24,8},{32,16},{40,24},{48,32},{56,40},{64,48},{72,56},{80,... | collective-permute-start | bytes 589832 | tf_op jit(solution)/shard_map/ppermute | solution.py:369
  99.7 14.0 %collective-permute-start.9 = (bf16[6,128,128]{2,1,0:T(8,128)(2,1)S(1)}, bf16[6,128,128]{2,1,0:T(8,128)(2,1)S(1)}, u32[]{:S(2)}, u32[]{:S(2)}) collective-permute-start(bf16[6,128,128]{2,1,0:T(8,128)(2,1)S(1)} %get-tuple-element.34), channel_id=1, source_target_pairs={{0,8},{8,0},{1,9},{9,1},{2,10},{10,2},{3,11},{11,3},{4,12},{12,4},... | collective-permute-start | bytes 589832 | tf_op jit(solution)/shard_map/ppermute | solution.py:363
  103.7 1.0 copy-start.11
Sparse Core Ops, SparseCore 0:
  10.7 51.3 all-gather.1

commit v2 on v1

--- a/solution.py
+++ b/solution.py
@@ -11,6 +11,8 @@
 HEAD_DIM = 128
 NDOCS = 16
 TOK = 128
+SHARD = 192
+Y = 8
 DI = HEADS * HEAD_DIM
 D = 2048
 CHIPS = 32
@@ -24,6 +26,7 @@
 
 VMEM = pl.BlockSpec(memory_space=pltpu.VMEM)
 SMEM = pl.BlockSpec(memory_space=pltpu.SMEM)
+HBM = pl.BlockSpec(memory_space=pltpu.HBM)
 
 
 def params(mib=24):
@@ -91,7 +94,47 @@
     return (columns <= rows) & (columns >= first)
 
 
-def local_state_kernel(lengths_ref, keys_ref, values_ref, keep_ref, give_ref, coef_ref):
+def take_half_kernel(weight_ref, cot_ref, half_ref, cot_keep_ref, cot_give_ref, sems):
+    _, core = chip_and_core()
+    width = D // 2
+    mine = pl.ds(pl.multiple_of(core * width, width), width)
+    theirs = pl.ds(pl.multiple_of((1 - core) * width, width), width)
+    copies = [
+        pltpu.make_async_copy(weight_ref.at[:, mine], half_ref, sems.at[0]),
+        pltpu.make_async_copy(cot_ref.at[:, theirs], cot_give_ref, sems.at[1]),
+        pltpu.make_async_copy(cot_ref.at[:, mine], cot_keep_ref, sems.at[2]),
+    ]
+    for copy in copies:
+        copy.start()
+    for copy in copies:
+        copy.wait()
+
+
+def take_half(weight, cotangent):
+    cot = jax.ShapeDtypeStruct((TOK, D // 2), BF16)
+    return pl.pallas_call(
+        take_half_kernel,
+        out_shape=(jax.ShapeDtypeStruct((SHARD, D // 2), BF16), cot, cot),
+        in_specs=[HBM, HBM],
+        out_specs=(VMEM, VMEM, VMEM),
+        scratch_shapes=[pltpu.SemaphoreType.DMA((3,))],
+        compiler_params=params(60),
+        cost_estimate=cost(1000, 2_000_000),
+        name="take_half",
+    )(weight, cotangent)
+
+
+def local_state_kernel(
+    lengths_ref, keys_hbm, values_hbm, keep_ref, give_ref, coef_ref, keys_ref, values_ref, sems
+):
+    copies = [
+        pltpu.make_async_copy(keys_hbm, keys_ref, sems.at[0]),
+        pltpu.make_async_copy(values_hbm, values_ref, sems.at[1]),
+    ]
+    for copy in copies:
+        copy.start()
+    for copy in copies:
+        copy.wait()
     chip, core = chip_and_core()
     ends = running_ends(lengths_ref)
     start = (chip * 2 + core) * TOK
@@ -143,8 +186,13 @@
     return pl.pallas_call(
         local_state_kernel,
         out_shape=(half, half, jax.ShapeDtypeStruct((ROWS, 128), F32)),
-        in_specs=[SMEM, VMEM, VMEM],
+        in_specs=[SMEM, HBM, HBM],
         out_specs=(VMEM, VMEM, VMEM),
+        scratch_shapes=[
+            pltpu.VMEM((TOK, DI), BF16),
+            pltpu.VMEM((TOK, DI), BF16),
+            pltpu.SemaphoreType.DMA((2,)),
+        ],
         compiler_params=params(),
         cost_estimate=cost(50_000_000, 1_200_000),
         name="local_state",
@@ -207,92 +255,130 @@
     )(lengths, queries, inside, mine, other, gain)
 
 
-PAIR = 2 * HEAD_DIM
+def shard_rows(distance, count=SHARD, skip=0):
+    owner = lax.rem(lax.axis_index("fsdp") + (distance + Y), Y)
+    return pl.ds(pl.multiple_of(owner * SHARD + skip, 32), count)
+
+
+EARLY = (0, -1, 1, -2, 2, -3, 3)
+
+
+def share_kernel(cot_keep_ref, cot_got_ref, *refs):
+    pieces, (own_ref, give_ref, cot_ref) = refs[: len(EARLY)], refs[len(EARLY) :]
+    cot_ref[:TOK] = cot_keep_ref[...]
+    cot_ref[TOK:] = cot_got_ref[...]
+    for distance, piece in zip(EARLY, pieces):
+        share = dot(piece[...], cot_ref[...], NT)
+        rows = shard_rows(distance)
+        own_ref[rows, :] = share[:, :TOK]
+        give_ref[rows, :] = share[:, TOK:].astype(BF16)
+
+
+SHARE_SHAPES = (jax.ShapeDtypeStruct((DI, TOK), F32), jax.ShapeDtypeStruct((DI, TOK), BF16))
+
+
+def share_part(cot_keep, cot_got, pieces):
+    return pl.pallas_call(
+        share_kernel,
+        out_shape=SHARE_SHAPES,
+        in_specs=[VMEM] * (2 + len(EARLY)),
+        out_specs=(VMEM, VMEM),
+        scratch_shapes=[pltpu.VMEM((2 * TOK, D // 2), BF16)],
+        compiler_params=params(),
+        cost_estimate=cost(700_000_000, 4_500_000),
+        name="share_part",
+    )(cot_keep, cot_got, *pieces)
+
+
+def share_end_kernel(
+    cot_keep_ref, cot_got_ref, top_ref, bottom_ref, own_in_ref, give_in_ref, own_ref, give_ref, cot_ref, piece_ref
+):
+    cot_ref[:TOK] = cot_keep_ref[...]
+    cot_ref[TOK:] = cot_got_ref[...]
+    piece_ref[: SHARD // 2] = top_ref[...]
+    piece_ref[SHARD // 2 :] = bottom_ref[...]
+    own_ref[...] = own_in_ref[...]
+    give_ref[...] = give_in_ref[...]
+    share = dot(piece_ref[...], cot_ref[...], NT)
+    rows = shard_rows(4)
+    own_ref[rows, :] = share[:, :TOK]
+    give_ref[rows, :] = share[:, TOK:].astype(BF16)
+
+
+def share_end(cot_keep, cot_got, top, bottom, own, give):
+    return pl.pallas_call(
+        share_end_kernel,
+        out_shape=SHARE_SHAPES,
+        in_specs=[VMEM] * 6,
+        out_specs=(VMEM, VMEM),
+        scratch_shapes=[pltpu.VMEM((2 * TOK, D // 2), BF16), pltpu.VMEM((SHARD, D // 2), BF16)],
+        compiler_params=params(),
+        cost_estimate=cost(100_000_000, 3_500_000),
+        name="share_end",
+    )(cot_keep, cot_got, top, bottom, own, give)
 
 
 def grad_mixed_kernel(
-    core_ref, lengths_ref, cot_ref, weight_ref, mixed_ref, gain_ref, queries_ref, low_ref, give_ref, keep_ref
+    lengths_ref, own_ref, got_ref, mixed_ref, gain_ref, queries_ref, low_ref, give_ref, keep_ref
 ):
-    step = pl.program_id(0)
     chip, core = chip_and_core()
     ends = running_ends(lengths_ref)
     start = (chip * 2 + core) * TOK
     head_rows = rows_of(start) < next_end(ends, start)
-    grad_scaled = dot(cot_ref[:, : D // 2], weight_ref[0], NT) + dot(cot_ref[:, D // 2 :], weight_ref[1], NT)
-    states = []
-    for j in range(2):
-        span = lanes(j)
-        mixed = mixed_ref[:, span]
-        inv_rms = lax.rsqrt(jnp.mean(mixed * mixed, axis=-1, keepdims=True) + EPSILON)
-        normed = mixed * inv_rms
-        g = grad_scaled[:, j * HEAD_DIM : (j + 1) * HEAD_DIM] * gain_ref[:, span]
-        low = (inv_rms * (g - normed * jnp.mean(g * normed, axis=-1, keepdims=True))).astype(BF16)
-        low_ref[:, span] = low
-        head_queries = jnp.where(head_rows, queries_ref[:, span], 0)
-        states.append(dot(head_queries, low, TN).astype(BF16))
-
-    @pl.when(step < 3)
-    def _():
-        give_ref[0] = states[0]
-        give_ref[1] = states[1]
-
-    @pl.when(step >= 3)
-    def _():
-        keep_ref[0] = states[0]
-        keep_ref[1] = states[1]
-
-
-def grad_mixed_part(core_index, lengths, cotangent, weight, mixed, gain, queries):
-    def pair(i, core_ref):
-        return lax.rem(i + 3 * (1 - core_ref[0]), 6)
-
+    for part, ref in ((0, give_ref), (1, keep_ref)):
+        first = HALF * (1 - core) if part == 0 else HALF * core
+        for j in range(HALF):
+            span = lanes(first + j)
+            grad_scaled = (own_ref[span, :] + got_ref[span, :].astype(F32)).T
+            mixed = mixed_ref[:, span]
+            inv_rms = lax.rsqrt(jnp.mean(mixed * mixed, axis=-1, keepdims=True) + EPSILON)
+            normed = mixed * inv_rms
+            g = grad_scaled * gain_ref[:, span]
+            low = (inv_rms * (g - normed * jnp.mean(g * normed, axis=-1, keepdims=True))).astype(BF16)
+            low_ref[:, span] = low
+            head_queries = jnp.where(head_rows, queries_ref[:, span], 0)
+            ref[j] = dot(head_queries, low, TN).astype(BF16)
+
+
+def grad_mixed_part(lengths, own, got, mixed, gain, queries):
     half = jax.ShapeDtypeStruct((HALF, HEAD_DIM, HEAD_DIM), BF16)
     return pl.pallas_call(
         grad_mixed_kernel,
         out_shape=(jax.ShapeDtypeStruct((TOK, DI), BF16), half, half),
-        grid_spec=pltpu.PrefetchScalarGridSpec(
-            num_scalar_prefetch=1,
-            grid=(6,),
-            in_specs=[
-                SMEM,
-                pl.BlockSpec((TOK, D), lambda i, c: (0, 0)),
-                pl.BlockSpec((2, PAIR, D // 2), lambda i, c: (0, pair(i, c), 0)),
-                pl.BlockSpec((TOK, PAIR), lambda i, c: (0, pair(i, c))),
-                pl.BlockSpec((1, PAIR), lambda i, c: (0, pair(i, c))),
-                pl.BlockSpec((TOK, PAIR), lambda i, c: (0, pair(i, c))),
-            ],
-            out_specs=(
-                pl.BlockSpec((TOK, PAIR), lambda i, c: (0, pair(i, c))),
-                pl.BlockSpec((2, HEAD_DIM, HEAD_DIM), lambda i, c: (jnp.minimum(i, 2), 0, 0)),
-                pl.BlockSpec((2, HEAD_DIM, HEAD_DIM), lambda i, c: (jnp.maximum(i - 3, 0), 0, 0)),
-            ),
-        ),
-        compiler_params=params(58),
-        cost_estimate=cost(860_000_000, 9_000_000),
+        in_specs=[SMEM] + [VMEM] * 5,
+        out_specs=(VMEM,) * 3,
+        compiler_params=params(),
+        cost_estimate=cost(60_000_000, 4_000_000),
         name="grad_mixed_part",
-    )(core_index, lengths, cotangent, weight, mixed, gain, queries)
-
-
-def output_kernel(scaled_ref, weight_ref, output_ref):
-    output_ref[...] = dot(scaled_ref[...], weight_ref[0], NN).astype(BF16)
-
-
-def output_part(scaled, weight):
-    width = 512
-    per = D // 2 // width
+    )(lengths, own, got, mixed, gain, queries)
+
+
+def output_kernel(scaled_ref, scaled_got_ref, *refs):
+    pieces, (top_ref, bottom_ref, own_ref, give_ref, both_ref, weight_ref) = refs[: len(EARLY)], refs[len(EARLY) :]
+    for distance, piece in zip(EARLY, pieces):
+        weight_ref[shard_rows(distance), :] = piece[...]
+    weight_ref[shard_rows(4, SHARD // 2), :] = top_ref[...]
+    weight_ref[shard_rows(4, SHARD // 2, SHARD // 2), :] = bottom_ref[...]
+    both_ref[:TOK] = scaled_ref[...]
+    both_ref[TOK:] = scaled_got_ref[...]
+    for start in range(0, D // 2, 256):
+        block = dot(both_ref[...], weight_ref[:, start : start + 256], NN).astype(BF16)
+        own_ref[:, start : start + 256] = block[:TOK]
+        give_ref[:, start : start + 256] = block[TOK:]
+
+
+def output_part(scaled, scaled_got, pieces, top, bottom):
+    half = jax.ShapeDtypeStruct((TOK, D // 2), BF16)
     return pl.pallas_call(
         output_kernel,
-        out_shape=jax.ShapeDtypeStruct((TOK, D), BF16),
-        grid=(D // width,),
-        in_specs=[
-            pl.BlockSpec((TOK, DI), lambda i: (0, 0)),
-            pl.BlockSpec((1, DI, width), lambda i: (i // per, 0, i % per)),
-        ],
-        out_specs=pl.BlockSpec((TOK, width), lambda i: (0, i)),
-        compiler_params=params(58),
-        cost_estimate=cost(810_000_000, 7_500_000),
+        out_shape=(half, half),
+        in_specs=[VMEM] * (4 + len(EARLY)),
+        out_specs=(VMEM, VMEM),
+        scratch_shapes=[pltpu.VMEM((2 * TOK, DI), BF16), pltpu.VMEM((DI, D // 2), BF16)],
+        compiler_params=params(),
+        cost_estimate=cost(810_000_000, 5_000_000),
         name="output_part",
-    )(scaled, weight)
+    )(scaled, scaled_got, *pieces, top, bottom)
 
 
 def grads_kernel(
@@ -330,8 +416,14 @@
     )(lengths, queries, keys, values, low, attn, mine, other)
 
 
-def last_kernel(lengths_ref, keys_ref, values_ref, dk_part_ref, dv_part_ref, mine_ref, other_ref, dk_ref, dv_ref):
+def last_kernel(
+    lengths_ref, keys_ref, values_ref, dk_part_ref, dv_part_ref, out_own_ref, out_got_ref, mine_ref, other_ref,
+    dk_ref, dv_ref, output_ref,
+):
     chip, core = chip_and_core()
+    width = D // 2
+    output_ref[:, pl.ds(pl.multiple_of(core * width, width), width)] = out_own_ref[...]
+    output_ref[:, pl.ds(pl.multiple_of((1 - core) * width, width), width)] = out_got_ref[...]
     ends = running_ends(lengths_ref)
     start = (chip * 2 + core) * TOK
     after = rows_of(start) >= last_end(ends, start + TOK)
@@ -346,17 +438,17 @@
             dv_ref[:, span] = (dv_part_ref[:, span] + from_values).astype(BF16)
 
 
-def last_part(lengths, keys, values, dk, dv, mine, other):
+def last_part(lengths, keys, values, dk, dv, out_own, out_got, mine, other):
     full = jax.ShapeDtypeStruct((TOK, DI), BF16)
     return pl.pallas_call(
         last_kernel,
-        out_shape=(full, full),
-        in_specs=[SMEM] + [VMEM] * 6,
-        out_specs=(VMEM,) * 2,
-        compiler_params=params(),
-        cost_estimate=cost(100_000_000, 3_500_000),
+        out_shape=(full, full, jax.ShapeDtypeStruct((TOK, D), BF16)),
+        in_specs=[SMEM] + [VMEM] * 8,
+        out_specs=(VMEM,) * 3,
+        compiler_params=params(),
+        cost_estimate=cost(100_000_000, 4_500_000),
         name="last_part",
-    )(lengths, keys, values, dk, dv, mine, other)
+    )(lengths, keys, values, dk, dv, out_own, out_got, mine, other)
 
 
 def swap_cores(block):
@@ -367,6 +459,10 @@
     chips = range(CHIPS)
     pairs = [(2 * (i - distance) + c, 2 * i + c) for i in chips for c in range(2) if i - distance in chips]
     return lax.ppermute(block, ("z", "x", "core"), pairs)
+
+
+def along_y(block, distance):
+    return lax.ppermute(block, "fsdp", [(i, (i + distance) % Y) for i in range(Y)])
 
 
 def window(keep, give, coef, sign):
@@ -388,22 +484,31 @@
 
 def layer(queries, keys, values, lengths, gain, out_weight, cotangent):
     queries, keys, values, cotangent = queries[0], keys[0], values[0], cotangent[0]
-    core = lax.axis_index("core")
-    part = lax.dynamic_slice(out_weight, (0, core * (D // 2)), (out_weight.shape[0], D // 2))
-    gathered = lax.all_gather(part, ("core", "fsdp"), axis=0, tiled=True)
-    weight = gathered.reshape(2, DI, D // 2)
     gain_row = gain.reshape(1, DI)
-    core_index = jnp.full((1,), core, jnp.int32)
+    half, cot_keep, cot_give = take_half(out_weight, cotangent)
+    up, down = [half], [half]
+    for _ in range(1, 4):
+        up.append(along_y(up[-1], 1))
+        down.append(along_y(down[-1], -1))
+    top = along_y(up[3][: SHARD // 2], 1)
+    bottom = along_y(down[3][SHARD // 2 :], -1)
+    pieces = (half, up[1], down[1], up[2], down[2], up[3], down[3])
+    cot_got = swap_cores(cot_give)
 
     keep, give, coef = local_state(lengths, keys, values)
     mine, other = window(keep, give, coef, 1)
     attn, inside = inside_part(lengths, queries, keys, values)
     mixed, scaled = mixed_part(lengths, queries, inside, mine, other, gain_row)
-    low, give_back, keep_back = grad_mixed_part(core_index, lengths, cotangent, weight, mixed, gain_row, queries)
+    scaled_got = swap_cores(scaled)
+    own_share, give_share = share_part(cot_keep, cot_got, pieces)
+    own_share, give_share = share_end(cot_keep, cot_got, top, bottom, own_share, give_share)
+    got_share = swap_cores(give_share)
+    low, give_back, keep_back = grad_mixed_part(lengths, own_share, got_share, mixed, gain_row, queries)
     back_mine, back_other = window(keep_back, give_back, coef, -1)
-    output = output_part(scaled, weight)
+    out_own, out_give = output_part(scaled, scaled_got, pieces, top, bottom)
+    out_got = swap_cores(out_give)
     dq, dk_part, dv_part = grads_part(lengths, queries, keys, values, low, attn, mine, other)
-    dk, dv = last_part(lengths, keys, values, dk_part, dv_part, back_mine, back_other)
+    dk, dv, output = last_part(lengths, keys, values, dk_part, dv_part, out_own, out_got, back_mine, back_other)
     return output[None], dq[None], dk[None], dv[None]
 
 

time: 123 us -> 112 us (0.911)
  starting transfers between devices: 33.6 us -> 71.2 us
  waiting for transfers between devices: 37.8 us -> 19.8 us
  between operations: 14.3 us -> 1.17 us
  local copies, waits for them, and re-layouts: 10.9 us -> 0.72 us
  Pallas kernels: 23.4 us -> 18.2 us
  other arithmetic: 2.55 us -> 0.71 us
    ppermute x0 -> x8, starting transfers between devices: none -> 27.8 us  [along_y(): lax.ppermute(block, 'fsdp', [(i, (i + distance) % Y) for i in range(Y)])]
    ppermute x6, waiting for transfers between devices: 24.3 us -> 12.2 us  [from_chip(): return lax.ppermute(block, ('z', 'x', 'core'), pairs)]
    ppermute x4 -> x8, starting transfers between devices: 12.7 us -> 24.5 us  [swap_cores(): return lax.ppermute(block, 'core', [(0, 1), (1, 0)])]
    all_gather x1 -> x0, waiting for transfers between devices: 11 us -> none  [layer(): gathered = lax.all_gather(part, ('core', 'fsdp'), axis=0, tiled=True)]
    unnamed x30 -> x16, local copies, waits for them, and re-layouts: 9.43 us -> 0.67 us
    ppermute x0 -> x8, waiting for transfers between devices: none -> 6.18 us  [along_y(): lax.ppermute(block, 'fsdp', [(i, (i + distance) % Y) for i in range(Y)])]
    pallas_call x1, Pallas kernels: 8.02 us -> 2.2 us  [grad_mixed_part(): pl.pallas_call(grad_mixed_kernel, out_shape=(jax.ShapeDtypeStruct((TOK, D...]
    ppermute x6, starting transfers between devices: 20.9 us -> 18.9 us  [from_chip(): return lax.ppermute(block, ('z', 'x', 'core'), pairs)]
  transfers between devices with their start and end apart: 11 -> 22, of which waited for: 8 -> 5; matrix products, arithmetic and copies ran while one was open for 1% -> 1% of each run, Pallas kernels for 11% -> 11%
where the time goes in v2:
time: 112 us
  starting transfers between devices  71.2 us (64%)
  waiting for transfers between devices  19.8 us (18%)
  Pallas kernels  18.2 us (16%)
  between operations  1.17 us (1%)
    ppermute x8, starting transfers between devices, along_y(): lax.ppermute(block, 'fsdp', [(i, (i + distance) % Y) for i in range(Y)])  27.8 us
    ppermute x8, starting transfers between devices, swap_cores(): return lax.ppermute(block, 'core', [(0, 1), (1, 0)])  24.5 us
    ppermute x6, starting transfers between devices, from_chip(): return lax.ppermute(block, ('z', 'x', 'core'), pairs)  18.9 us
    ppermute x6, waiting for transfers between devices, from_chip(): return lax.ppermute(block, ('z', 'x', 'core'), pairs)  12.2 us
    ppermute x8, waiting for transfers between devices, along_y(): lax.ppermute(block, 'fsdp', [(i, (i + distance) % Y) for i in range(Y)])  6.18 us
    pallas_call x1, Pallas kernels, grads_part(): pl.pallas_call(grads_kernel, out_shape=(jax.ShapeDtypeStruct((TOK, DI), B...  4 us
    pallas_call x1, Pallas kernels, inside_part(): pl.pallas_call(inside_kernel, out_shape=(jax.ShapeDtypeStruct((HEADS, TOK...  2.5 us
  transfers between devices with their start and end apart: 22, of which 5 were waited for; matrix products, arithmetic and copies ran while one was open for 1% of the time, Pallas kernels for 11%

profile of v2, /device:TPU:199, one launch (start us, length us, event | category | flops | bytes accessed | tf_op | source)
XLA Modules:
  0.0 111.7 jit_solution(5821136922899514966)
XLA Ops:
  0.7 2.2 %take_half.1 = (bf16[192,1024]{1,0:T(8,128)(2,1)}, bf16[128,1024]{1,0:T(8,128)(2,1)}, bf16[128,1024]{1,0:T(8,128)(2,1)}) custom-call(bf16[192,2048]{1,0:T(8,128)(2,1)} %weight_ref.1, bf16[128,2048]{1,0:T(8,128)(2,1)} %bitcast.56), custom_call_target="tpu_custom_call" | custom-call | flops 1000 | bytes 2000000 | tf_op jit(solution)/shard_map/take_half/pallas_call | solution.py:115
  2.8 5.1 %collective-permute-start.5 = (bf16[192,1024]{1,0:T(8,128)(2,1)}, bf16[192,1024]{1,0:T(8,128)(2,1)S(1)}, u32[]{:S(2)}, u32[]{:S(2)}) collective-permute-start(bf16[192,1024]{1,0:T(8,128)(2,1)} %get-tuple-element.31.refs_0_), channel_id=1, source_target_pairs={{0,7},{1,0},{2,1},{3,2},{4,3},{5,4},{6,5},{7,6},{8,15},{9,8},{10,9... | collective-permute-start | bytes 1179656 | tf_op jit(solution)/shard_map/ppermute | solution.py:465
  7.9 1.9 %collective-permute-start.1 = (bf16[192,1024]{1,0:T(8,128)(2,1)}, bf16[192,1024]{1,0:T(8,128)(2,1)S(1)}, u32[]{:S(2)}, u32[]{:S(2)}) collective-permute-start(bf16[192,1024]{1,0:T(8,128)(2,1)} %get-tuple-element.31.refs_0_), channel_id=1, source_target_pairs={{0,1},{1,2},{2,3},{3,4},{4,5},{5,6},{6,7},{7,0},{8,9},{9,10},{10,1... | collective-permute-start | bytes 1179656 | tf_op jit(solution)/shard_map/ppermute | solution.py:465
  9.9 6.2 %collective-permute-done.5.refs_2_ = bf16[192,1024]{1,0:T(8,128)(2,1)S(1)} collective-permute-done((bf16[192,1024]{1,0:T(8,128)(2,1)}, bf16[192,1024]{1,0:T(8,128)(2,1)S(1)}, u32[]{:S(2)}, u32[]{:S(2)}) %collective-permute-start.5) | collective-permute-done | bytes 393248 | tf_op jit(solution)/shard_map/ppermute | solution.py:465
  16.0 5.2 %collective-permute-start.6 = (bf16[192,1024]{1,0:T(8,128)(2,1)S(1)}, bf16[192,1024]{1,0:T(8,128)(2,1)S(1)}, u32[]{:S(2)}, u32[]{:S(2)}) collective-permute-start(bf16[192,1024]{1,0:T(8,128)(2,1)S(1)} %collective-permute-done.5.refs_2_), channel_id=1, source_target_pairs={{0,7},{1,0},{2,1},{3,2},{4,3},{5,4},{6,5},{7,6},{8,15},{9,8},{10,9... | collective-permute-start | bytes 1179656 | tf_op jit(solution)/shard_map/ppermute | solution.py:465
  21.2 1.9 %collective-permute-start.2 = (bf16[192,1024]{1,0:T(8,128)(2,1)S(1)}, bf16[192,1024]{1,0:T(8,128)(2,1)S(1)}, u32[]{:S(2)}, u32[]{:S(2)}) collective-permute-start(bf16[192,1024]{1,0:T(8,128)(2,1)S(1)} %collective-permute-done.1.refs_1_), channel_id=1, source_target_pairs={{0,1},{1,2},{2,3},{3,4},{4,5},{5,6},{6,7},{7,0},{8,9},{9,10},{10,1... | collective-permute-start | bytes 1179656 | tf_op jit(solution)/shard_map/ppermute | solution.py:465
  23.2 0.0 copy-start.5
  23.2 0.6 copy-done.5
  23.8 1.3 %local_state.1 = (bf16[6,128,128]{2,1,0:T(8,128)(2,1)S(1)}, bf16[6,128,128]{2,1,0:T(8,128)(2,1)S(1)}, f32[24,128]{1,0:T(8,128)S(1)}) custom-call(s32[1,16]{1,0:T(1,128)S(1)} %copy-done.5, bf16[128,1536]{1,0:T(8,128)(2,1)S(1)} %bitcast.48, bf16[128,1536]{1,0:T(8,128)(2,1)S(1)} %bitcast.52), custom_call_target="tpu_custom_call" | custom-call | flops 50000000 | bytes 1200000 | tf_op jit(solution)/shard_map/local_state/pallas_call | solution.py:186
  25.2 3.7 %collective-permute-start.10 = (bf16[6,128,128]{2,1,0:T(8,128)(2,1)S(1)}, bf16[6,128,128]{2,1,0:T(8,128)(2,1)S(1)}, u32[]{:S(2)}, u32[]{:S(2)}) collective-permute-start(bf16[6,128,128]{2,1,0:T(8,128)(2,1)S(1)} %get-tuple-element.38), channel_id=1, source_target_pairs={{0,8},{8,0},{1,9},{9,1},{2,10},{10,2},{3,11},{11,3},{4,12},{12,4},... | collective-permute-start | bytes 589832 | tf_op jit(solution)/shard_map/ppermute | solution.py:455
  28.9 4.8 %collective-permute-start.7 = (bf16[192,1024]{1,0:T(8,128)(2,1)S(1)}, bf16[192,1024]{1,0:T(8,128)(2,1)S(1)}, u32[]{:S(2)}, u32[]{:S(2)}) collective-permute-start(bf16[192,1024]{1,0:T(8,128)(2,1)S(1)} %collective-permute-done.6.refs_4_), channel_id=1, source_target_pairs={{0,7},{1,0},{2,1},{3,2},{4,3},{5,4},{6,5},{7,6},{8,15},{9,8},{10,9... | collective-permute-start | bytes 1179656 | tf_op jit(solution)/shard_map/ppermute | solution.py:465
  33.8 1.9 %collective-permute-start.3 = (bf16[192,1024]{1,0:T(8,128)(2,1)S(1)}, bf16[192,1024]{1,0:T(8,128)(2,1)S(1)}, u32[]{:S(2)}, u32[]{:S(2)}) collective-permute-start(bf16[192,1024]{1,0:T(8,128)(2,1)S(1)} %collective-permute-done.2.refs_3_), channel_id=1, source_target_pairs={{0,1},{1,2},{2,3},{3,4},{4,5},{5,6},{6,7},{7,0},{8,9},{9,10},{10,1... | collective-permute-start | bytes 1179656 | tf_op jit(solution)/shard_map/ppermute | solution.py:465
  35.7 0.0 copy-start.7
  35.8 0.1 fusion.3
  35.9 5.1 %collective-permute-start.11 = (bf16[6,128,128]{2,1,0:T(8,128)(2,1)S(1)}, bf16[6,128,128]{2,1,0:T(8,128)(2,1)S(1)}, u32[]{:S(2)}, u32[]{:S(2)}) collective-permute-start(bf16[6,128,128]{2,1,0:T(8,128)(2,1)S(1)} %fusion.3), channel_id=1, source_target_pairs={{0,16},{8,24},{16,32},{24,40},{32,48},{40,56},{48,64},{56,72},{64,... | collective-permute-start | bytes 589832 | tf_op jit(solution)/shard_map/ppermute | solution.py:461
  41.0 4.5 %collective-permute-start = (bf16[128,1024]{1,0:T(8,128)(2,1)S(1)}, bf16[128,1024]{1,0:T(8,128)(2,1)S(1)}, u32[]{:S(2)}, u32[]{:S(2)}) collective-permute-start(bf16[128,1024]{1,0:T(8,128)(2,1)S(1)} %copy-done.7), channel_id=1, source_target_pairs={{0,8},{8,0},{1,9},{9,1},{2,10},{10,2},{3,11},{11,3},{4,12},{12,4},... | collective-permute-start | bytes 786440 | tf_op jit(solution)/shard_map/ppermute | solution.py:455
  45.6 4.9 %collective-permute-start.8 = (bf16[96,1024]{1,0:T(8,128)(2,1)S(1)}, bf16[96,1024]{1,0:T(8,128)(2,1)S(1)}, u32[]{:S(2)}, u32[]{:S(2)}) collective-permute-start(bf16[96,1024]{1,0:T(8,128)(2,1)S(1)} %slice.81), channel_id=1, source_target_pairs={{0,7},{1,0},{2,1},{3,2},{4,3},{5,4},{6,5},{7,6},{8,15},{9,8},{10,9... | collective-permute-start | bytes 589832 | tf_op jit(solution)/shard_map/ppermute | solution.py:465
  50.4 0.0 copy-start.4
  50.5 2.1 %collective-permute-start.4 = (bf16[96,1024]{1,0:T(8,128)(2,1)S(1)}, bf16[96,1024]{1,0:T(8,128)(2,1)S(1)}, u32[]{:S(2)}, u32[]{:S(2)}) collective-permute-start(bf16[96,1024]{1,0:T(8,128)(2,1)S(1)} %slice.80), channel_id=1, source_target_pairs={{0,1},{1,2},{2,3},{3,4},{4,5},{5,6},{6,7},{7,0},{8,9},{9,10},{10,1... | collective-permute-start | bytes 589832 | tf_op jit(solution)/shard_map/ppermute | solution.py:465
  52.6 0.1 add_convert_fusion.1
  52.6 3.2 %collective-permute-start.13 = (bf16[6,128,128]{2,1,0:T(8,128)(2,1)S(1)}, bf16[6,128,128]{2,1,0:T(8,128)(2,1)S(1)}, u32[]{:S(2)}, u32[]{:S(2)}) collective-permute-start(bf16[6,128,128]{2,1,0:T(8,128)(2,1)S(1)} %add_convert_fusion.1), channel_id=1, source_target_pairs={{0,48},{8,56},{16,64},{24,72},{32,80},{40,88},{48,96},{56,104},{64... | collective-permute-start | bytes 589832 | tf_op jit(solution)/shard_map/ppermute | solution.py:461
  55.8 4.2 %collective-permute-start.12 = (bf16[6,128,128]{2,1,0:T(8,128)(2,1)S(1)}, bf16[6,128,128]{2,1,0:T(8,128)(2,1)S(1)}, u32[]{:S(2)}, u32[]{:S(2)}) collective-permute-start(bf16[6,128,128]{2,1,0:T(8,128)(2,1)S(1)} %add_convert_fusion.1), channel_id=1, source_target_pairs={{0,16},{8,24},{16,32},{24,40},{32,48},{40,56},{48,64},{56,72},{64,... | collective-permute-start | bytes 589832 | tf_op jit(solution)/shard_map/ppermute | solution.py:461
  60.1 1.4 %share_part.1 = (f32[1536,128]{1,0:T(8,128)S(1)}, bf16[1536,128]{1,0:T(8,128)(2,1)S(1)}) custom-call(bf16[128,1024]{1,0:T(8,128)(2,1)S(1)} %copy-done.4, bf16[128,1024]{1,0:T(8,128)(2,1)S(1)} %collective-permute-done.cot_got_ref, bf16[192,1024]{1,0:T(8,128)(2,1)S(1)} %copy-done.3, bf16[192,1024]{1,0:T(8,128)(2,1)S(1)} %collective-permute-done.1.refs_1_, ...), custom_call_target="tpu_custom_call" | custom-call | flops 700000000 | bytes 4500000 | tf_op jit(solution)/shard_map/share_part/pallas_call | solution.py:281
  61.5 0.3 share_end.1
  61.8 2.9 %collective-permute-start.9 = (bf16[1536,128]{1,0:T(8,128)(2,1)S(1)}, bf16[1536,128]{1,0:T(8,128)(2,1)S(1)}, u32[]{:S(2)}, u32[]{:S(2)}) collective-permute-start(bf16[1536,128]{1,0:T(8,128)(2,1)S(1)} %get-tuple-element.35), channel_id=1, source_target_pairs={{0,8},{8,0},{1,9},{9,1},{2,10},{10,2},{3,11},{11,3},{4,12},{12,4},... | collective-permute-start | bytes 1179656 | tf_op jit(solution)/shard_map/ppermute | solution.py:455
  64.7 0.0 copy-start
  64.7 0.2 fusion.5
  65.0 2.3 %collective-permute-start.14 = (bf16[6,128,128]{2,1,0:T(8,128)(2,1)S(1)}, bf16[6,128,128]{2,1,0:T(8,128)(2,1)S(1)}, u32[]{:S(2)}, u32[]{:S(2)}) collective-permute-start(bf16[6,128,128]{2,1,0:T(8,128)(2,1)S(1)} %get-tuple-element.56), channel_id=1, source_target_pairs={{0,8},{8,0},{1,9},{9,1},{2,10},{10,2},{3,11},{11,3},{4,12},{12,4},... | collective-permute-start | bytes 589832 | tf_op jit(solution)/shard_map/ppermute | solution.py:455
  67.3 2.5 %inside_part.1 = (bf16[12,128,128]{2,1,0:T(8,128)(2,1)S(1)}, f32[128,1536]{1,0:T(8,128)S(1)}) custom-call(s32[1,16]{1,0:T(1,128)S(1)} %copy-done.5, bf16[128,1536]{1,0:T(8,128)(2,1)S(1)} %bitcast.44, bf16[128,1536]{1,0:T(8,128)(2,1)S(1)} %bitcast.49, bf16[128,1536]{1,0:T(8,128)(2,1)S(1)} %bitcast.53), custom_call_target="tpu_custom_call" | custom-call | flops 100000000 | bytes 2400000 | tf_op jit(solution)/shard_map/inside_part/pallas_call | solution.py:216
  69.8 1.0 mixed_part.1
  70.8 2.2 %grad_mixed_part.1 = (bf16[128,1536]{1,0:T(8,128)(2,1)S(1)}, bf16[6,128,128]{2,1,0:T(8,128)(2,1)S(1)}, bf16[6,128,128]{2,1,0:T(8,128)(2,1)S(1)}) custom-call(s32[1,16]{1,0:T(1,128)S(1)} %copy-done.5, f32[1536,128]{1,0:T(8,128)S(1)} %get-tuple-element.34.own_ref, bf16[1536,128]{1,0:T(8,128)(2,1)S(1)} %collective-permute-done.9.got_ref, ...), custom_call_target="tpu_custom_call" | custom-call | flops 60000000 | bytes 4000000 | tf_op jit(solution)/shard_map/grad_mixed_part/pallas_call | solution.py:345
  73.0 2.0 %collective-permute-start.17 = (bf16[6,128,128]{2,1,0:T(8,128)(2,1)S(1)}, bf16[6,128,128]{2,1,0:T(8,128)(2,1)S(1)}, u32[]{:S(2)}, u32[]{:S(2)}) collective-permute-start(bf16[6,128,128]{2,1,0:T(8,128)(2,1)S(1)} %get-tuple-element.48), channel_id=1, source_target_pairs={{0,8},{8,0},{1,9},{9,1},{2,10},{10,2},{3,11},{11,3},{4,12},{12,4},... | collective-permute-start | bytes 589832 | tf_op jit(solution)/shard_map/ppermute | solution.py:455
  75.1 1.3 %collective-permute-done.17 = bf16[6,128,128]{2,1,0:T(8,128)(2,1)S(1)} collective-permute-done((bf16[6,128,128]{2,1,0:T(8,128)(2,1)S(1)}, bf16[6,128,128]{2,1,0:T(8,128)(2,1)S(1)}, u32[]{:S(2)}, u32[]{:S(2)}) %collective-permute-start.17) | collective-permute-done | bytes 196640 | tf_op jit(solution)/shard_map/ppermute | solution.py:455
  76.4 0.1 fusion.9
  76.5 2.3 %collective-permute-start.18 = (bf16[6,128,128]{2,1,0:T(8,128)(2,1)S(1)}, bf16[6,128,128]{2,1,0:T(8,128)(2,1)S(1)}, u32[]{:S(2)}, u32[]{:S(2)}) collective-permute-start(bf16[6,128,128]{2,1,0:T(8,128)(2,1)S(1)} %fusion.9), channel_id=1, source_target_pairs={{16,0},{24,8},{32,16},{40,24},{48,32},{56,40},{64,48},{72,56},{80,... | collective-permute-start | bytes 589832 | tf_op jit(solution)/shard_map/ppermute | solution.py:461
  78.8 2.3 %collective-permute-start.15 = (bf16[128,1536]{1,0:T(8,128)(2,1)S(1)}, bf16[128,1536]{1,0:T(8,128)(2,1)S(1)}, u32[]{:S(2)}, u32[]{:S(2)}) collective-permute-start(bf16[128,1536]{1,0:T(8,128)(2,1)S(1)} %get-tuple-element.45.scaled_ref), channel_id=1, source_target_pairs={{0,8},{8,0},{1,9},{9,1},{2,10},{10,2},{3,11},{11,3},{4,12},{12,4},... | collective-permute-start | bytes 1179656 | tf_op jit(solution)/shard_map/ppermute | solution.py:455
  81.1 7.9 %collective-permute-done.18 = bf16[6,128,128]{2,1,0:T(8,128)(2,1)S(1)} collective-permute-done((bf16[6,128,128]{2,1,0:T(8,128)(2,1)S(1)}, bf16[6,128,128]{2,1,0:T(8,128)(2,1)S(1)}, u32[]{:S(2)}, u32[]{:S(2)}) %collective-permute-start.18) | collective-permute-done | bytes 196640 | tf_op jit(solution)/shard_map/ppermute | solution.py:461
  89.0 0.1 add_convert_fusion
  89.1 1.9 %collective-permute-start.20 = (bf16[6,128,128]{2,1,0:T(8,128)(2,1)S(1)}, bf16[6,128,128]{2,1,0:T(8,128)(2,1)S(1)}, u32[]{:S(2)}, u32[]{:S(2)}) collective-permute-start(bf16[6,128,128]{2,1,0:T(8,128)(2,1)S(1)} %add_convert_fusion), channel_id=1, source_target_pairs={{48,0},{56,8},{64,16},{72,24},{80,32},{88,40},{96,48},{104,56},{11... | collective-permute-start | bytes 589832 | tf_op jit(solution)/shard_map/ppermute | solution.py:461
  91.0 2.1 %collective-permute-start.19 = (bf16[6,128,128]{2,1,0:T(8,128)(2,1)S(1)}, bf16[6,128,128]{2,1,0:T(8,128)(2,1)S(1)}, u32[]{:S(2)}, u32[]{:S(2)}) collective-permute-start(bf16[6,128,128]{2,1,0:T(8,128)(2,1)S(1)} %add_convert_fusion), channel_id=1, source_target_pairs={{16,0},{24,8},{32,16},{40,24},{48,32},{56,40},{64,48},{72,56},{80,... | collective-permute-start | bytes 589832 | tf_op jit(solution)/shard_map/ppermute | solution.py:461
  93.2 1.2 %output_part.1 = (bf16[128,1024]{1,0:T(8,128)(2,1)S(1)}, bf16[128,1024]{1,0:T(8,128)(2,1)S(1)}) custom-call(bf16[128,1536]{1,0:T(8,128)(2,1)S(1)} %get-tuple-element.45.scaled_ref, bf16[128,1536]{1,0:T(8,128)(2,1)S(1)} %collective-permute-done.15.scaled_got_ref, bf16[192,1024]{1,0:T(8,128)(2,1)S(1)} %copy-done.3, ...), custom_call_target="tpu_custom_call" | custom-call | flops 810000000 | bytes 5000000 | tf_op jit(solution)/shard_map/output_part/pallas_call | solution.py:372
  94.4 3.2 %collective-permute-start.16 = (bf16[128,1024]{1,0:T(8,128)(2,1)S(1)}, bf16[128,1024]{1,0:T(8,128)(2,1)S(1)}, u32[]{:S(2)}, u32[]{:S(2)}) collective-permute-start(bf16[128,1024]{1,0:T(8,128)(2,1)S(1)} %get-tuple-element.47), channel_id=1, source_target_pairs={{0,8},{8,0},{1,9},{9,1},{2,10},{10,2},{3,11},{11,3},{4,12},{12,4},... | collective-permute-start | bytes 786440 | tf_op jit(solution)/shard_map/ppermute | solution.py:455
  97.6 1.2 %collective-permute-done.20 = bf16[6,128,128]{2,1,0:T(8,128)(2,1)S(1)} collective-permute-done((bf16[6,128,128]{2,1,0:T(8,128)(2,1)S(1)}, bf16[6,128,128]{2,1,0:T(8,128)(2,1)S(1)}, u32[]{:S(2)}, u32[]{:S(2)}) %collective-permute-start.20) | collective-permute-done | bytes 196640 | tf_op jit(solution)/shard_map/ppermute | solution.py:461
  98.8 3.1 %collective-permute-done.19 = bf16[6,128,128]{2,1,0:T(8,128)(2,1)S(1)} collective-permute-done((bf16[6,128,128]{2,1,0:T(8,128)(2,1)S(1)}, bf16[6,128,128]{2,1,0:T(8,128)(2,1)S(1)}, u32[]{:S(2)}, u32[]{:S(2)}) %collective-permute-start.19) | collective-permute-done | bytes 196640 | tf_op jit(solution)/shard_map/ppermute | solution.py:461
  102.0 0.2 fusion.11
  102.2 3.5 %collective-permute-start.21 = (bf16[6,128,128]{2,1,0:T(8,128)(2,1)S(1)}, bf16[6,128,128]{2,1,0:T(8,128)(2,1)S(1)}, u32[]{:S(2)}, u32[]{:S(2)}) collective-permute-start(bf16[6,128,128]{2,1,0:T(8,128)(2,1)S(1)} %get-tuple-element.54), channel_id=1, source_target_pairs={{0,8},{8,0},{1,9},{9,1},{2,10},{10,2},{3,11},{11,3},{4,12},{12,4},... | collective-permute-start | bytes 589832 | tf_op jit(solution)/shard_map/ppermute | solution.py:455
  105.7 4.0 %grads_part.1 = (bf16[128,1536]{1,0:T(8,128)(2,1)}, f32[128,1536]{1,0:T(8,128)S(1)}, f32[128,1536]{1,0:T(8,128)S(1)}) custom-call(s32[1,16]{1,0:T(1,128)S(1)} %copy-done.5, bf16[128,1536]{1,0:T(8,128)(2,1)S(1)} %bitcast.47, bf16[128,1536]{1,0:T(8,128)(2,1)S(1)} %bitcast.50, bf16[128,1536]{1,0:T(8,128)(2,1)S(1)} %bitcast.54, ...), custom_call_target="tpu_custom_call" | custom-call | flops 250000000 | bytes 5000000 | tf_op jit(solution)/shard_map/grads_part/pallas_call | solution.py:408
  109.7 2.1 %last_part.1 = (bf16[128,1536]{1,0:T(8,128)(2,1)}, bf16[128,1536]{1,0:T(8,128)(2,1)}, bf16[128,2048]{1,0:T(8,128)(2,1)}) custom-call(s32[1,16]{1,0:T(1,128)S(1)} %copy-done.5, bf16[128,1536]{1,0:T(8,128)(2,1)S(1)} %bitcast.51, bf16[128,1536]{1,0:T(8,128)(2,1)S(1)} %bitcast.55, f32[128,1536]{1,0:T(8,128)S(1)} %get-tuple-element.43.dk_part_ref, ...), custom_call_target="tpu_custom_call" | custom-call | flops 100000000 | bytes 4500000 | tf_op jit(solution)/shard_map/last_part/pallas_call | solution.py:443
  (32 shorter events, 0.1 us)
Async XLA Ops:
  0.6 22.6 %copy-start.1 = (bf16[1,128,1536]{2,1,0:T(8,128)(2,1)S(1)}, bf16[1,128,1536]{2,1,0:T(8,128)(2,1)}, u32[]{:S(2)}) copy-start(bf16[1,128,1536]{2,1,0:T(8,128)(2,1)} %param.8) | copy-start | bytes 1179652
  0.6 22.6 %copy-start.2 = (bf16[1,128,1536]{2,1,0:T(8,128)(2,1)S(1)}, bf16[1,128,1536]{2,1,0:T(8,128)(2,1)}, u32[]{:S(2)}) copy-start(bf16[1,128,1536]{2,1,0:T(8,128)(2,1)} %param.9) | copy-start | bytes 1179652
  2.8 13.2 %collective-permute-start.5 = (bf16[192,1024]{1,0:T(8,128)(2,1)}, bf16[192,1024]{1,0:T(8,128)(2,1)S(1)}, u32[]{:S(2)}, u32[]{:S(2)}) collective-permute-start(bf16[192,1024]{1,0:T(8,128)(2,1)} %get-tuple-element.31.refs_0_), channel_id=1, source_target_pairs={{0,7},{1,0},{2,1},{3,2},{4,3},{5,4},{6,5},{7,6},{8,15},{9,8},{10,9... | collective-permute-start | bytes 1179656 | tf_op jit(solution)/shard_map/ppermute | solution.py:465
  7.9 13.3 %collective-permute-start.1 = (bf16[192,1024]{1,0:T(8,128)(2,1)}, bf16[192,1024]{1,0:T(8,128)(2,1)S(1)}, u32[]{:S(2)}, u32[]{:S(2)}) collective-permute-start(bf16[192,1024]{1,0:T(8,128)(2,1)} %get-tuple-element.31.refs_0_), channel_id=1, source_target_pairs={{0,1},{1,2},{2,3},{3,4},{4,5},{5,6},{6,7},{7,0},{8,9},{9,10},{10,1... | collective-permute-start | bytes 1179656 | tf_op jit(solution)/shard_map/ppermute | solution.py:465
  16.0 12.9 %collective-permute-start.6 = (bf16[192,1024]{1,0:T(8,128)(2,1)S(1)}, bf16[192,1024]{1,0:T(8,128)(2,1)S(1)}, u32[]{:S(2)}, u32[]{:S(2)}) collective-permute-start(bf16[192,1024]{1,0:T(8,128)(2,1)S(1)} %collective-permute-done.5.refs_2_), channel_id=1, source_target_pairs={{0,7},{1,0},{2,1},{3,2},{4,3},{5,4},{6,5},{7,6},{8,15},{9,8},{10,9... | collective-permute-start | bytes 1179656 | tf_op jit(solution)/shard_map/ppermute | solution.py:465
  21.2 12.6 %collective-permute-start.2 = (bf16[192,1024]{1,0:T(8,128)(2,1)S(1)}, bf16[192,1024]{1,0:T(8,128)(2,1)S(1)}, u32[]{:S(2)}, u32[]{:S(2)}) collective-permute-start(bf16[192,1024]{1,0:T(8,128)(2,1)S(1)} %collective-permute-done.1.refs_1_), channel_id=1, source_target_pairs={{0,1},{1,2},{2,3},{3,4},{4,5},{5,6},{6,7},{7,0},{8,9},{9,10},{10,1... | collective-permute-start | bytes 1179656 | tf_op jit(solution)/shard_map/ppermute | solution.py:465
  23.2 0.7 copy-start.5
  25.2 10.6 %collective-permute-start.10 = (bf16[6,128,128]{2,1,0:T(8,128)(2,1)S(1)}, bf16[6,128,128]{2,1,0:T(8,128)(2,1)S(1)}, u32[]{:S(2)}, u32[]{:S(2)}) collective-permute-start(bf16[6,128,128]{2,1,0:T(8,128)(2,1)S(1)} %get-tuple-element.38), channel_id=1, source_target_pairs={{0,8},{8,0},{1,9},{9,1},{2,10},{10,2},{3,11},{11,3},{4,12},{12,4},... | collective-permute-start | bytes 589832 | tf_op jit(solution)/shard_map/ppermute | solution.py:455
  28.9 16.6 %collective-permute-start.7 = (bf16[192,1024]{1,0:T(8,128)(2,1)S(1)}, bf16[192,1024]{1,0:T(8,128)(2,1)S(1)}, u32[]{:S(2)}, u32[]{:S(2)}) collective-permute-start(bf16[192,1024]{1,0:T(8,128)(2,1)S(1)} %collective-permute-done.6.refs_4_), channel_id=1, source_target_pairs={{0,7},{1,0},{2,1},{3,2},{4,3},{5,4},{6,5},{7,6},{8,15},{9,8},{10,9... | collective-permute-start | bytes 1179656 | tf_op jit(solution)/shard_map/ppermute | solution.py:465
  33.8 16.6 %collective-permute-start.3 = (bf16[192,1024]{1,0:T(8,128)(2,1)S(1)}, bf16[192,1024]{1,0:T(8,128)(2,1)S(1)}, u32[]{:S(2)}, u32[]{:S(2)}) collective-permute-start(bf16[192,1024]{1,0:T(8,128)(2,1)S(1)} %collective-permute-done.2.refs_3_), channel_id=1, source_target_pairs={{0,1},{1,2},{2,3},{3,4},{4,5},{5,6},{6,7},{7,0},{8,9},{9,10},{10,1... | collective-permute-start | bytes 1179656 | tf_op jit(solution)/shard_map/ppermute | solution.py:465
  35.7 5.2 %copy-start.7 = (bf16[128,1024]{1,0:T(8,128)(2,1)S(1)}, bf16[128,1024]{1,0:T(8,128)(2,1)}, u32[]{:S(2)}) copy-start(bf16[128,1024]{1,0:T(8,128)(2,1)} %get-tuple-element.30) | copy-start | bytes 786436
  35.9 16.7 %collective-permute-start.11 = (bf16[6,128,128]{2,1,0:T(8,128)(2,1)S(1)}, bf16[6,128,128]{2,1,0:T(8,128)(2,1)S(1)}, u32[]{:S(2)}, u32[]{:S(2)}) collective-permute-start(bf16[6,128,128]{2,1,0:T(8,128)(2,1)S(1)} %fusion.3), channel_id=1, source_target_pairs={{0,16},{8,24},{16,32},{24,40},{32,48},{40,56},{48,64},{56,72},{64,... | collective-permute-start | bytes 589832 | tf_op jit(solution)/shard_map/ppermute | solution.py:461
  41.0 19.1 %collective-permute-start = (bf16[128,1024]{1,0:T(8,128)(2,1)S(1)}, bf16[128,1024]{1,0:T(8,128)(2,1)S(1)}, u32[]{:S(2)}, u32[]{:S(2)}) collective-permute-start(bf16[128,1024]{1,0:T(8,128)(2,1)S(1)} %copy-done.7), channel_id=1, source_target_pairs={{0,8},{8,0},{1,9},{9,1},{2,10},{10,2},{3,11},{11,3},{4,12},{12,4},... | collective-permute-start | bytes 786440 | tf_op jit(solution)/shard_map/ppermute | solution.py:455
  45.6 15.9 %collective-permute-start.8 = (bf16[96,1024]{1,0:T(8,128)(2,1)S(1)}, bf16[96,1024]{1,0:T(8,128)(2,1)S(1)}, u32[]{:S(2)}, u32[]{:S(2)}) collective-permute-start(bf16[96,1024]{1,0:T(8,128)(2,1)S(1)} %slice.81), channel_id=1, source_target_pairs={{0,7},{1,0},{2,1},{3,2},{4,3},{5,4},{6,5},{7,6},{8,15},{9,8},{10,9... | collective-permute-start | bytes 589832 | tf_op jit(solution)/shard_map/ppermute | solution.py:465
  50.4 9.6 %copy-start.4 = (bf16[128,1024]{1,0:T(8,128)(2,1)S(1)}, bf16[128,1024]{1,0:T(8,128)(2,1)}, u32[]{:S(2)}) copy-start(bf16[128,1024]{1,0:T(8,128)(2,1)} %get-tuple-element.29.cot_keep_ref) | copy-start | bytes 786436
  50.5 9.6 %copy-start.3 = (bf16[192,1024]{1,0:T(8,128)(2,1)S(1)}, bf16[192,1024]{1,0:T(8,128)(2,1)}, u32[]{:S(2)}) copy-start(bf16[192,1024]{1,0:T(8,128)(2,1)} %get-tuple-element.31.refs_0_) | copy-start | bytes 1179652
  50.5 11.0 %collective-permute-start.4 = (bf16[96,1024]{1,0:T(8,128)(2,1)S(1)}, bf16[96,1024]{1,0:T(8,128)(2,1)S(1)}, u32[]{:S(2)}, u32[]{:S(2)}) collective-permute-start(bf16[96,1024]{1,0:T(8,128)(2,1)S(1)} %slice.80), channel_id=1, source_target_pairs={{0,1},{1,2},{2,3},{3,4},{4,5},{5,6},{6,7},{7,0},{8,9},{9,10},{10,1... | collective-permute-start | bytes 589832 | tf_op jit(solution)/shard_map/ppermute | solution.py:465
  52.6 12.1 %collective-permute-start.13 = (bf16[6,128,128]{2,1,0:T(8,128)(2,1)S(1)}, bf16[6,128,128]{2,1,0:T(8,128)(2,1)S(1)}, u32[]{:S(2)}, u32[]{:S(2)}) collective-permute-start(bf16[6,128,128]{2,1,0:T(8,128)(2,1)S(1)} %add_convert_fusion.1), channel_id=1, source_target_pairs={{0,48},{8,56},{16,64},{24,72},{32,80},{40,88},{48,96},{56,104},{64... | collective-permute-start | bytes 589832 | tf_op jit(solution)/shard_map/ppermute | solution.py:461
  55.8 8.9 %collective-permute-start.12 = (bf16[6,128,128]{2,1,0:T(8,128)(2,1)S(1)}, bf16[6,128,128]{2,1,0:T(8,128)(2,1)S(1)}, u32[]{:S(2)}, u32[]{:S(2)}) collective-permute-start(bf16[6,128,128]{2,1,0:T(8,128)(2,1)S(1)} %add_convert_fusion.1), channel_id=1, source_target_pairs={{0,16},{8,24},{16,32},{24,40},{32,48},{40,56},{48,64},{56,72},{64,... | collective-permute-start | bytes 589832 | tf_op jit(solution)/shard_map/ppermute | solution.py:461
  61.8 9.0 %collective-permute-start.9 = (bf16[1536,128]{1,0:T(8,128)(2,1)S(1)}, bf16[1536,128]{1,0:T(8,128)(2,1)S(1)}, u32[]{:S(2)}, u32[]{:S(2)}) collective-permute-start(bf16[1536,128]{1,0:T(8,128)(2,1)S(1)} %get-tuple-element.35), channel_id=1, source_target_pairs={{0,8},{8,0},{1,9},{9,1},{2,10},{10,2},{3,11},{11,3},{4,12},{12,4},... | collective-permute-start | bytes 1179656 | tf_op jit(solution)/shard_map/ppermute | solution.py:455
  64.7 2.5 %copy-start.6 = (f32[1536]{0:T(1024)S(1)}, f32[1536]{0:T(1024)}, u32[]{:S(2)}) copy-start(f32[1536]{0:T(1024)} %param.11) | copy-start | bytes 18436
  64.7 2.6 %copy-start = (bf16[1,128,1536]{2,1,0:T(8,128)(2,1)S(1)}, bf16[1,128,1536]{2,1,0:T(8,128)(2,1)}, u32[]{:S(2)}) copy-start(bf16[1,128,1536]{2,1,0:T(8,128)(2,1)} %param.7) | copy-start | bytes 1179652
  65.0 4.8 %collective-permute-start.14 = (bf16[6,128,128]{2,1,0:T(8,128)(2,1)S(1)}, bf16[6,128,128]{2,1,0:T(8,128)(2,1)S(1)}, u32[]{:S(2)}, u32[]{:S(2)}) collective-permute-start(bf16[6,128,128]{2,1,0:T(8,128)(2,1)S(1)} %get-tuple-element.56), channel_id=1, source_target_pairs={{0,8},{8,0},{1,9},{9,1},{2,10},{10,2},{3,11},{11,3},{4,12},{12,4},... | collective-permute-start | bytes 589832 | tf_op jit(solution)/shard_map/ppermute | solution.py:455
  73.0 3.3 %collective-permute-start.17 = (bf16[6,128,128]{2,1,0:T(8,128)(2,1)S(1)}, bf16[6,128,128]{2,1,0:T(8,128)(2,1)S(1)}, u32[]{:S(2)}, u32[]{:S(2)}) collective-permute-start(bf16[6,128,128]{2,1,0:T(8,128)(2,1)S(1)} %get-tuple-element.48), channel_id=1, source_target_pairs={{0,8},{8,0},{1,9},{9,1},{2,10},{10,2},{3,11},{11,3},{4,12},{12,4},... | collective-permute-start | bytes 589832 | tf_op jit(solution)/shard_map/ppermute | solution.py:455
  76.5 12.6 %collective-permute-start.18 = (bf16[6,128,128]{2,1,0:T(8,128)(2,1)S(1)}, bf16[6,128,128]{2,1,0:T(8,128)(2,1)S(1)}, u32[]{:S(2)}, u32[]{:S(2)}) collective-permute-start(bf16[6,128,128]{2,1,0:T(8,128)(2,1)S(1)} %fusion.9), channel_id=1, source_target_pairs={{16,0},{24,8},{32,16},{40,24},{48,32},{56,40},{64,48},{72,56},{80,... | collective-permute-start | bytes 589832 | tf_op jit(solution)/shard_map/ppermute | solution.py:461
  78.8 14.4 %collective-permute-start.15 = (bf16[128,1536]{1,0:T(8,128)(2,1)S(1)}, bf16[128,1536]{1,0:T(8,128)(2,1)S(1)}, u32[]{:S(2)}, u32[]{:S(2)}) collective-permute-start(bf16[128,1536]{1,0:T(8,128)(2,1)S(1)} %get-tuple-element.45.scaled_ref), channel_id=1, source_target_pairs={{0,8},{8,0},{1,9},{9,1},{2,10},{10,2},{3,11},{11,3},{4,12},{12,4},... | collective-permute-start | bytes 1179656 | tf_op jit(solution)/shard_map/ppermute | solution.py:455
  89.1 9.7 %collective-permute-start.20 = (bf16[6,128,128]{2,1,0:T(8,128)(2,1)S(1)}, bf16[6,128,128]{2,1,0:T(8,128)(2,1)S(1)}, u32[]{:S(2)}, u32[]{:S(2)}) collective-permute-start(bf16[6,128,128]{2,1,0:T(8,128)(2,1)S(1)} %add_convert_fusion), channel_id=1, source_target_pairs={{48,0},{56,8},{64,16},{72,24},{80,32},{88,40},{96,48},{104,56},{11... | collective-permute-start | bytes 589832 | tf_op jit(solution)/shard_map/ppermute | solution.py:461
  91.0 11.0 %collective-permute-start.19 = (bf16[6,128,128]{2,1,0:T(8,128)(2,1)S(1)}, bf16[6,128,128]{2,1,0:T(8,128)(2,1)S(1)}, u32[]{:S(2)}, u32[]{:S(2)}) collective-permute-start(bf16[6,128,128]{2,1,0:T(8,128)(2,1)S(1)} %add_convert_fusion), channel_id=1, source_target_pairs={{16,0},{24,8},{32,16},{40,24},{48,32},{56,40},{64,48},{72,56},{80,... | collective-permute-start | bytes 589832 | tf_op jit(solution)/shard_map/ppermute | solution.py:461
  94.4 15.2 %collective-permute-start.16 = (bf16[128,1024]{1,0:T(8,128)(2,1)S(1)}, bf16[128,1024]{1,0:T(8,128)(2,1)S(1)}, u32[]{:S(2)}, u32[]{:S(2)}) collective-permute-start(bf16[128,1024]{1,0:T(8,128)(2,1)S(1)} %get-tuple-element.47), channel_id=1, source_target_pairs={{0,8},{8,0},{1,9},{9,1},{2,10},{10,2},{3,11},{11,3},{4,12},{12,4},... | collective-permute-start | bytes 786440 | tf_op jit(solution)/shard_map/ppermute | solution.py:455
  102.2 7.5 %collective-permute-start.21 = (bf16[6,128,128]{2,1,0:T(8,128)(2,1)S(1)}, bf16[6,128,128]{2,1,0:T(8,128)(2,1)S(1)}, u32[]{:S(2)}, u32[]{:S(2)}) collective-permute-start(bf16[6,128,128]{2,1,0:T(8,128)(2,1)S(1)} %get-tuple-element.54), channel_id=1, source_target_pairs={{0,8},{8,0},{1,9},{9,1},{2,10},{10,2},{3,11},{11,3},{4,12},{12,4},... | collective-permute-start | bytes 589832 | tf_op jit(solution)/shard_map/ppermute | solution.py:455

commit v3 on v2

--- a/solution.py
+++ b/solution.py
@@ -22,6 +22,7 @@
 
 CA, CB, MP, ME1, ME3, CS, ES, CR, ER = range(9)
 BACK = 9
+BACK_2, BACK_4 = 18, 19
 ROWS = 24
 
 VMEM = pl.BlockSpec(memory_space=pltpu.VMEM)
@@ -177,7 +178,9 @@
     put(BACK + ES, jnp.where(low, one, across))
     put(BACK + CR, jnp.where(low, one, zero))
     put(BACK + ER, jnp.where(low, across, one))
-    for row in range(2 * BACK, ROWS):
+    put(BACK_2, flag((chip <= CHIPS - 3) & same(ends, base + 256, base + 512)))
+    put(BACK_4, flag((chip <= CHIPS - 5) & same(ends, base + 256, base + 1024)))
+    for row in range(BACK_4 + 1, ROWS):
         put(row, zero)
 
 
@@ -255,21 +258,22 @@
     )(lengths, queries, inside, mine, other, gain)
 
 
-def shard_rows(distance, count=SHARD, skip=0):
-    owner = lax.rem(lax.axis_index("fsdp") + (distance + Y), Y)
-    return pl.ds(pl.multiple_of(owner * SHARD + skip, 32), count)
-
-
-EARLY = (0, -1, 1, -2, 2, -3, 3)
+def shard_rows(step):
+    way = 2 * lax.axis_index("core") - 1
+    owner = lax.rem(lax.axis_index("fsdp") + Y + way * step, Y)
+    return pl.ds(pl.multiple_of(owner * SHARD, 64), SHARD)
+
+
+EARLY = range(Y - 1)
 
 
 def share_kernel(cot_keep_ref, cot_got_ref, *refs):
     pieces, (own_ref, give_ref, cot_ref) = refs[: len(EARLY)], refs[len(EARLY) :]
     cot_ref[:TOK] = cot_keep_ref[...]
     cot_ref[TOK:] = cot_got_ref[...]
-    for distance, piece in zip(EARLY, pieces):
+    for step, piece in zip(EARLY, pieces):
         share = dot(piece[...], cot_ref[...], NT)
-        rows = shard_rows(distance)
+        rows = shard_rows(step)
         own_ref[rows, :] = share[:, :TOK]
         give_ref[rows, :] = share[:, TOK:].astype(BF16)
 
@@ -291,31 +295,29 @@
 
 
 def share_end_kernel(
-    cot_keep_ref, cot_got_ref, top_ref, bottom_ref, own_in_ref, give_in_ref, own_ref, give_ref, cot_ref, piece_ref
+    cot_keep_ref, cot_got_ref, piece_ref, own_in_ref, give_in_ref, own_ref, give_ref, cot_ref
 ):
     cot_ref[:TOK] = cot_keep_ref[...]
     cot_ref[TOK:] = cot_got_ref[...]
-    piece_ref[: SHARD // 2] = top_ref[...]
-    piece_ref[SHARD // 2 :] = bottom_ref[...]
     own_ref[...] = own_in_ref[...]
     give_ref[...] = give_in_ref[...]
     share = dot(piece_ref[...], cot_ref[...], NT)
-    rows = shard_rows(4)
+    rows = shard_rows(Y - 1)
     own_ref[rows, :] = share[:, :TOK]
     give_ref[rows, :] = share[:, TOK:].astype(BF16)
 
 
-def share_end(cot_keep, cot_got, top, bottom, own, give):
+def share_end(cot_keep, cot_got, piece, own, give):
     return pl.pallas_call(
         share_end_kernel,
         out_shape=SHARE_SHAPES,
-        in_specs=[VMEM] * 6,
+        in_specs=[VMEM] * 5,
         out_specs=(VMEM, VMEM),
-        scratch_shapes=[pltpu.VMEM((2 * TOK, D // 2), BF16), pltpu.VMEM((SHARD, D // 2), BF16)],
+        scratch_shapes=[pltpu.VMEM((2 * TOK, D // 2), BF16)],
         compiler_params=params(),
         cost_estimate=cost(100_000_000, 3_500_000),
         name="share_end",
-    )(cot_keep, cot_got, top, bottom, own, give)
+    )(cot_keep, cot_got, piece, own, give)
 
 
 def grad_mixed_kernel(
@@ -354,11 +356,9 @@
 
 
 def output_kernel(scaled_ref, scaled_got_ref, *refs):
-    pieces, (top_ref, bottom_ref, own_ref, give_ref, both_ref, weight_ref) = refs[: len(EARLY)], refs[len(EARLY) :]
-    for distance, piece in zip(EARLY, pieces):
-        weight_ref[shard_rows(distance), :] = piece[...]
-    weight_ref[shard_rows(4, SHARD // 2), :] = top_ref[...]
-    weight_ref[shard_rows(4, SHARD // 2, SHARD // 2), :] = bottom_ref[...]
+    pieces, (own_ref, give_ref, both_ref, weight_ref) = refs[:Y], refs[Y:]
+    for step, piece in enumerate(pieces):
+        weight_ref[shard_rows(step), :] = piece[...]
     both_ref[:TOK] = scaled_ref[...]
     both_ref[TOK:] = scaled_got_ref[...]
     for start in range(0, D // 2, 256):
@@ -367,18 +367,18 @@
         give_ref[:, start : start + 256] = block[TOK:]
 
 
-def output_part(scaled, scaled_got, pieces, top, bottom):
+def output_part(scaled, scaled_got, pieces):
     half = jax.ShapeDtypeStruct((TOK, D // 2), BF16)
     return pl.pallas_call(
         output_kernel,
         out_shape=(half, half),
-        in_specs=[VMEM] * (4 + len(EARLY)),
+        in_specs=[VMEM] * (2 + Y),
         out_specs=(VMEM, VMEM),
         scratch_shapes=[pltpu.VMEM((2 * TOK, DI), BF16), pltpu.VMEM((DI, D // 2), BF16)],
         compiler_params=params(),
         cost_estimate=cost(810_000_000, 5_000_000),
         name="output_part",
-    )(scaled, scaled_got, *pieces, top, bottom)
+    )(scaled, scaled_got, *pieces)
 
 
 def grads_kernel(
@@ -461,8 +461,9 @@
     return lax.ppermute(block, ("z", "x", "core"), pairs)
 
 
-def along_y(block, distance):
-    return lax.ppermute(block, "fsdp", [(i, (i + distance) % Y) for i in range(Y)])
+def along_y(block):
+    pairs = [(i, (i + 1) % Y) for i in range(Y)] + [(Y + i, Y + (i - 1) % Y) for i in range(Y)]
+    return lax.ppermute(block, ("core", "fsdp"), pairs)
 
 
 def window(keep, give, coef, sign):
@@ -472,11 +473,17 @@
     got = swap_cores(give).astype(F32)
     own = keep.astype(F32)
     chip_sum = (row(CA) * own + row(CB) * got).astype(BF16)
-    before = from_chip(chip_sum, sign)
-    pair_sum = (chip_sum.astype(F32) + row(MP) * before.astype(F32)).astype(BF16)
-    near = from_chip(pair_sum, sign)
-    far = from_chip(pair_sum, 3 * sign)
-    enter = row(ME1) * near.astype(F32) + row(ME3) * far.astype(F32)
+    if sign > 0:
+        before = from_chip(chip_sum, sign)
+        pair_sum = (chip_sum.astype(F32) + row(MP) * before.astype(F32)).astype(BF16)
+        near = from_chip(pair_sum, sign)
+        far = from_chip(pair_sum, 3 * sign)
+        enter = row(ME1) * near.astype(F32) + row(ME3) * far.astype(F32)
+    else:
+        sums = []
+        for chips in (1, 2, 3, 4):
+            sums.append(from_chip(chip_sum, chips * sign).astype(F32))
+        enter = row(ME1) * sums[0] + coef[BACK_2] * sums[1] + row(ME3) * sums[2] + coef[BACK_4] * sums[3]
     other = swap_cores((row(CS) * own + row(ES) * enter).astype(BF16))
     mine = (row(CR) * got + row(ER) * enter).astype(BF16)
     return mine, other
@@ -486,13 +493,9 @@
     queries, keys, values, cotangent = queries[0], keys[0], values[0], cotangent[0]
     gain_row = gain.reshape(1, DI)
     half, cot_keep, cot_give = take_half(out_weight, cotangent)
-    up, down = [half], [half]
-    for _ in range(1, 4):
-        up.append(along_y(up[-1], 1))
-        down.append(along_y(down[-1], -1))
-    top = along_y(up[3][: SHARD // 2], 1)
-    bottom = along_y(down[3][SHARD // 2 :], -1)
-    pieces = (half, up[1], down[1], up[2], down[2], up[3], down[3])
+    pieces = [half]
+    for _ in range(1, Y):
+        pieces.append(along_y(pieces[-1]))
     cot_got = swap_cores(cot_give)
 
     keep, give, coef = local_state(lengths, keys, values)
@@ -500,12 +503,12 @@
     attn, inside = inside_part(lengths, queries, keys, values)
     mixed, scaled = mixed_part(lengths, queries, inside, mine, other, gain_row)
     scaled_got = swap_cores(scaled)
-    own_share, give_share = share_part(cot_keep, cot_got, pieces)
-    own_share, give_share = share_end(cot_keep, cot_got, top, bottom, own_share, give_share)
+    own_share, give_share = share_part(cot_keep, cot_got, pieces[:-1])
+    own_share, give_share = share_end(cot_keep, cot_got, pieces[-1], own_share, give_share)
     got_share = swap_cores(give_share)
     low, give_back, keep_back = grad_mixed_part(lengths, own_share, got_share, mixed, gain_row, queries)
     back_mine, back_other = window(keep_back, give_back, coef, -1)
-    out_own, out_give = output_part(scaled, scaled_got, pieces, top, bottom)
+    out_own, out_give = output_part(scaled, scaled_got, pieces)
     out_got = swap_cores(out_give)
     dq, dk_part, dv_part = grads_part(lengths, queries, keys, values, low, attn, mine, other)
     dk, dv, output = last_part(lengths, keys, values, dk_part, dv_part, out_own, out_got, back_mine, back_other)

time: 112 us -> 134 us (1.20)
  the two profiles are of different devices: /device:TPU:199 before, /device:TPU:223 now
where the time goes in v3:
time: 134 us; the launch traced here: 133 us
  starting transfers between devices  69.5 us (52%)
  waiting for transfers between devices  43.3 us (32%)
  Pallas kernels  18.2 us (14%)
    ppermute x8, starting transfers between devices, swap_cores(): return lax.ppermute(block, 'core', [(0, 1), (1, 0)])  34.2 us
    ppermute x7, waiting for transfers between devices, along_y(): return lax.ppermute(block, ('core', 'fsdp'), pairs)  31.3 us
    ppermute x7, starting transfers between devices, from_chip(): return lax.ppermute(block, ('z', 'x', 'core'), pairs)  21.7 us
    ppermute x7, starting transfers between devices, along_y(): return lax.ppermute(block, ('core', 'fsdp'), pairs)  13.6 us
    ppermute x7, waiting for transfers between devices, from_chip(): return lax.ppermute(block, ('z', 'x', 'core'), pairs)  12 us
    pallas_call x1, Pallas kernels, grads_part(): pl.pallas_call(grads_kernel, out_shape=(jax.ShapeDtypeStruct((TOK, DI), B...  3.98 us
  transfers between devices with their start and end apart: 22, of which 7 were waited for; matrix products, arithmetic and copies ran while one was open for 1% of the time, Pallas kernels for 9%

profile of v3, /device:TPU:223, one launch (start us, length us, event | category | flops | bytes accessed | tf_op | source)
XLA Modules:
  0.0 133.5 jit_solution(14572720624029911312)
XLA Ops:
  0.7 2.2 %take_half.1 = (bf16[192,1024]{1,0:T(8,128)(2,1)}, bf16[128,1024]{1,0:T(8,128)(2,1)}, bf16[128,1024]{1,0:T(8,128)(2,1)}) custom-call(bf16[192,2048]{1,0:T(8,128)(2,1)} %weight_ref.1, bf16[128,2048]{1,0:T(8,128)(2,1)} %bitcast.58), custom_call_target="tpu_custom_call" | custom-call | flops 1000 | bytes 2000000 | tf_op jit(solution)/shard_map/take_half/pallas_call | solution.py:116
  2.8 2.1 %collective-permute-start.1 = (bf16[192,1024]{1,0:T(8,128)(2,1)}, bf16[192,1024]{1,0:T(8,128)(2,1)S(1)}, u32[]{:S(2)}, u32[]{:S(2)}) collective-permute-start(bf16[192,1024]{1,0:T(8,128)(2,1)} %get-tuple-element.31.refs_0_), channel_id=1, source_target_pairs={{0,1},{1,2},{2,3},{3,4},{4,5},{5,6},{6,7},{7,0},{8,15},{9,8},{10,9... | collective-permute-start | bytes 1179656 | tf_op jit(solution)/shard_map/ppermute | solution.py:466
  4.9 7.9 %collective-permute-done.1.refs_1_ = bf16[192,1024]{1,0:T(8,128)(2,1)S(1)} collective-permute-done((bf16[192,1024]{1,0:T(8,128)(2,1)}, bf16[192,1024]{1,0:T(8,128)(2,1)S(1)}, u32[]{:S(2)}, u32[]{:S(2)}) %collective-permute-start.1) | collective-permute-done | bytes 393248 | tf_op jit(solution)/shard_map/ppermute | solution.py:466
  12.8 1.9 %collective-permute-start.2 = (bf16[192,1024]{1,0:T(8,128)(2,1)S(1)}, bf16[192,1024]{1,0:T(8,128)(2,1)S(1)}, u32[]{:S(2)}, u32[]{:S(2)}) collective-permute-start(bf16[192,1024]{1,0:T(8,128)(2,1)S(1)} %collective-permute-done.1.refs_1_), channel_id=1, source_target_pairs={{0,1},{1,2},{2,3},{3,4},{4,5},{5,6},{6,7},{7,0},{8,15},{9,8},{10,9... | collective-permute-start | bytes 1179656 | tf_op jit(solution)/shard_map/ppermute | solution.py:466
  14.7 7.8 %collective-permute-done.2.refs_2_ = bf16[192,1024]{1,0:T(8,128)(2,1)S(1)} collective-permute-done((bf16[192,1024]{1,0:T(8,128)(2,1)S(1)}, bf16[192,1024]{1,0:T(8,128)(2,1)S(1)}, u32[]{:S(2)}, u32[]{:S(2)}) %collective-permute-start.2) | collective-permute-done | bytes 393248 | tf_op jit(solution)/shard_map/ppermute | solution.py:466
  22.5 1.9 %collective-permute-start.3 = (bf16[192,1024]{1,0:T(8,128)(2,1)S(1)}, bf16[192,1024]{1,0:T(8,128)(2,1)S(1)}, u32[]{:S(2)}, u32[]{:S(2)}) collective-permute-start(bf16[192,1024]{1,0:T(8,128)(2,1)S(1)} %collective-permute-done.2.refs_2_), channel_id=1, source_target_pairs={{0,1},{1,2},{2,3},{3,4},{4,5},{5,6},{6,7},{7,0},{8,15},{9,8},{10,9... | collective-permute-start | bytes 1179656 | tf_op jit(solution)/shard_map/ppermute | solution.py:466
  24.4 7.8 %collective-permute-done.3.refs_3_ = bf16[192,1024]{1,0:T(8,128)(2,1)S(1)} collective-permute-done((bf16[192,1024]{1,0:T(8,128)(2,1)S(1)}, bf16[192,1024]{1,0:T(8,128)(2,1)S(1)}, u32[]{:S(2)}, u32[]{:S(2)}) %collective-permute-start.3) | collective-permute-done | bytes 393248 | tf_op jit(solution)/shard_map/ppermute | solution.py:466
  32.2 1.9 %collective-permute-start.4 = (bf16[192,1024]{1,0:T(8,128)(2,1)S(1)}, bf16[192,1024]{1,0:T(8,128)(2,1)S(1)}, u32[]{:S(2)}, u32[]{:S(2)}) collective-permute-start(bf16[192,1024]{1,0:T(8,128)(2,1)S(1)} %collective-permute-done.3.refs_3_), channel_id=1, source_target_pairs={{0,1},{1,2},{2,3},{3,4},{4,5},{5,6},{6,7},{7,0},{8,15},{9,8},{10,9... | collective-permute-start | bytes 1179656 | tf_op jit(solution)/shard_map/ppermute | solution.py:466
  34.1 7.8 %collective-permute-done.4.refs_4_ = bf16[192,1024]{1,0:T(8,128)(2,1)S(1)} collective-permute-done((bf16[192,1024]{1,0:T(8,128)(2,1)S(1)}, bf16[192,1024]{1,0:T(8,128)(2,1)S(1)}, u32[]{:S(2)}, u32[]{:S(2)}) %collective-permute-start.4) | collective-permute-done | bytes 393248 | tf_op jit(solution)/shard_map/ppermute | solution.py:466
  41.9 1.9 %collective-permute-start.5 = (bf16[192,1024]{1,0:T(8,128)(2,1)S(1)}, bf16[192,1024]{1,0:T(8,128)(2,1)S(1)}, u32[]{:S(2)}, u32[]{:S(2)}) collective-permute-start(bf16[192,1024]{1,0:T(8,128)(2,1)S(1)} %collective-permute-done.4.refs_4_), channel_id=1, source_target_pairs={{0,1},{1,2},{2,3},{3,4},{4,5},{5,6},{6,7},{7,0},{8,15},{9,8},{10,9... | collective-permute-start | bytes 1179656 | tf_op jit(solution)/shard_map/ppermute | solution.py:466
  43.8 0.0 copy-start.5
  43.9 0.6 copy-done.5
  44.5 1.4 %local_state.1 = (bf16[6,128,128]{2,1,0:T(8,128)(2,1)S(1)}, bf16[6,128,128]{2,1,0:T(8,128)(2,1)S(1)}, f32[24,128]{1,0:T(8,128)S(1)}) custom-call(s32[1,16]{1,0:T(1,128)S(1)} %copy-done.5, bf16[128,1536]{1,0:T(8,128)(2,1)S(1)} %bitcast.50, bf16[128,1536]{1,0:T(8,128)(2,1)S(1)} %bitcast.54), custom_call_target="tpu_custom_call" | custom-call | flops 50000000 | bytes 1200000 | tf_op jit(solution)/shard_map/local_state/pallas_call | solution.py:189
  45.9 10.0 %collective-permute-start.9 = (bf16[6,128,128]{2,1,0:T(8,128)(2,1)S(1)}, bf16[6,128,128]{2,1,0:T(8,128)(2,1)S(1)}, u32[]{:S(2)}, u32[]{:S(2)}) collective-permute-start(bf16[6,128,128]{2,1,0:T(8,128)(2,1)S(1)} %get-tuple-element.38), channel_id=1, source_target_pairs={{0,8},{8,0},{1,9},{9,1},{2,10},{10,2},{3,11},{11,3},{4,12},{12,4},... | collective-permute-start | bytes 589832 | tf_op jit(solution)/shard_map/ppermute | solution.py:455
  55.9 1.9 %collective-permute-start.6 = (bf16[192,1024]{1,0:T(8,128)(2,1)S(1)}, bf16[192,1024]{1,0:T(8,128)(2,1)S(1)}, u32[]{:S(2)}, u32[]{:S(2)}) collective-permute-start(bf16[192,1024]{1,0:T(8,128)(2,1)S(1)} %collective-permute-done.5.refs_5_), channel_id=1, source_target_pairs={{0,1},{1,2},{2,3},{3,4},{4,5},{5,6},{6,7},{7,0},{8,15},{9,8},{10,9... | collective-permute-start | bytes 1179656 | tf_op jit(solution)/shard_map/ppermute | solution.py:466
  57.8 0.0 copy-start.4
  57.8 0.1 fusion.3
  57.9 0.0 copy-start.3
  57.9 5.3 %collective-permute-start.10 = (bf16[6,128,128]{2,1,0:T(8,128)(2,1)S(1)}, bf16[6,128,128]{2,1,0:T(8,128)(2,1)S(1)}, u32[]{:S(2)}, u32[]{:S(2)}) collective-permute-start(bf16[6,128,128]{2,1,0:T(8,128)(2,1)S(1)} %fusion.3), channel_id=1, source_target_pairs={{0,16},{8,24},{16,32},{24,40},{32,48},{40,56},{48,64},{56,72},{64,... | collective-permute-start | bytes 589832 | tf_op jit(solution)/shard_map/ppermute | solution.py:461
  63.2 7.1 %collective-permute-start = (bf16[128,1024]{1,0:T(8,128)(2,1)S(1)}, bf16[128,1024]{1,0:T(8,128)(2,1)S(1)}, u32[]{:S(2)}, u32[]{:S(2)}) collective-permute-start(bf16[128,1024]{1,0:T(8,128)(2,1)S(1)} %copy-done.7), channel_id=1, source_target_pairs={{0,8},{8,0},{1,9},{9,1},{2,10},{10,2},{3,11},{11,3},{4,12},{12,4},... | collective-permute-start | bytes 786440 | tf_op jit(solution)/shard_map/ppermute | solution.py:455
  70.4 1.9 %collective-permute-start.7 = (bf16[192,1024]{1,0:T(8,128)(2,1)S(1)}, bf16[192,1024]{1,0:T(8,128)(2,1)S(1)}, u32[]{:S(2)}, u32[]{:S(2)}) collective-permute-start(bf16[192,1024]{1,0:T(8,128)(2,1)S(1)} %collective-permute-done.6.refs_6_), channel_id=1, source_target_pairs={{0,1},{1,2},{2,3},{3,4},{4,5},{5,6},{6,7},{7,0},{8,15},{9,8},{10,9... | collective-permute-start | bytes 1179656 | tf_op jit(solution)/shard_map/ppermute | solution.py:466
  72.3 0.1 add_convert_fusion
  72.4 3.2 %collective-permute-start.12 = (bf16[6,128,128]{2,1,0:T(8,128)(2,1)S(1)}, bf16[6,128,128]{2,1,0:T(8,128)(2,1)S(1)}, u32[]{:S(2)}, u32[]{:S(2)}) collective-permute-start(bf16[6,128,128]{2,1,0:T(8,128)(2,1)S(1)} %add_convert_fusion), channel_id=1, source_target_pairs={{0,48},{8,56},{16,64},{24,72},{32,80},{40,88},{48,96},{56,104},{64... | collective-permute-start | bytes 589832 | tf_op jit(solution)/shard_map/ppermute | solution.py:461
  75.6 4.2 %collective-permute-start.11 = (bf16[6,128,128]{2,1,0:T(8,128)(2,1)S(1)}, bf16[6,128,128]{2,1,0:T(8,128)(2,1)S(1)}, u32[]{:S(2)}, u32[]{:S(2)}) collective-permute-start(bf16[6,128,128]{2,1,0:T(8,128)(2,1)S(1)} %add_convert_fusion), channel_id=1, source_target_pairs={{0,16},{8,24},{16,32},{24,40},{32,48},{40,56},{48,64},{56,72},{64,... | collective-permute-start | bytes 589832 | tf_op jit(solution)/shard_map/ppermute | solution.py:461
  79.9 1.3 %share_part.1 = (f32[1536,128]{1,0:T(8,128)S(1)}, bf16[1536,128]{1,0:T(8,128)(2,1)S(1)}) custom-call(bf16[128,1024]{1,0:T(8,128)(2,1)S(1)} %copy-done.4, bf16[128,1024]{1,0:T(8,128)(2,1)S(1)} %collective-permute-done.cot_got_ref, bf16[192,1024]{1,0:T(8,128)(2,1)S(1)} %copy-done.3, bf16[192,1024]{1,0:T(8,128)(2,1)S(1)} %collective-permute-done.1.refs_1_, ...), custom_call_target="tpu_custom_call" | custom-call | flops 700000000 | bytes 4500000 | tf_op jit(solution)/shard_map/share_part/pallas_call | solution.py:285
  81.2 0.3 share_end.1
  81.6 5.9 %collective-permute-start.8 = (bf16[1536,128]{1,0:T(8,128)(2,1)S(1)}, bf16[1536,128]{1,0:T(8,128)(2,1)S(1)}, u32[]{:S(2)}, u32[]{:S(2)}) collective-permute-start(bf16[1536,128]{1,0:T(8,128)(2,1)S(1)} %get-tuple-element.35), channel_id=1, source_target_pairs={{0,8},{8,0},{1,9},{9,1},{2,10},{10,2},{3,11},{11,3},{4,12},{12,4},... | collective-permute-start | bytes 1179656 | tf_op jit(solution)/shard_map/ppermute | solution.py:455
  87.5 0.2 fusion.5
  87.7 1.9 %collective-permute-start.13 = (bf16[6,128,128]{2,1,0:T(8,128)(2,1)S(1)}, bf16[6,128,128]{2,1,0:T(8,128)(2,1)S(1)}, u32[]{:S(2)}, u32[]{:S(2)}) collective-permute-start(bf16[6,128,128]{2,1,0:T(8,128)(2,1)S(1)} %get-tuple-element.56), channel_id=1, source_target_pairs={{0,8},{8,0},{1,9},{9,1},{2,10},{10,2},{3,11},{11,3},{4,12},{12,4},... | collective-permute-start | bytes 589832 | tf_op jit(solution)/shard_map/ppermute | solution.py:455
  89.7 2.5 %inside_part.1 = (bf16[12,128,128]{2,1,0:T(8,128)(2,1)S(1)}, f32[128,1536]{1,0:T(8,128)S(1)}) custom-call(s32[1,16]{1,0:T(1,128)S(1)} %copy-done.5, bf16[128,1536]{1,0:T(8,128)(2,1)S(1)} %bitcast.46, bf16[128,1536]{1,0:T(8,128)(2,1)S(1)} %bitcast.51, bf16[128,1536]{1,0:T(8,128)(2,1)S(1)} %bitcast.55), custom_call_target="tpu_custom_call" | custom-call | flops 100000000 | bytes 2400000 | tf_op jit(solution)/shard_map/inside_part/pallas_call | solution.py:219
  92.2 1.0 mixed_part.1
  93.2 2.2 %grad_mixed_part.1 = (bf16[128,1536]{1,0:T(8,128)(2,1)S(1)}, bf16[6,128,128]{2,1,0:T(8,128)(2,1)S(1)}, bf16[6,128,128]{2,1,0:T(8,128)(2,1)S(1)}) custom-call(s32[1,16]{1,0:T(1,128)S(1)} %copy-done.5, f32[1536,128]{1,0:T(8,128)S(1)} %get-tuple-element.34.own_ref, bf16[1536,128]{1,0:T(8,128)(2,1)S(1)} %collective-permute-done.8.got_ref, ...), custom_call_target="tpu_custom_call" | custom-call | flops 60000000 | bytes 4000000 | tf_op jit(solution)/shard_map/grad_mixed_part/pallas_call | solution.py:347
  95.4 2.4 %collective-permute-start.16 = (bf16[6,128,128]{2,1,0:T(8,128)(2,1)S(1)}, bf16[6,128,128]{2,1,0:T(8,128)(2,1)S(1)}, u32[]{:S(2)}, u32[]{:S(2)}) collective-permute-start(bf16[6,128,128]{2,1,0:T(8,128)(2,1)S(1)} %get-tuple-element.48), channel_id=1, source_target_pairs={{0,8},{8,0},{1,9},{9,1},{2,10},{10,2},{3,11},{11,3},{4,12},{12,4},... | collective-permute-start | bytes 589832 | tf_op jit(solution)/shard_map/ppermute | solution.py:455
  97.8 1.9 %collective-permute-start.14 = (bf16[128,1536]{1,0:T(8,128)(2,1)S(1)}, bf16[128,1536]{1,0:T(8,128)(2,1)S(1)}, u32[]{:S(2)}, u32[]{:S(2)}) collective-permute-start(bf16[128,1536]{1,0:T(8,128)(2,1)S(1)} %get-tuple-element.45.scaled_ref), channel_id=1, source_target_pairs={{0,8},{8,0},{1,9},{9,1},{2,10},{10,2},{3,11},{11,3},{4,12},{12,4},... | collective-permute-start | bytes 1179656 | tf_op jit(solution)/shard_map/ppermute | solution.py:455
  99.8 0.1 fusion.9
  99.9 1.9 %collective-permute-start.20 = (bf16[6,128,128]{2,1,0:T(8,128)(2,1)S(1)}, bf16[6,128,128]{2,1,0:T(8,128)(2,1)S(1)}, u32[]{:S(2)}, u32[]{:S(2)}) collective-permute-start(bf16[6,128,128]{2,1,0:T(8,128)(2,1)S(1)} %fusion.9), channel_id=1, source_target_pairs={{64,0},{72,8},{80,16},{88,24},{96,32},{104,40},{112,48},{120,56},{... | collective-permute-start | bytes 589832 | tf_op jit(solution)/shard_map/ppermute | solution.py:461
  101.8 2.7 %collective-permute-start.19 = (bf16[6,128,128]{2,1,0:T(8,128)(2,1)S(1)}, bf16[6,128,128]{2,1,0:T(8,128)(2,1)S(1)}, u32[]{:S(2)}, u32[]{:S(2)}) collective-permute-start(bf16[6,128,128]{2,1,0:T(8,128)(2,1)S(1)} %fusion.9), channel_id=1, source_target_pairs={{48,0},{56,8},{64,16},{72,24},{80,32},{88,40},{96,48},{104,56},{11... | collective-permute-start | bytes 589832 | tf_op jit(solution)/shard_map/ppermute | solution.py:461
  104.5 1.9 %collective-permute-start.18 = (bf16[6,128,128]{2,1,0:T(8,128)(2,1)S(1)}, bf16[6,128,128]{2,1,0:T(8,128)(2,1)S(1)}, u32[]{:S(2)}, u32[]{:S(2)}) collective-permute-start(bf16[6,128,128]{2,1,0:T(8,128)(2,1)S(1)} %fusion.9), channel_id=1, source_target_pairs={{32,0},{40,8},{48,16},{56,24},{64,32},{72,40},{80,48},{88,56},{96,... | collective-permute-start | bytes 589832 | tf_op jit(solution)/shard_map/ppermute | solution.py:461
  106.4 2.5 %collective-permute-start.17 = (bf16[6,128,128]{2,1,0:T(8,128)(2,1)S(1)}, bf16[6,128,128]{2,1,0:T(8,128)(2,1)S(1)}, u32[]{:S(2)}, u32[]{:S(2)}) collective-permute-start(bf16[6,128,128]{2,1,0:T(8,128)(2,1)S(1)} %fusion.9), channel_id=1, source_target_pairs={{16,0},{24,8},{32,16},{40,24},{48,32},{56,40},{64,48},{72,56},{80,... | collective-permute-start | bytes 589832 | tf_op jit(solution)/shard_map/ppermute | solution.py:461
  108.9 1.2 output_part.1
  110.2 2.5 %collective-permute-start.15 = (bf16[128,1024]{1,0:T(8,128)(2,1)S(1)}, bf16[128,1024]{1,0:T(8,128)(2,1)S(1)}, u32[]{:S(2)}, u32[]{:S(2)}) collective-permute-start(bf16[128,1024]{1,0:T(8,128)(2,1)S(1)} %get-tuple-element.47), channel_id=1, source_target_pairs={{0,8},{8,0},{1,9},{9,1},{2,10},{10,2},{3,11},{11,3},{4,12},{12,4},... | collective-permute-start | bytes 786440 | tf_op jit(solution)/shard_map/ppermute | solution.py:455
  112.7 0.5 collective-permute-done.19
  113.1 5.1 %collective-permute-done.18 = bf16[6,128,128]{2,1,0:T(8,128)(2,1)S(1)} collective-permute-done((bf16[6,128,128]{2,1,0:T(8,128)(2,1)S(1)}, bf16[6,128,128]{2,1,0:T(8,128)(2,1)S(1)}, u32[]{:S(2)}, u32[]{:S(2)}) %collective-permute-start.18) | collective-permute-done | bytes 196640 | tf_op jit(solution)/shard_map/ppermute | solution.py:461
  118.2 6.4 %collective-permute-done.17 = bf16[6,128,128]{2,1,0:T(8,128)(2,1)S(1)} collective-permute-done((bf16[6,128,128]{2,1,0:T(8,128)(2,1)S(1)}, bf16[6,128,128]{2,1,0:T(8,128)(2,1)S(1)}, u32[]{:S(2)}, u32[]{:S(2)}) %collective-permute-start.17) | collective-permute-done | bytes 196640 | tf_op jit(solution)/shard_map/ppermute | solution.py:461
  124.6 0.3 fusion.11
  124.9 2.5 %collective-permute-start.21 = (bf16[6,128,128]{2,1,0:T(8,128)(2,1)S(1)}, bf16[6,128,128]{2,1,0:T(8,128)(2,1)S(1)}, u32[]{:S(2)}, u32[]{:S(2)}) collective-permute-start(bf16[6,128,128]{2,1,0:T(8,128)(2,1)S(1)} %get-tuple-element.54), channel_id=1, source_target_pairs={{0,8},{8,0},{1,9},{9,1},{2,10},{10,2},{3,11},{11,3},{4,12},{12,4},... | collective-permute-start | bytes 589832 | tf_op jit(solution)/shard_map/ppermute | solution.py:455
  127.4 4.0 %grads_part.1 = (bf16[128,1536]{1,0:T(8,128)(2,1)}, f32[128,1536]{1,0:T(8,128)S(1)}, f32[128,1536]{1,0:T(8,128)S(1)}) custom-call(s32[1,16]{1,0:T(1,128)S(1)} %copy-done.5, bf16[128,1536]{1,0:T(8,128)(2,1)S(1)} %bitcast.49, bf16[128,1536]{1,0:T(8,128)(2,1)S(1)} %bitcast.52, bf16[128,1536]{1,0:T(8,128)(2,1)S(1)} %bitcast.56, ...), custom_call_target="tpu_custom_call" | custom-call | flops 250000000 | bytes 5000000 | tf_op jit(solution)/shard_map/grads_part/pallas_call | solution.py:408
  131.4 2.1 %last_part.1 = (bf16[128,1536]{1,0:T(8,128)(2,1)}, bf16[128,1536]{1,0:T(8,128)(2,1)}, bf16[128,2048]{1,0:T(8,128)(2,1)}) custom-call(s32[1,16]{1,0:T(1,128)S(1)} %copy-done.5, bf16[128,1536]{1,0:T(8,128)(2,1)S(1)} %bitcast.53, bf16[128,1536]{1,0:T(8,128)(2,1)S(1)} %bitcast.57, f32[128,1536]{1,0:T(8,128)S(1)} %get-tuple-element.43.dk_part_ref, ...), custom_call_target="tpu_custom_call" | custom-call | flops 100000000 | bytes 4500000 | tf_op jit(solution)/shard_map/last_part/pallas_call | solution.py:443
  (29 shorter events, 0.1 us)
Async XLA Ops:
  0.6 43.2 %copy-start.1 = (bf16[1,128,1536]{2,1,0:T(8,128)(2,1)S(1)}, bf16[1,128,1536]{2,1,0:T(8,128)(2,1)}, u32[]{:S(2)}) copy-start(bf16[1,128,1536]{2,1,0:T(8,128)(2,1)} %param.8) | copy-start | bytes 1179652
  0.6 43.2 %copy-start.2 = (bf16[1,128,1536]{2,1,0:T(8,128)(2,1)S(1)}, bf16[1,128,1536]{2,1,0:T(8,128)(2,1)}, u32[]{:S(2)}) copy-start(bf16[1,128,1536]{2,1,0:T(8,128)(2,1)} %param.9) | copy-start | bytes 1179652
  2.8 9.9 %collective-permute-start.1 = (bf16[192,1024]{1,0:T(8,128)(2,1)}, bf16[192,1024]{1,0:T(8,128)(2,1)S(1)}, u32[]{:S(2)}, u32[]{:S(2)}) collective-permute-start(bf16[192,1024]{1,0:T(8,128)(2,1)} %get-tuple-element.31.refs_0_), channel_id=1, source_target_pairs={{0,1},{1,2},{2,3},{3,4},{4,5},{5,6},{6,7},{7,0},{8,15},{9,8},{10,9... | collective-permute-start | bytes 1179656 | tf_op jit(solution)/shard_map/ppermute | solution.py:466
  12.8 9.7 %collective-permute-start.2 = (bf16[192,1024]{1,0:T(8,128)(2,1)S(1)}, bf16[192,1024]{1,0:T(8,128)(2,1)S(1)}, u32[]{:S(2)}, u32[]{:S(2)}) collective-permute-start(bf16[192,1024]{1,0:T(8,128)(2,1)S(1)} %collective-permute-done.1.refs_1_), channel_id=1, source_target_pairs={{0,1},{1,2},{2,3},{3,4},{4,5},{5,6},{6,7},{7,0},{8,15},{9,8},{10,9... | collective-permute-start | bytes 1179656 | tf_op jit(solution)/shard_map/ppermute | solution.py:466
  22.5 9.7 %collective-permute-start.3 = (bf16[192,1024]{1,0:T(8,128)(2,1)S(1)}, bf16[192,1024]{1,0:T(8,128)(2,1)S(1)}, u32[]{:S(2)}, u32[]{:S(2)}) collective-permute-start(bf16[192,1024]{1,0:T(8,128)(2,1)S(1)} %collective-permute-done.2.refs_2_), channel_id=1, source_target_pairs={{0,1},{1,2},{2,3},{3,4},{4,5},{5,6},{6,7},{7,0},{8,15},{9,8},{10,9... | collective-permute-start | bytes 1179656 | tf_op jit(solution)/shard_map/ppermute | solution.py:466
  32.2 9.7 %collective-permute-start.4 = (bf16[192,1024]{1,0:T(8,128)(2,1)S(1)}, bf16[192,1024]{1,0:T(8,128)(2,1)S(1)}, u32[]{:S(2)}, u32[]{:S(2)}) collective-permute-start(bf16[192,1024]{1,0:T(8,128)(2,1)S(1)} %collective-permute-done.3.refs_3_), channel_id=1, source_target_pairs={{0,1},{1,2},{2,3},{3,4},{4,5},{5,6},{6,7},{7,0},{8,15},{9,8},{10,9... | collective-permute-start | bytes 1179656 | tf_op jit(solution)/shard_map/ppermute | solution.py:466
  41.9 13.9 %collective-permute-start.5 = (bf16[192,1024]{1,0:T(8,128)(2,1)S(1)}, bf16[192,1024]{1,0:T(8,128)(2,1)S(1)}, u32[]{:S(2)}, u32[]{:S(2)}) collective-permute-start(bf16[192,1024]{1,0:T(8,128)(2,1)S(1)} %collective-permute-done.4.refs_4_), channel_id=1, source_target_pairs={{0,1},{1,2},{2,3},{3,4},{4,5},{5,6},{6,7},{7,0},{8,15},{9,8},{10,9... | collective-permute-start | bytes 1179656 | tf_op jit(solution)/shard_map/ppermute | solution.py:466
  43.8 0.7 copy-start.5
  45.9 11.9 %collective-permute-start.9 = (bf16[6,128,128]{2,1,0:T(8,128)(2,1)S(1)}, bf16[6,128,128]{2,1,0:T(8,128)(2,1)S(1)}, u32[]{:S(2)}, u32[]{:S(2)}) collective-permute-start(bf16[6,128,128]{2,1,0:T(8,128)(2,1)S(1)} %get-tuple-element.38), channel_id=1, source_target_pairs={{0,8},{8,0},{1,9},{9,1},{2,10},{10,2},{3,11},{11,3},{4,12},{12,4},... | collective-permute-start | bytes 589832 | tf_op jit(solution)/shard_map/ppermute | solution.py:455
  55.9 14.5 %collective-permute-start.6 = (bf16[192,1024]{1,0:T(8,128)(2,1)S(1)}, bf16[192,1024]{1,0:T(8,128)(2,1)S(1)}, u32[]{:S(2)}, u32[]{:S(2)}) collective-permute-start(bf16[192,1024]{1,0:T(8,128)(2,1)S(1)} %collective-permute-done.5.refs_5_), channel_id=1, source_target_pairs={{0,1},{1,2},{2,3},{3,4},{4,5},{5,6},{6,7},{7,0},{8,15},{9,8},{10,9... | collective-permute-start | bytes 1179656 | tf_op jit(solution)/shard_map/ppermute | solution.py:466
  57.8 5.4 %copy-start.7 = (bf16[128,1024]{1,0:T(8,128)(2,1)S(1)}, bf16[128,1024]{1,0:T(8,128)(2,1)}, u32[]{:S(2)}) copy-start(bf16[128,1024]{1,0:T(8,128)(2,1)} %get-tuple-element.30) | copy-start | bytes 786436
  57.8 22.0 %copy-start.4 = (bf16[128,1024]{1,0:T(8,128)(2,1)S(1)}, bf16[128,1024]{1,0:T(8,128)(2,1)}, u32[]{:S(2)}) copy-start(bf16[128,1024]{1,0:T(8,128)(2,1)} %get-tuple-element.29.cot_keep_ref) | copy-start | bytes 786436
  57.9 21.9 %copy-start.3 = (bf16[192,1024]{1,0:T(8,128)(2,1)S(1)}, bf16[192,1024]{1,0:T(8,128)(2,1)}, u32[]{:S(2)}) copy-start(bf16[192,1024]{1,0:T(8,128)(2,1)} %get-tuple-element.31.refs_0_) | copy-start | bytes 1179652
  57.9 14.4 %collective-permute-start.10 = (bf16[6,128,128]{2,1,0:T(8,128)(2,1)S(1)}, bf16[6,128,128]{2,1,0:T(8,128)(2,1)S(1)}, u32[]{:S(2)}, u32[]{:S(2)}) collective-permute-start(bf16[6,128,128]{2,1,0:T(8,128)(2,1)S(1)} %fusion.3), channel_id=1, source_target_pairs={{0,16},{8,24},{16,32},{24,40},{32,48},{40,56},{48,64},{56,72},{64,... | collective-permute-start | bytes 589832 | tf_op jit(solution)/shard_map/ppermute | solution.py:461
  63.2 16.6 %collective-permute-start = (bf16[128,1024]{1,0:T(8,128)(2,1)S(1)}, bf16[128,1024]{1,0:T(8,128)(2,1)S(1)}, u32[]{:S(2)}, u32[]{:S(2)}) collective-permute-start(bf16[128,1024]{1,0:T(8,128)(2,1)S(1)} %copy-done.7), channel_id=1, source_target_pairs={{0,8},{8,0},{1,9},{9,1},{2,10},{10,2},{3,11},{11,3},{4,12},{12,4},... | collective-permute-start | bytes 786440 | tf_op jit(solution)/shard_map/ppermute | solution.py:455
  70.4 10.8 %collective-permute-start.7 = (bf16[192,1024]{1,0:T(8,128)(2,1)S(1)}, bf16[192,1024]{1,0:T(8,128)(2,1)S(1)}, u32[]{:S(2)}, u32[]{:S(2)}) collective-permute-start(bf16[192,1024]{1,0:T(8,128)(2,1)S(1)} %collective-permute-done.6.refs_6_), channel_id=1, source_target_pairs={{0,1},{1,2},{2,3},{3,4},{4,5},{5,6},{6,7},{7,0},{8,15},{9,8},{10,9... | collective-permute-start | bytes 1179656 | tf_op jit(solution)/shard_map/ppermute | solution.py:466
  72.4 15.1 %collective-permute-start.12 = (bf16[6,128,128]{2,1,0:T(8,128)(2,1)S(1)}, bf16[6,128,128]{2,1,0:T(8,128)(2,1)S(1)}, u32[]{:S(2)}, u32[]{:S(2)}) collective-permute-start(bf16[6,128,128]{2,1,0:T(8,128)(2,1)S(1)} %add_convert_fusion), channel_id=1, source_target_pairs={{0,48},{8,56},{16,64},{24,72},{32,80},{40,88},{48,96},{56,104},{64... | collective-permute-start | bytes 589832 | tf_op jit(solution)/shard_map/ppermute | solution.py:461
  75.6 11.9 %collective-permute-start.11 = (bf16[6,128,128]{2,1,0:T(8,128)(2,1)S(1)}, bf16[6,128,128]{2,1,0:T(8,128)(2,1)S(1)}, u32[]{:S(2)}, u32[]{:S(2)}) collective-permute-start(bf16[6,128,128]{2,1,0:T(8,128)(2,1)S(1)} %add_convert_fusion), channel_id=1, source_target_pairs={{0,16},{8,24},{16,32},{24,40},{32,48},{40,56},{48,64},{56,72},{64,... | collective-permute-start | bytes 589832 | tf_op jit(solution)/shard_map/ppermute | solution.py:461
  81.6 11.6 %collective-permute-start.8 = (bf16[1536,128]{1,0:T(8,128)(2,1)S(1)}, bf16[1536,128]{1,0:T(8,128)(2,1)S(1)}, u32[]{:S(2)}, u32[]{:S(2)}) collective-permute-start(bf16[1536,128]{1,0:T(8,128)(2,1)S(1)} %get-tuple-element.35), channel_id=1, source_target_pairs={{0,8},{8,0},{1,9},{9,1},{2,10},{10,2},{3,11},{11,3},{4,12},{12,4},... | collective-permute-start | bytes 1179656 | tf_op jit(solution)/shard_map/ppermute | solution.py:455
  87.5 2.2 %copy-start.6 = (f32[1536]{0:T(1024)S(1)}, f32[1536]{0:T(1024)}, u32[]{:S(2)}) copy-start(f32[1536]{0:T(1024)} %param.11) | copy-start | bytes 18436
  87.5 2.2 %copy-start = (bf16[1,128,1536]{2,1,0:T(8,128)(2,1)S(1)}, bf16[1,128,1536]{2,1,0:T(8,128)(2,1)}, u32[]{:S(2)}) copy-start(bf16[1,128,1536]{2,1,0:T(8,128)(2,1)} %param.7) | copy-start | bytes 1179652
  87.7 4.5 %collective-permute-start.13 = (bf16[6,128,128]{2,1,0:T(8,128)(2,1)S(1)}, bf16[6,128,128]{2,1,0:T(8,128)(2,1)S(1)}, u32[]{:S(2)}, u32[]{:S(2)}) collective-permute-start(bf16[6,128,128]{2,1,0:T(8,128)(2,1)S(1)} %get-tuple-element.56), channel_id=1, source_target_pairs={{0,8},{8,0},{1,9},{9,1},{2,10},{10,2},{3,11},{11,3},{4,12},{12,4},... | collective-permute-start | bytes 589832 | tf_op jit(solution)/shard_map/ppermute | solution.py:455
  95.4 4.3 %collective-permute-start.16 = (bf16[6,128,128]{2,1,0:T(8,128)(2,1)S(1)}, bf16[6,128,128]{2,1,0:T(8,128)(2,1)S(1)}, u32[]{:S(2)}, u32[]{:S(2)}) collective-permute-start(bf16[6,128,128]{2,1,0:T(8,128)(2,1)S(1)} %get-tuple-element.48), channel_id=1, source_target_pairs={{0,8},{8,0},{1,9},{9,1},{2,10},{10,2},{3,11},{11,3},{4,12},{12,4},... | collective-permute-start | bytes 589832 | tf_op jit(solution)/shard_map/ppermute | solution.py:455
  97.8 11.1 %collective-permute-start.14 = (bf16[128,1536]{1,0:T(8,128)(2,1)S(1)}, bf16[128,1536]{1,0:T(8,128)(2,1)S(1)}, u32[]{:S(2)}, u32[]{:S(2)}) collective-permute-start(bf16[128,1536]{1,0:T(8,128)(2,1)S(1)} %get-tuple-element.45.scaled_ref), channel_id=1, source_target_pairs={{0,8},{8,0},{1,9},{9,1},{2,10},{10,2},{3,11},{11,3},{4,12},{12,4},... | collective-permute-start | bytes 1179656 | tf_op jit(solution)/shard_map/ppermute | solution.py:455
  99.9 12.8 %collective-permute-start.20 = (bf16[6,128,128]{2,1,0:T(8,128)(2,1)S(1)}, bf16[6,128,128]{2,1,0:T(8,128)(2,1)S(1)}, u32[]{:S(2)}, u32[]{:S(2)}) collective-permute-start(bf16[6,128,128]{2,1,0:T(8,128)(2,1)S(1)} %fusion.9), channel_id=1, source_target_pairs={{64,0},{72,8},{80,16},{88,24},{96,32},{104,40},{112,48},{120,56},{... | collective-permute-start | bytes 589832 | tf_op jit(solution)/shard_map/ppermute | solution.py:461
  101.8 11.3 %collective-permute-start.19 = (bf16[6,128,128]{2,1,0:T(8,128)(2,1)S(1)}, bf16[6,128,128]{2,1,0:T(8,128)(2,1)S(1)}, u32[]{:S(2)}, u32[]{:S(2)}) collective-permute-start(bf16[6,128,128]{2,1,0:T(8,128)(2,1)S(1)} %fusion.9), channel_id=1, source_target_pairs={{48,0},{56,8},{64,16},{72,24},{80,32},{88,40},{96,48},{104,56},{11... | collective-permute-start | bytes 589832 | tf_op jit(solution)/shard_map/ppermute | solution.py:461
  104.5 13.7 %collective-permute-start.18 = (bf16[6,128,128]{2,1,0:T(8,128)(2,1)S(1)}, bf16[6,128,128]{2,1,0:T(8,128)(2,1)S(1)}, u32[]{:S(2)}, u32[]{:S(2)}) collective-permute-start(bf16[6,128,128]{2,1,0:T(8,128)(2,1)S(1)} %fusion.9), channel_id=1, source_target_pairs={{32,0},{40,8},{48,16},{56,24},{64,32},{72,40},{80,48},{88,56},{96,... | collective-permute-start | bytes 589832 | tf_op jit(solution)/shard_map/ppermute | solution.py:461
  106.4 18.2 %collective-permute-start.17 = (bf16[6,128,128]{2,1,0:T(8,128)(2,1)S(1)}, bf16[6,128,128]{2,1,0:T(8,128)(2,1)S(1)}, u32[]{:S(2)}, u32[]{:S(2)}) collective-permute-start(bf16[6,128,128]{2,1,0:T(8,128)(2,1)S(1)} %fusion.9), channel_id=1, source_target_pairs={{16,0},{24,8},{32,16},{40,24},{48,32},{56,40},{64,48},{72,56},{80,... | collective-permute-start | bytes 589832 | tf_op jit(solution)/shard_map/ppermute | solution.py:461
  110.2 21.2 %collective-permute-start.15 = (bf16[128,1024]{1,0:T(8,128)(2,1)S(1)}, bf16[128,1024]{1,0:T(8,128)(2,1)S(1)}, u32[]{:S(2)}, u32[]{:S(2)}) collective-permute-start(bf16[128,1024]{1,0:T(8,128)(2,1)S(1)} %get-tuple-element.47), channel_id=1, source_target_pairs={{0,8},{8,0},{1,9},{9,1},{2,10},{10,2},{3,11},{11,3},{4,12},{12,4},... | collective-permute-start | bytes 786440 | tf_op jit(solution)/shard_map/ppermute | solution.py:455
  124.9 6.5 %collective-permute-start.21 = (bf16[6,128,128]{2,1,0:T(8,128)(2,1)S(1)}, bf16[6,128,128]{2,1,0:T(8,128)(2,1)S(1)}, u32[]{:S(2)}, u32[]{:S(2)}) collective-permute-start(bf16[6,128,128]{2,1,0:T(8,128)(2,1)S(1)} %get-tuple-element.54), channel_id=1, source_target_pairs={{0,8},{8,0},{1,9},{9,1},{2,10},{10,2},{3,11},{11,3},{4,12},{12,4},... | collective-permute-start | bytes 589832 | tf_op jit(solution)/shard_map/ppermute | solution.py:455

commit v4 on v3

--- a/solution.py
+++ b/solution.py
@@ -258,56 +258,59 @@
     )(lengths, queries, inside, mine, other, gain)
 
 
-def shard_rows(step):
-    way = 2 * lax.axis_index("core") - 1
-    owner = lax.rem(lax.axis_index("fsdp") + Y + way * step, Y)
+HELD = ((0, 1), (-1, -2), (2, 3), (-3, -4))
+
+
+def shard_rows(offset):
+    y = lax.axis_index("fsdp")
+    way = 1 - 2 * lax.rem(y + lax.axis_index("core"), 2)
+    owner = lax.rem(y + Y + way * offset, Y)
     return pl.ds(pl.multiple_of(owner * SHARD, 64), SHARD)
 
 
-EARLY = range(Y - 1)
+def add_share(held, block_ref, cot_ref, own_ref, give_ref):
+    for number, offset in enumerate(held):
+        share = dot(block_ref[number * SHARD : (number + 1) * SHARD], cot_ref[...], NT)
+        rows = shard_rows(offset)
+        own_ref[rows, :] = share[:, :TOK]
+        give_ref[rows, :] = share[:, TOK:].astype(BF16)
 
 
 def share_kernel(cot_keep_ref, cot_got_ref, *refs):
-    pieces, (own_ref, give_ref, cot_ref) = refs[: len(EARLY)], refs[len(EARLY) :]
+    blocks, (own_ref, give_ref, cot_ref) = refs[:3], refs[3:]
     cot_ref[:TOK] = cot_keep_ref[...]
     cot_ref[TOK:] = cot_got_ref[...]
-    for step, piece in zip(EARLY, pieces):
-        share = dot(piece[...], cot_ref[...], NT)
-        rows = shard_rows(step)
-        own_ref[rows, :] = share[:, :TOK]
-        give_ref[rows, :] = share[:, TOK:].astype(BF16)
+    for held, block_ref in zip(HELD, blocks):
+        add_share(held, block_ref, cot_ref, own_ref, give_ref)
 
 
 SHARE_SHAPES = (jax.ShapeDtypeStruct((DI, TOK), F32), jax.ShapeDtypeStruct((DI, TOK), BF16))
 
 
-def share_part(cot_keep, cot_got, pieces):
+def share_part(cot_keep, cot_got, blocks):
     return pl.pallas_call(
         share_kernel,
         out_shape=SHARE_SHAPES,
-        in_specs=[VMEM] * (2 + len(EARLY)),
+        in_specs=[VMEM] * 5,
         out_specs=(VMEM, VMEM),
         scratch_shapes=[pltpu.VMEM((2 * TOK, D // 2), BF16)],
         compiler_params=params(),
         cost_estimate=cost(700_000_000, 4_500_000),
         name="share_part",
-    )(cot_keep, cot_got, *pieces)
+    )(cot_keep, cot_got, *blocks)
 
 
 def share_end_kernel(
-    cot_keep_ref, cot_got_ref, piece_ref, own_in_ref, give_in_ref, own_ref, give_ref, cot_ref
+    cot_keep_ref, cot_got_ref, block_ref, own_in_ref, give_in_ref, own_ref, give_ref, cot_ref
 ):
     cot_ref[:TOK] = cot_keep_ref[...]
     cot_ref[TOK:] = cot_got_ref[...]
     own_ref[...] = own_in_ref[...]
     give_ref[...] = give_in_ref[...]
-    share = dot(piece_ref[...], cot_ref[...], NT)
-    rows = shard_rows(Y - 1)
-    own_ref[rows, :] = share[:, :TOK]
-    give_ref[rows, :] = share[:, TOK:].astype(BF16)
-
-
-def share_end(cot_keep, cot_got, piece, own, give):
+    add_share(HELD[3], block_ref, cot_ref, own_ref, give_ref)
+
+
+def share_end(cot_keep, cot_got, block, own, give):
     return pl.pallas_call(
         share_end_kernel,
         out_shape=SHARE_SHAPES,
@@ -317,7 +320,7 @@
         compiler_params=params(),
         cost_estimate=cost(100_000_000, 3_500_000),
         name="share_end",
-    )(cot_keep, cot_got, piece, own, give)
+    )(cot_keep, cot_got, block, own, give)
 
 
 def grad_mixed_kernel(
@@ -356,9 +359,10 @@
 
 
 def output_kernel(scaled_ref, scaled_got_ref, *refs):
-    pieces, (own_ref, give_ref, both_ref, weight_ref) = refs[:Y], refs[Y:]
-    for step, piece in enumerate(pieces):
-        weight_ref[shard_rows(step), :] = piece[...]
+    blocks, (own_ref, give_ref, both_ref, weight_ref) = refs[:4], refs[4:]
+    for held, block_ref in zip(HELD, blocks):
+        for number, offset in enumerate(held):
+            weight_ref[shard_rows(offset), :] = block_ref[number * SHARD : (number + 1) * SHARD]
     both_ref[:TOK] = scaled_ref[...]
     both_ref[TOK:] = scaled_got_ref[...]
     for start in range(0, D // 2, 256):
@@ -367,18 +371,18 @@
         give_ref[:, start : start + 256] = block[TOK:]
 
 
-def output_part(scaled, scaled_got, pieces):
+def output_part(scaled, scaled_got, blocks):
     half = jax.ShapeDtypeStruct((TOK, D // 2), BF16)
     return pl.pallas_call(
         output_kernel,
         out_shape=(half, half),
-        in_specs=[VMEM] * (2 + Y),
+        in_specs=[VMEM] * 6,
         out_specs=(VMEM, VMEM),
         scratch_shapes=[pltpu.VMEM((2 * TOK, DI), BF16), pltpu.VMEM((DI, D // 2), BF16)],
         compiler_params=params(),
         cost_estimate=cost(810_000_000, 5_000_000),
         name="output_part",
-    )(scaled, scaled_got, *pieces)
+    )(scaled, scaled_got, *blocks)
 
 
 def grads_kernel(
@@ -461,8 +465,12 @@
     return lax.ppermute(block, ("z", "x", "core"), pairs)
 
 
-def along_y(block):
-    pairs = [(i, (i + 1) % Y) for i in range(Y)] + [(Y + i, Y + (i - 1) % Y) for i in range(Y)]
+def exchange(block, sense):
+    pairs = []
+    for core in range(2):
+        for y in range(Y):
+            way = 1 - 2 * ((y + core) % 2)
+            pairs.append((core * Y + y, core * Y + (y + sense * way) % Y))
     return lax.ppermute(block, ("core", "fsdp"), pairs)
 
 
@@ -493,9 +501,10 @@
     queries, keys, values, cotangent = queries[0], keys[0], values[0], cotangent[0]
     gain_row = gain.reshape(1, DI)
     half, cot_keep, cot_give = take_half(out_weight, cotangent)
-    pieces = [half]
-    for _ in range(1, Y):
-        pieces.append(along_y(pieces[-1]))
+    got_half = exchange(half, 1)
+    blocks = [jnp.concatenate([half, got_half], axis=0)]
+    for sense in (-1, 1, -1):
+        blocks.append(exchange(blocks[-1], sense))
     cot_got = swap_cores(cot_give)
 
     keep, give, coef = local_state(lengths, keys, values)
@@ -503,12 +512,12 @@
     attn, inside = inside_part(lengths, queries, keys, values)
     mixed, scaled = mixed_part(lengths, queries, inside, mine, other, gain_row)
     scaled_got = swap_cores(scaled)
-    own_share, give_share = share_part(cot_keep, cot_got, pieces[:-1])
-    own_share, give_share = share_end(cot_keep, cot_got, pieces[-1], own_share, give_share)
+    own_share, give_share = share_part(cot_keep, cot_got, blocks[:3])
+    own_share, give_share = share_end(cot_keep, cot_got, blocks[3], own_share, give_share)
     got_share = swap_cores(give_share)
     low, give_back, keep_back = grad_mixed_part(lengths, own_share, got_share, mixed, gain_row, queries)
     back_mine, back_other = window(keep_back, give_back, coef, -1)
-    out_own, out_give = output_part(scaled, scaled_got, pieces)
+    out_own, out_give = output_part(scaled, scaled_got, blocks)
     out_got = swap_cores(out_give)
     dq, dk_part, dv_part = grads_part(lengths, queries, keys, values, low, attn, mine, other)
     dk, dv, output = last_part(lengths, keys, values, dk_part, dv_part, out_own, out_got, back_mine, back_other)

time: 134 us -> 117 us (0.87)
  the two profiles are of different devices: /device:TPU:223 before, /device:TPU:199 now
where the time goes in v4:
time: 117 us; the launch traced here: 116 us
  starting transfers between devices  62.8 us (54%)
  waiting for transfers between devices  31.8 us (27%)
  Pallas kernels  18.1 us (15%)
  local copies, waits for them, and re-layouts  1.75 us (1%)
    ppermute x8, starting transfers between devices, swap_cores(): return lax.ppermute(block, 'core', [(0, 1), (1, 0)])  26 us
    ppermute x7, starting transfers between devices, from_chip(): return lax.ppermute(block, ('z', 'x', 'core'), pairs)  23.3 us
    ppermute x4, waiting for transfers between devices, exchange(): return lax.ppermute(block, ('core', 'fsdp'), pairs)  20.8 us
    ppermute x4, starting transfers between devices, exchange(): return lax.ppermute(block, ('core', 'fsdp'), pairs)  13.5 us
    ppermute x7, waiting for transfers between devices, from_chip(): return lax.ppermute(block, ('z', 'x', 'core'), pairs)  11 us
    pallas_call x1, Pallas kernels, grads_part(): pl.pallas_call(grads_kernel, out_shape=(jax.ShapeDtypeStruct((TOK, DI), B...  3.95 us
    pallas_call x1, Pallas kernels, inside_part(): pl.pallas_call(inside_kernel, out_shape=(jax.ShapeDtypeStruct((HEADS, TOK...  2.5 us
  transfers between devices with their start and end apart: 19, of which 6 were waited for; matrix products, arithmetic and copies ran while one was open for 2% of the time, Pallas kernels for 10%

profile of v4, /device:TPU:199, one launch (start us, length us, event | category | flops | bytes accessed | tf_op | source)
XLA Modules:
  0.0 116.2 jit_solution(1784461051587828409)
XLA Ops:
  0.6 2.1 %take_half.1 = (bf16[192,1024]{1,0:T(8,128)(2,1)}, bf16[128,1024]{1,0:T(8,128)(2,1)}, bf16[128,1024]{1,0:T(8,128)(2,1)}) custom-call(bf16[192,2048]{1,0:T(8,128)(2,1)} %weight_ref.1, bf16[128,2048]{1,0:T(8,128)(2,1)} %bitcast.58), custom_call_target="tpu_custom_call" | custom-call | flops 1000 | bytes 2000000 | tf_op jit(solution)/shard_map/take_half/pallas_call | solution.py:116
  2.7 5.1 %collective-permute-start.1 = (bf16[192,1024]{1,0:T(8,128)(2,1)}, bf16[192,1024]{1,0:T(8,128)(2,1)S(1)}, u32[]{:S(2)}, u32[]{:S(2)}) collective-permute-start(bf16[192,1024]{1,0:T(8,128)(2,1)} %get-tuple-element.31), channel_id=1, source_target_pairs={{0,1},{1,0},{2,3},{3,2},{4,5},{5,4},{6,7},{7,6},{8,15},{9,10},{10,... | collective-permute-start | bytes 1179656 | tf_op jit(solution)/shard_map/ppermute | solution.py:474
  7.8 1.0 constant_dynamic-update-slice_fusion.1
  8.9 0.0 copy-start.1
  8.9 0.0 copy-start.2
  8.9 4.3 %collective-permute-done.1 = bf16[192,1024]{1,0:T(8,128)(2,1)S(1)} collective-permute-done((bf16[192,1024]{1,0:T(8,128)(2,1)}, bf16[192,1024]{1,0:T(8,128)(2,1)S(1)}, u32[]{:S(2)}, u32[]{:S(2)}) %collective-permute-start.1) | collective-permute-done | bytes 393248 | tf_op jit(solution)/shard_map/ppermute | solution.py:474
  13.2 1.9 %collective-permute-start.2 = (bf16[384,1024]{1,0:T(8,128)(2,1)S(1)}, bf16[384,1024]{1,0:T(8,128)(2,1)S(1)}, u32[]{:S(2)}, u32[]{:S(2)}) collective-permute-start(bf16[384,1024]{1,0:T(8,128)(2,1)S(1)} %constant_dynamic-update-slice_fusion.refs_0_), channel_id=1, source_target_pairs={{0,7},{1,2},{2,1},{3,4},{4,3},{5,6},{6,5},{7,0},{8,9},{9,8},{10,11... | collective-permute-start | bytes 2359304 | tf_op jit(solution)/shard_map/ppermute | solution.py:474
  15.2 11.1 %collective-permute-done.2.refs_1_ = bf16[384,1024]{1,0:T(8,128)(2,1)S(1)} collective-permute-done((bf16[384,1024]{1,0:T(8,128)(2,1)S(1)}, bf16[384,1024]{1,0:T(8,128)(2,1)S(1)}, u32[]{:S(2)}, u32[]{:S(2)}) %collective-permute-start.2) | collective-permute-done | bytes 786464 | tf_op jit(solution)/shard_map/ppermute | solution.py:474
  26.3 4.6 %collective-permute-start.3 = (bf16[384,1024]{1,0:T(8,128)(2,1)S(1)}, bf16[384,1024]{1,0:T(8,128)(2,1)S(1)}, u32[]{:S(2)}, u32[]{:S(2)}) collective-permute-start(bf16[384,1024]{1,0:T(8,128)(2,1)S(1)} %collective-permute-done.2.refs_1_), channel_id=1, source_target_pairs={{0,1},{1,0},{2,3},{3,2},{4,5},{5,4},{6,7},{7,6},{8,15},{9,10},{10,... | collective-permute-start | bytes 2359304 | tf_op jit(solution)/shard_map/ppermute | solution.py:474
  30.8 0.0 copy-start.4
  30.9 0.6 copy-done.4
  31.5 1.4 %local_state.1 = (bf16[6,128,128]{2,1,0:T(8,128)(2,1)S(1)}, bf16[6,128,128]{2,1,0:T(8,128)(2,1)S(1)}, f32[24,128]{1,0:T(8,128)S(1)}) custom-call(s32[1,16]{1,0:T(1,128)S(1)} %copy-done.4, bf16[128,1536]{1,0:T(8,128)(2,1)S(1)} %bitcast.50, bf16[128,1536]{1,0:T(8,128)(2,1)S(1)} %bitcast.54), custom_call_target="tpu_custom_call" | custom-call | flops 50000000 | bytes 1200000 | tf_op jit(solution)/shard_map/local_state/pallas_call | solution.py:189
  32.9 1.9 %collective-permute-start.6 = (bf16[6,128,128]{2,1,0:T(8,128)(2,1)S(1)}, bf16[6,128,128]{2,1,0:T(8,128)(2,1)S(1)}, u32[]{:S(2)}, u32[]{:S(2)}) collective-permute-start(bf16[6,128,128]{2,1,0:T(8,128)(2,1)S(1)} %get-tuple-element.38), channel_id=1, source_target_pairs={{0,8},{8,0},{1,9},{9,1},{2,10},{10,2},{3,11},{11,3},{4,12},{12,4},... | collective-permute-start | bytes 589832 | tf_op jit(solution)/shard_map/ppermute | solution.py:459
  34.8 5.4 %collective-permute-done.3.refs_2_ = bf16[384,1024]{1,0:T(8,128)(2,1)S(1)} collective-permute-done((bf16[384,1024]{1,0:T(8,128)(2,1)S(1)}, bf16[384,1024]{1,0:T(8,128)(2,1)S(1)}, u32[]{:S(2)}, u32[]{:S(2)}) %collective-permute-start.3) | collective-permute-done | bytes 786464 | tf_op jit(solution)/shard_map/ppermute | solution.py:474
  40.2 1.9 %collective-permute-start.4 = (bf16[384,1024]{1,0:T(8,128)(2,1)S(1)}, bf16[384,1024]{1,0:T(8,128)(2,1)S(1)}, u32[]{:S(2)}, u32[]{:S(2)}) collective-permute-start(bf16[384,1024]{1,0:T(8,128)(2,1)S(1)} %collective-permute-done.3.refs_2_), channel_id=1, source_target_pairs={{0,7},{1,2},{2,1},{3,4},{4,3},{5,6},{6,5},{7,0},{8,9},{9,8},{10,11... | collective-permute-start | bytes 2359304 | tf_op jit(solution)/shard_map/ppermute | solution.py:474
  42.1 0.1 fusion.3
  42.2 5.1 %collective-permute-start.7 = (bf16[6,128,128]{2,1,0:T(8,128)(2,1)S(1)}, bf16[6,128,128]{2,1,0:T(8,128)(2,1)S(1)}, u32[]{:S(2)}, u32[]{:S(2)}) collective-permute-start(bf16[6,128,128]{2,1,0:T(8,128)(2,1)S(1)} %fusion.3), channel_id=1, source_target_pairs={{0,16},{8,24},{16,32},{24,40},{32,48},{40,56},{48,64},{56,72},{64,... | collective-permute-start | bytes 589832 | tf_op jit(solution)/shard_map/ppermute | solution.py:465
  47.4 7.7 %collective-permute-start = (bf16[128,1024]{1,0:T(8,128)(2,1)S(1)}, bf16[128,1024]{1,0:T(8,128)(2,1)S(1)}, u32[]{:S(2)}, u32[]{:S(2)}) collective-permute-start(bf16[128,1024]{1,0:T(8,128)(2,1)S(1)} %copy-done.6), channel_id=1, source_target_pairs={{0,8},{8,0},{1,9},{9,1},{2,10},{10,2},{3,11},{11,3},{4,12},{12,4},... | collective-permute-start | bytes 786440 | tf_op jit(solution)/shard_map/ppermute | solution.py:459
  55.1 0.0 copy-start.3
  55.1 0.1 add_convert_fusion
  55.2 3.2 %collective-permute-start.9 = (bf16[6,128,128]{2,1,0:T(8,128)(2,1)S(1)}, bf16[6,128,128]{2,1,0:T(8,128)(2,1)S(1)}, u32[]{:S(2)}, u32[]{:S(2)}) collective-permute-start(bf16[6,128,128]{2,1,0:T(8,128)(2,1)S(1)} %add_convert_fusion), channel_id=1, source_target_pairs={{0,48},{8,56},{16,64},{24,72},{32,80},{40,88},{48,96},{56,104},{64... | collective-permute-start | bytes 589832 | tf_op jit(solution)/shard_map/ppermute | solution.py:465
  58.4 4.2 %collective-permute-start.8 = (bf16[6,128,128]{2,1,0:T(8,128)(2,1)S(1)}, bf16[6,128,128]{2,1,0:T(8,128)(2,1)S(1)}, u32[]{:S(2)}, u32[]{:S(2)}) collective-permute-start(bf16[6,128,128]{2,1,0:T(8,128)(2,1)S(1)} %add_convert_fusion), channel_id=1, source_target_pairs={{0,16},{8,24},{16,32},{24,40},{32,48},{40,56},{48,64},{56,72},{64,... | collective-permute-start | bytes 589832 | tf_op jit(solution)/shard_map/ppermute | solution.py:465
  62.7 1.2 %share_part.1 = (f32[1536,128]{1,0:T(8,128)S(1)}, bf16[1536,128]{1,0:T(8,128)(2,1)S(1)}) custom-call(bf16[128,1024]{1,0:T(8,128)(2,1)S(1)} %copy-done.3, bf16[128,1024]{1,0:T(8,128)(2,1)S(1)} %collective-permute-done.cot_got_ref, bf16[384,1024]{1,0:T(8,128)(2,1)S(1)} %constant_dynamic-update-slice_fusion.refs_0_, ...), custom_call_target="tpu_custom_call" | custom-call | flops 700000000 | bytes 4500000 | tf_op jit(solution)/shard_map/share_part/pallas_call | solution.py:291
  63.9 0.5 share_end.1
  64.4 5.3 %collective-permute-start.5 = (bf16[1536,128]{1,0:T(8,128)(2,1)S(1)}, bf16[1536,128]{1,0:T(8,128)(2,1)S(1)}, u32[]{:S(2)}, u32[]{:S(2)}) collective-permute-start(bf16[1536,128]{1,0:T(8,128)(2,1)S(1)} %get-tuple-element.35), channel_id=1, source_target_pairs={{0,8},{8,0},{1,9},{9,1},{2,10},{10,2},{3,11},{11,3},{4,12},{12,4},... | collective-permute-start | bytes 1179656 | tf_op jit(solution)/shard_map/ppermute | solution.py:459
  69.8 0.0 copy-start.5
  69.8 0.0 copy-start
  69.8 0.2 fusion.5
  70.0 1.9 %collective-permute-start.10 = (bf16[6,128,128]{2,1,0:T(8,128)(2,1)S(1)}, bf16[6,128,128]{2,1,0:T(8,128)(2,1)S(1)}, u32[]{:S(2)}, u32[]{:S(2)}) collective-permute-start(bf16[6,128,128]{2,1,0:T(8,128)(2,1)S(1)} %get-tuple-element.56), channel_id=1, source_target_pairs={{0,8},{8,0},{1,9},{9,1},{2,10},{10,2},{3,11},{11,3},{4,12},{12,4},... | collective-permute-start | bytes 589832 | tf_op jit(solution)/shard_map/ppermute | solution.py:459
  72.0 2.5 %inside_part.1 = (bf16[12,128,128]{2,1,0:T(8,128)(2,1)S(1)}, f32[128,1536]{1,0:T(8,128)S(1)}) custom-call(s32[1,16]{1,0:T(1,128)S(1)} %copy-done.4, bf16[128,1536]{1,0:T(8,128)(2,1)S(1)} %bitcast.46, bf16[128,1536]{1,0:T(8,128)(2,1)S(1)} %bitcast.51, bf16[128,1536]{1,0:T(8,128)(2,1)S(1)} %bitcast.55), custom_call_target="tpu_custom_call" | custom-call | flops 100000000 | bytes 2400000 | tf_op jit(solution)/shard_map/inside_part/pallas_call | solution.py:219
  74.5 1.0 mixed_part.1
  75.5 2.2 %grad_mixed_part.1 = (bf16[128,1536]{1,0:T(8,128)(2,1)S(1)}, bf16[6,128,128]{2,1,0:T(8,128)(2,1)S(1)}, bf16[6,128,128]{2,1,0:T(8,128)(2,1)S(1)}) custom-call(s32[1,16]{1,0:T(1,128)S(1)} %copy-done.4, f32[1536,128]{1,0:T(8,128)S(1)} %get-tuple-element.34.own_ref, bf16[1536,128]{1,0:T(8,128)(2,1)S(1)} %collective-permute-done.5.got_ref, ...), custom_call_target="tpu_custom_call" | custom-call | flops 60000000 | bytes 4000000 | tf_op jit(solution)/shard_map/grad_mixed_part/pallas_call | solution.py:350
  77.7 2.4 %collective-permute-start.13 = (bf16[6,128,128]{2,1,0:T(8,128)(2,1)S(1)}, bf16[6,128,128]{2,1,0:T(8,128)(2,1)S(1)}, u32[]{:S(2)}, u32[]{:S(2)}) collective-permute-start(bf16[6,128,128]{2,1,0:T(8,128)(2,1)S(1)} %get-tuple-element.48), channel_id=1, source_target_pairs={{0,8},{8,0},{1,9},{9,1},{2,10},{10,2},{3,11},{11,3},{4,12},{12,4},... | collective-permute-start | bytes 589832 | tf_op jit(solution)/shard_map/ppermute | solution.py:459
  80.1 1.9 %collective-permute-start.11 = (bf16[128,1536]{1,0:T(8,128)(2,1)S(1)}, bf16[128,1536]{1,0:T(8,128)(2,1)S(1)}, u32[]{:S(2)}, u32[]{:S(2)}) collective-permute-start(bf16[128,1536]{1,0:T(8,128)(2,1)S(1)} %get-tuple-element.45.scaled_ref), channel_id=1, source_target_pairs={{0,8},{8,0},{1,9},{9,1},{2,10},{10,2},{3,11},{11,3},{4,12},{12,4},... | collective-permute-start | bytes 1179656 | tf_op jit(solution)/shard_map/ppermute | solution.py:459
  82.0 0.1 fusion.9
  82.1 1.9 %collective-permute-start.17 = (bf16[6,128,128]{2,1,0:T(8,128)(2,1)S(1)}, bf16[6,128,128]{2,1,0:T(8,128)(2,1)S(1)}, u32[]{:S(2)}, u32[]{:S(2)}) collective-permute-start(bf16[6,128,128]{2,1,0:T(8,128)(2,1)S(1)} %fusion.9), channel_id=1, source_target_pairs={{64,0},{72,8},{80,16},{88,24},{96,32},{104,40},{112,48},{120,56},{... | collective-permute-start | bytes 589832 | tf_op jit(solution)/shard_map/ppermute | solution.py:465
  84.1 3.6 %collective-permute-start.16 = (bf16[6,128,128]{2,1,0:T(8,128)(2,1)S(1)}, bf16[6,128,128]{2,1,0:T(8,128)(2,1)S(1)}, u32[]{:S(2)}, u32[]{:S(2)}) collective-permute-start(bf16[6,128,128]{2,1,0:T(8,128)(2,1)S(1)} %fusion.9), channel_id=1, source_target_pairs={{48,0},{56,8},{64,16},{72,24},{80,32},{88,40},{96,48},{104,56},{11... | collective-permute-start | bytes 589832 | tf_op jit(solution)/shard_map/ppermute | solution.py:465
  87.7 3.3 %collective-permute-start.15 = (bf16[6,128,128]{2,1,0:T(8,128)(2,1)S(1)}, bf16[6,128,128]{2,1,0:T(8,128)(2,1)S(1)}, u32[]{:S(2)}, u32[]{:S(2)}) collective-permute-start(bf16[6,128,128]{2,1,0:T(8,128)(2,1)S(1)} %fusion.9), channel_id=1, source_target_pairs={{32,0},{40,8},{48,16},{56,24},{64,32},{72,40},{80,48},{88,56},{96,... | collective-permute-start | bytes 589832 | tf_op jit(solution)/shard_map/ppermute | solution.py:465
  91.0 1.9 %collective-permute-start.14 = (bf16[6,128,128]{2,1,0:T(8,128)(2,1)S(1)}, bf16[6,128,128]{2,1,0:T(8,128)(2,1)S(1)}, u32[]{:S(2)}, u32[]{:S(2)}) collective-permute-start(bf16[6,128,128]{2,1,0:T(8,128)(2,1)S(1)} %fusion.9), channel_id=1, source_target_pairs={{16,0},{24,8},{32,16},{40,24},{48,32},{56,40},{64,48},{72,56},{80,... | collective-permute-start | bytes 589832 | tf_op jit(solution)/shard_map/ppermute | solution.py:465
  92.9 1.2 %output_part.1 = (bf16[128,1024]{1,0:T(8,128)(2,1)S(1)}, bf16[128,1024]{1,0:T(8,128)(2,1)S(1)}) custom-call(bf16[128,1536]{1,0:T(8,128)(2,1)S(1)} %get-tuple-element.45.scaled_ref, bf16[128,1536]{1,0:T(8,128)(2,1)S(1)} %collective-permute-done.11.scaled_got_ref, bf16[384,1024]{1,0:T(8,128)(2,1)S(1)} %constant_dynamic-update-slice_fusion.refs_0_, ...), custom_call_target="tpu_custom_call" | custom-call | flops 810000000 | bytes 5000000 | tf_op jit(solution)/shard_map/output_part/pallas_call | solution.py:376
  94.2 2.2 %collective-permute-start.12 = (bf16[128,1024]{1,0:T(8,128)(2,1)S(1)}, bf16[128,1024]{1,0:T(8,128)(2,1)S(1)}, u32[]{:S(2)}, u32[]{:S(2)}) collective-permute-start(bf16[128,1024]{1,0:T(8,128)(2,1)S(1)} %get-tuple-element.47), channel_id=1, source_target_pairs={{0,8},{8,0},{1,9},{9,1},{2,10},{10,2},{3,11},{11,3},{4,12},{12,4},... | collective-permute-start | bytes 786440 | tf_op jit(solution)/shard_map/ppermute | solution.py:459
  96.4 0.3 collective-permute-done.16
  96.7 6.3 %collective-permute-done.15 = bf16[6,128,128]{2,1,0:T(8,128)(2,1)S(1)} collective-permute-done((bf16[6,128,128]{2,1,0:T(8,128)(2,1)S(1)}, bf16[6,128,128]{2,1,0:T(8,128)(2,1)S(1)}, u32[]{:S(2)}, u32[]{:S(2)}) %collective-permute-start.15) | collective-permute-done | bytes 196640 | tf_op jit(solution)/shard_map/ppermute | solution.py:465
  102.9 4.4 %collective-permute-done.14 = bf16[6,128,128]{2,1,0:T(8,128)(2,1)S(1)} collective-permute-done((bf16[6,128,128]{2,1,0:T(8,128)(2,1)S(1)}, bf16[6,128,128]{2,1,0:T(8,128)(2,1)S(1)}, u32[]{:S(2)}, u32[]{:S(2)}) %collective-permute-start.14) | collective-permute-done | bytes 196640 | tf_op jit(solution)/shard_map/ppermute | solution.py:465
  107.4 0.3 fusion.11
  107.6 2.6 %collective-permute-start.18 = (bf16[6,128,128]{2,1,0:T(8,128)(2,1)S(1)}, bf16[6,128,128]{2,1,0:T(8,128)(2,1)S(1)}, u32[]{:S(2)}, u32[]{:S(2)}) collective-permute-start(bf16[6,128,128]{2,1,0:T(8,128)(2,1)S(1)} %get-tuple-element.54), channel_id=1, source_target_pairs={{0,8},{8,0},{1,9},{9,1},{2,10},{10,2},{3,11},{11,3},{4,12},{12,4},... | collective-permute-start | bytes 589832 | tf_op jit(solution)/shard_map/ppermute | solution.py:459
  110.2 3.9 %grads_part.1 = (bf16[128,1536]{1,0:T(8,128)(2,1)}, f32[128,1536]{1,0:T(8,128)S(1)}, f32[128,1536]{1,0:T(8,128)S(1)}) custom-call(s32[1,16]{1,0:T(1,128)S(1)} %copy-done.4, bf16[128,1536]{1,0:T(8,128)(2,1)S(1)} %bitcast.49, bf16[128,1536]{1,0:T(8,128)(2,1)S(1)} %bitcast.52, bf16[128,1536]{1,0:T(8,128)(2,1)S(1)} %bitcast.56, ...), custom_call_target="tpu_custom_call" | custom-call | flops 250000000 | bytes 5000000 | tf_op jit(solution)/shard_map/grads_part/pallas_call | solution.py:412
  114.2 2.1 %last_part.1 = (bf16[128,1536]{1,0:T(8,128)(2,1)}, bf16[128,1536]{1,0:T(8,128)(2,1)}, bf16[128,2048]{1,0:T(8,128)(2,1)}) custom-call(s32[1,16]{1,0:T(1,128)S(1)} %copy-done.4, bf16[128,1536]{1,0:T(8,128)(2,1)S(1)} %bitcast.53, bf16[128,1536]{1,0:T(8,128)(2,1)S(1)} %bitcast.57, f32[128,1536]{1,0:T(8,128)S(1)} %get-tuple-element.43.dk_part_ref, ...), custom_call_target="tpu_custom_call" | custom-call | flops 100000000 | bytes 4500000 | tf_op jit(solution)/shard_map/last_part/pallas_call | solution.py:447
  (23 shorter events, 0.1 us)
Async XLA Ops:
  2.7 10.5 %collective-permute-start.1 = (bf16[192,1024]{1,0:T(8,128)(2,1)}, bf16[192,1024]{1,0:T(8,128)(2,1)S(1)}, u32[]{:S(2)}, u32[]{:S(2)}) collective-permute-start(bf16[192,1024]{1,0:T(8,128)(2,1)} %get-tuple-element.31), channel_id=1, source_target_pairs={{0,1},{1,0},{2,3},{3,2},{4,5},{5,4},{6,7},{7,6},{8,15},{9,10},{10,... | collective-permute-start | bytes 1179656 | tf_op jit(solution)/shard_map/ppermute | solution.py:474
  8.9 22.0 %copy-start.1 = (bf16[1,128,1536]{2,1,0:T(8,128)(2,1)S(1)}, bf16[1,128,1536]{2,1,0:T(8,128)(2,1)}, u32[]{:S(2)}) copy-start(bf16[1,128,1536]{2,1,0:T(8,128)(2,1)} %param.8) | copy-start | bytes 1179652
  8.9 22.0 %copy-start.2 = (bf16[1,128,1536]{2,1,0:T(8,128)(2,1)S(1)}, bf16[1,128,1536]{2,1,0:T(8,128)(2,1)}, u32[]{:S(2)}) copy-start(bf16[1,128,1536]{2,1,0:T(8,128)(2,1)} %param.9) | copy-start | bytes 1179652
  13.2 13.0 %collective-permute-start.2 = (bf16[384,1024]{1,0:T(8,128)(2,1)S(1)}, bf16[384,1024]{1,0:T(8,128)(2,1)S(1)}, u32[]{:S(2)}, u32[]{:S(2)}) collective-permute-start(bf16[384,1024]{1,0:T(8,128)(2,1)S(1)} %constant_dynamic-update-slice_fusion.refs_0_), channel_id=1, source_target_pairs={{0,7},{1,2},{2,1},{3,4},{4,3},{5,6},{6,5},{7,0},{8,9},{9,8},{10,11... | collective-permute-start | bytes 2359304 | tf_op jit(solution)/shard_map/ppermute | solution.py:474
  26.3 13.9 %collective-permute-start.3 = (bf16[384,1024]{1,0:T(8,128)(2,1)S(1)}, bf16[384,1024]{1,0:T(8,128)(2,1)S(1)}, u32[]{:S(2)}, u32[]{:S(2)}) collective-permute-start(bf16[384,1024]{1,0:T(8,128)(2,1)S(1)} %collective-permute-done.2.refs_1_), channel_id=1, source_target_pairs={{0,1},{1,0},{2,3},{3,2},{4,5},{5,4},{6,7},{7,6},{8,15},{9,10},{10,... | collective-permute-start | bytes 2359304 | tf_op jit(solution)/shard_map/ppermute | solution.py:474
  30.8 0.7 copy-start.4
  32.9 9.2 %collective-permute-start.6 = (bf16[6,128,128]{2,1,0:T(8,128)(2,1)S(1)}, bf16[6,128,128]{2,1,0:T(8,128)(2,1)S(1)}, u32[]{:S(2)}, u32[]{:S(2)}) collective-permute-start(bf16[6,128,128]{2,1,0:T(8,128)(2,1)S(1)} %get-tuple-element.38), channel_id=1, source_target_pairs={{0,8},{8,0},{1,9},{9,1},{2,10},{10,2},{3,11},{11,3},{4,12},{12,4},... | collective-permute-start | bytes 589832 | tf_op jit(solution)/shard_map/ppermute | solution.py:459
  40.2 23.7 %collective-permute-start.4 = (bf16[384,1024]{1,0:T(8,128)(2,1)S(1)}, bf16[384,1024]{1,0:T(8,128)(2,1)S(1)}, u32[]{:S(2)}, u32[]{:S(2)}) collective-permute-start(bf16[384,1024]{1,0:T(8,128)(2,1)S(1)} %collective-permute-done.3.refs_2_), channel_id=1, source_target_pairs={{0,7},{1,2},{2,1},{3,4},{4,3},{5,6},{6,5},{7,0},{8,9},{9,8},{10,11... | collective-permute-start | bytes 2359304 | tf_op jit(solution)/shard_map/ppermute | solution.py:474
  42.1 5.2 %copy-start.6 = (bf16[128,1024]{1,0:T(8,128)(2,1)S(1)}, bf16[128,1024]{1,0:T(8,128)(2,1)}, u32[]{:S(2)}) copy-start(bf16[128,1024]{1,0:T(8,128)(2,1)} %get-tuple-element.30) | copy-start | bytes 786436
  42.2 12.9 %collective-permute-start.7 = (bf16[6,128,128]{2,1,0:T(8,128)(2,1)S(1)}, bf16[6,128,128]{2,1,0:T(8,128)(2,1)S(1)}, u32[]{:S(2)}, u32[]{:S(2)}) collective-permute-start(bf16[6,128,128]{2,1,0:T(8,128)(2,1)S(1)} %fusion.3), channel_id=1, source_target_pairs={{0,16},{8,24},{16,32},{24,40},{32,48},{40,56},{48,64},{56,72},{64,... | collective-permute-start | bytes 589832 | tf_op jit(solution)/shard_map/ppermute | solution.py:465
  47.4 15.3 %collective-permute-start = (bf16[128,1024]{1,0:T(8,128)(2,1)S(1)}, bf16[128,1024]{1,0:T(8,128)(2,1)S(1)}, u32[]{:S(2)}, u32[]{:S(2)}) collective-permute-start(bf16[128,1024]{1,0:T(8,128)(2,1)S(1)} %copy-done.6), channel_id=1, source_target_pairs={{0,8},{8,0},{1,9},{9,1},{2,10},{10,2},{3,11},{11,3},{4,12},{12,4},... | collective-permute-start | bytes 786440 | tf_op jit(solution)/shard_map/ppermute | solution.py:459
  55.1 7.5 %copy-start.3 = (bf16[128,1024]{1,0:T(8,128)(2,1)S(1)}, bf16[128,1024]{1,0:T(8,128)(2,1)}, u32[]{:S(2)}) copy-start(bf16[128,1024]{1,0:T(8,128)(2,1)} %get-tuple-element.29.cot_keep_ref) | copy-start | bytes 786436
  55.2 14.5 %collective-permute-start.9 = (bf16[6,128,128]{2,1,0:T(8,128)(2,1)S(1)}, bf16[6,128,128]{2,1,0:T(8,128)(2,1)S(1)}, u32[]{:S(2)}, u32[]{:S(2)}) collective-permute-start(bf16[6,128,128]{2,1,0:T(8,128)(2,1)S(1)} %add_convert_fusion), channel_id=1, source_target_pairs={{0,48},{8,56},{16,64},{24,72},{32,80},{40,88},{48,96},{56,104},{64... | collective-permute-start | bytes 589832 | tf_op jit(solution)/shard_map/ppermute | solution.py:465
  58.4 11.4 %collective-permute-start.8 = (bf16[6,128,128]{2,1,0:T(8,128)(2,1)S(1)}, bf16[6,128,128]{2,1,0:T(8,128)(2,1)S(1)}, u32[]{:S(2)}, u32[]{:S(2)}) collective-permute-start(bf16[6,128,128]{2,1,0:T(8,128)(2,1)S(1)} %add_convert_fusion), channel_id=1, source_target_pairs={{0,16},{8,24},{16,32},{24,40},{32,48},{40,56},{48,64},{56,72},{64,... | collective-permute-start | bytes 589832 | tf_op jit(solution)/shard_map/ppermute | solution.py:465
  64.4 11.1 %collective-permute-start.5 = (bf16[1536,128]{1,0:T(8,128)(2,1)S(1)}, bf16[1536,128]{1,0:T(8,128)(2,1)S(1)}, u32[]{:S(2)}, u32[]{:S(2)}) collective-permute-start(bf16[1536,128]{1,0:T(8,128)(2,1)S(1)} %get-tuple-element.35), channel_id=1, source_target_pairs={{0,8},{8,0},{1,9},{9,1},{2,10},{10,2},{3,11},{11,3},{4,12},{12,4},... | collective-permute-start | bytes 1179656 | tf_op jit(solution)/shard_map/ppermute | solution.py:459
  69.8 2.2 %copy-start.5 = (f32[1536]{0:T(1024)S(1)}, f32[1536]{0:T(1024)}, u32[]{:S(2)}) copy-start(f32[1536]{0:T(1024)} %param.11) | copy-start | bytes 18436
  69.8 2.2 %copy-start = (bf16[1,128,1536]{2,1,0:T(8,128)(2,1)S(1)}, bf16[1,128,1536]{2,1,0:T(8,128)(2,1)}, u32[]{:S(2)}) copy-start(bf16[1,128,1536]{2,1,0:T(8,128)(2,1)} %param.7) | copy-start | bytes 1179652
  70.0 4.5 %collective-permute-start.10 = (bf16[6,128,128]{2,1,0:T(8,128)(2,1)S(1)}, bf16[6,128,128]{2,1,0:T(8,128)(2,1)S(1)}, u32[]{:S(2)}, u32[]{:S(2)}) collective-permute-start(bf16[6,128,128]{2,1,0:T(8,128)(2,1)S(1)} %get-tuple-element.56), channel_id=1, source_target_pairs={{0,8},{8,0},{1,9},{9,1},{2,10},{10,2},{3,11},{11,3},{4,12},{12,4},... | collective-permute-start | bytes 589832 | tf_op jit(solution)/shard_map/ppermute | solution.py:459
  77.7 4.3 %collective-permute-start.13 = (bf16[6,128,128]{2,1,0:T(8,128)(2,1)S(1)}, bf16[6,128,128]{2,1,0:T(8,128)(2,1)S(1)}, u32[]{:S(2)}, u32[]{:S(2)}) collective-permute-start(bf16[6,128,128]{2,1,0:T(8,128)(2,1)S(1)} %get-tuple-element.48), channel_id=1, source_target_pairs={{0,8},{8,0},{1,9},{9,1},{2,10},{10,2},{3,11},{11,3},{4,12},{12,4},... | collective-permute-start | bytes 589832 | tf_op jit(solution)/shard_map/ppermute | solution.py:459
  80.1 12.8 %collective-permute-start.11 = (bf16[128,1536]{1,0:T(8,128)(2,1)S(1)}, bf16[128,1536]{1,0:T(8,128)(2,1)S(1)}, u32[]{:S(2)}, u32[]{:S(2)}) collective-permute-start(bf16[128,1536]{1,0:T(8,128)(2,1)S(1)} %get-tuple-element.45.scaled_ref), channel_id=1, source_target_pairs={{0,8},{8,0},{1,9},{9,1},{2,10},{10,2},{3,11},{11,3},{4,12},{12,4},... | collective-permute-start | bytes 1179656 | tf_op jit(solution)/shard_map/ppermute | solution.py:459
  82.1 14.3 %collective-permute-start.17 = (bf16[6,128,128]{2,1,0:T(8,128)(2,1)S(1)}, bf16[6,128,128]{2,1,0:T(8,128)(2,1)S(1)}, u32[]{:S(2)}, u32[]{:S(2)}) collective-permute-start(bf16[6,128,128]{2,1,0:T(8,128)(2,1)S(1)} %fusion.9), channel_id=1, source_target_pairs={{64,0},{72,8},{80,16},{88,24},{96,32},{104,40},{112,48},{120,56},{... | collective-permute-start | bytes 589832 | tf_op jit(solution)/shard_map/ppermute | solution.py:465
  84.1 12.6 %collective-permute-start.16 = (bf16[6,128,128]{2,1,0:T(8,128)(2,1)S(1)}, bf16[6,128,128]{2,1,0:T(8,128)(2,1)S(1)}, u32[]{:S(2)}, u32[]{:S(2)}) collective-permute-start(bf16[6,128,128]{2,1,0:T(8,128)(2,1)S(1)} %fusion.9), channel_id=1, source_target_pairs={{48,0},{56,8},{64,16},{72,24},{80,32},{88,40},{96,48},{104,56},{11... | collective-permute-start | bytes 589832 | tf_op jit(solution)/shard_map/ppermute | solution.py:465
  87.7 15.2 %collective-permute-start.15 = (bf16[6,128,128]{2,1,0:T(8,128)(2,1)S(1)}, bf16[6,128,128]{2,1,0:T(8,128)(2,1)S(1)}, u32[]{:S(2)}, u32[]{:S(2)}) collective-permute-start(bf16[6,128,128]{2,1,0:T(8,128)(2,1)S(1)} %fusion.9), channel_id=1, source_target_pairs={{32,0},{40,8},{48,16},{56,24},{64,32},{72,40},{80,48},{88,56},{96,... | collective-permute-start | bytes 589832 | tf_op jit(solution)/shard_map/ppermute | solution.py:465
  91.0 16.4 %collective-permute-start.14 = (bf16[6,128,128]{2,1,0:T(8,128)(2,1)S(1)}, bf16[6,128,128]{2,1,0:T(8,128)(2,1)S(1)}, u32[]{:S(2)}, u32[]{:S(2)}) collective-permute-start(bf16[6,128,128]{2,1,0:T(8,128)(2,1)S(1)} %fusion.9), channel_id=1, source_target_pairs={{16,0},{24,8},{32,16},{40,24},{48,32},{56,40},{64,48},{72,56},{80,... | collective-permute-start | bytes 589832 | tf_op jit(solution)/shard_map/ppermute | solution.py:465
  94.2 20.0 %collective-permute-start.12 = (bf16[128,1024]{1,0:T(8,128)(2,1)S(1)}, bf16[128,1024]{1,0:T(8,128)(2,1)S(1)}, u32[]{:S(2)}, u32[]{:S(2)}) collective-permute-start(bf16[128,1024]{1,0:T(8,128)(2,1)S(1)} %get-tuple-element.47), channel_id=1, source_target_pairs={{0,8},{8,0},{1,9},{9,1},{2,10},{10,2},{3,11},{11,3},{4,12},{12,4},... | collective-permute-start | bytes 786440 | tf_op jit(solution)/shard_map/ppermute | solution.py:459
  107.6 6.5 %collective-permute-start.18 = (bf16[6,128,128]{2,1,0:T(8,128)(2,1)S(1)}, bf16[6,128,128]{2,1,0:T(8,128)(2,1)S(1)}, u32[]{:S(2)}, u32[]{:S(2)}) collective-permute-start(bf16[6,128,128]{2,1,0:T(8,128)(2,1)S(1)} %get-tuple-element.54), channel_id=1, source_target_pairs={{0,8},{8,0},{1,9},{9,1},{2,10},{10,2},{3,11},{11,3},{4,12},{12,4},... | collective-permute-start | bytes 589832 | tf_op jit(solution)/shard_map/ppermute | solution.py:459

commit v5 on v4

--- a/solution.py
+++ b/solution.py
@@ -22,7 +22,6 @@
 
 CA, CB, MP, ME1, ME3, CS, ES, CR, ER = range(9)
 BACK = 9
-BACK_2, BACK_4 = 18, 19
 ROWS = 24
 
 VMEM = pl.BlockSpec(memory_space=pltpu.VMEM)
@@ -178,9 +177,7 @@
     put(BACK + ES, jnp.where(low, one, across))
     put(BACK + CR, jnp.where(low, one, zero))
     put(BACK + ER, jnp.where(low, across, one))
-    put(BACK_2, flag((chip <= CHIPS - 3) & same(ends, base + 256, base + 512)))
-    put(BACK_4, flag((chip <= CHIPS - 5) & same(ends, base + 256, base + 1024)))
-    for row in range(BACK_4 + 1, ROWS):
+    for row in range(2 * BACK, ROWS):
         put(row, zero)
 
 
@@ -481,17 +478,11 @@
     got = swap_cores(give).astype(F32)
     own = keep.astype(F32)
     chip_sum = (row(CA) * own + row(CB) * got).astype(BF16)
-    if sign > 0:
-        before = from_chip(chip_sum, sign)
-        pair_sum = (chip_sum.astype(F32) + row(MP) * before.astype(F32)).astype(BF16)
-        near = from_chip(pair_sum, sign)
-        far = from_chip(pair_sum, 3 * sign)
-        enter = row(ME1) * near.astype(F32) + row(ME3) * far.astype(F32)
-    else:
-        sums = []
-        for chips in (1, 2, 3, 4):
-            sums.append(from_chip(chip_sum, chips * sign).astype(F32))
-        enter = row(ME1) * sums[0] + coef[BACK_2] * sums[1] + row(ME3) * sums[2] + coef[BACK_4] * sums[3]
+    before = from_chip(chip_sum, sign)
+    pair_sum = (chip_sum.astype(F32) + row(MP) * before.astype(F32)).astype(BF16)
+    near = from_chip(pair_sum, sign)
+    far = from_chip(pair_sum, 3 * sign)
+    enter = row(ME1) * near.astype(F32) + row(ME3) * far.astype(F32)
     other = swap_cores((row(CS) * own + row(ES) * enter).astype(BF16))
     mine = (row(CR) * got + row(ER) * enter).astype(BF16)
     return mine, other

time: 117 us -> 116 us (level)
  starting transfers between devices: 62.8 us -> 61.3 us
    ppermute x7 -> x6, starting transfers between devices: 23.3 us -> 19.2 us  [from_chip(): return lax.ppermute(block, ('z', 'x', 'core'), pairs)]
    ppermute x8, starting transfers between devices: 26 us -> 28.6 us  [swap_cores(): return lax.ppermute(block, 'core', [(0, 1), (1, 0)])]
    ppermute x7 -> x6, waiting for transfers between devices: 11 us -> 10.5 us  [from_chip(): return lax.ppermute(block, ('z', 'x', 'core'), pairs)]
  transfers between devices with their start and end apart: 19 -> 18, of which waited for: 6 -> 7; matrix products, arithmetic and copies ran while one was open for 2% -> 1% of each run, Pallas kernels for 10% -> 10%
where the time goes in v5:
time: 116 us; the launch traced here: 115 us
  starting transfers between devices  61.3 us (53%)
  waiting for transfers between devices  32.4 us (28%)
  Pallas kernels  18.1 us (16%)
  local copies, waits for them, and re-layouts  1.75 us (2%)
    ppermute x8, starting transfers between devices, swap_cores(): return lax.ppermute(block, 'core', [(0, 1), (1, 0)])  28.6 us
    ppermute x4, waiting for transfers between devices, exchange(): return lax.ppermute(block, ('core', 'fsdp'), pairs)  20.8 us
    ppermute x6, starting transfers between devices, from_chip(): return lax.ppermute(block, ('z', 'x', 'core'), pairs)  19.2 us
    ppermute x4, starting transfers between devices, exchange(): return lax.ppermute(block, ('core', 'fsdp'), pairs)  13.5 us
    ppermute x6, waiting for transfers between devices, from_chip(): return lax.ppermute(block, ('z', 'x', 'core'), pairs)  10.5 us
    pallas_call x1, Pallas kernels, grads_part(): pl.pallas_call(grads_kernel, out_shape=(jax.ShapeDtypeStruct((TOK, DI), B...  4 us
    pallas_call x1, Pallas kernels, inside_part(): pl.pallas_call(inside_kernel, out_shape=(jax.ShapeDtypeStruct((HEADS, TOK...  2.5 us
  transfers between devices with their start and end apart: 18, of which 7 were waited for; matrix products, arithmetic and copies ran while one was open for 1% of the time, Pallas kernels for 10%

profile of v5, /device:TPU:199, one launch (start us, length us, event | category | flops | bytes accessed | tf_op | source)
XLA Modules:
  0.0 115.4 jit_solution(17332777944425000837)
XLA Ops:
  0.6 2.1 %take_half.1 = (bf16[192,1024]{1,0:T(8,128)(2,1)}, bf16[128,1024]{1,0:T(8,128)(2,1)}, bf16[128,1024]{1,0:T(8,128)(2,1)}) custom-call(bf16[192,2048]{1,0:T(8,128)(2,1)} %weight_ref.1, bf16[128,2048]{1,0:T(8,128)(2,1)} %bitcast.56), custom_call_target="tpu_custom_call" | custom-call | flops 1000 | bytes 2000000 | tf_op jit(solution)/shard_map/take_half/pallas_call | solution.py:115
  2.7 5.1 %collective-permute-start.1 = (bf16[192,1024]{1,0:T(8,128)(2,1)}, bf16[192,1024]{1,0:T(8,128)(2,1)S(1)}, u32[]{:S(2)}, u32[]{:S(2)}) collective-permute-start(bf16[192,1024]{1,0:T(8,128)(2,1)} %get-tuple-element.31), channel_id=1, source_target_pairs={{0,1},{1,0},{2,3},{3,2},{4,5},{5,4},{6,7},{7,6},{8,15},{9,10},{10,... | collective-permute-start | bytes 1179656 | tf_op jit(solution)/shard_map/ppermute | solution.py:471
  7.8 1.0 constant_dynamic-update-slice_fusion.1
  8.9 0.0 copy-start.1
  8.9 4.3 %collective-permute-done.1 = bf16[192,1024]{1,0:T(8,128)(2,1)S(1)} collective-permute-done((bf16[192,1024]{1,0:T(8,128)(2,1)}, bf16[192,1024]{1,0:T(8,128)(2,1)S(1)}, u32[]{:S(2)}, u32[]{:S(2)}) %collective-permute-start.1) | collective-permute-done | bytes 393248 | tf_op jit(solution)/shard_map/ppermute | solution.py:471
  13.2 1.9 %collective-permute-start.2 = (bf16[384,1024]{1,0:T(8,128)(2,1)S(1)}, bf16[384,1024]{1,0:T(8,128)(2,1)S(1)}, u32[]{:S(2)}, u32[]{:S(2)}) collective-permute-start(bf16[384,1024]{1,0:T(8,128)(2,1)S(1)} %constant_dynamic-update-slice_fusion.refs_0_), channel_id=1, source_target_pairs={{0,7},{1,2},{2,1},{3,4},{4,3},{5,6},{6,5},{7,0},{8,9},{9,8},{10,11... | collective-permute-start | bytes 2359304 | tf_op jit(solution)/shard_map/ppermute | solution.py:471
  15.2 11.1 %collective-permute-done.2.refs_1_ = bf16[384,1024]{1,0:T(8,128)(2,1)S(1)} collective-permute-done((bf16[384,1024]{1,0:T(8,128)(2,1)S(1)}, bf16[384,1024]{1,0:T(8,128)(2,1)S(1)}, u32[]{:S(2)}, u32[]{:S(2)}) %collective-permute-start.2) | collective-permute-done | bytes 786464 | tf_op jit(solution)/shard_map/ppermute | solution.py:471
  26.3 4.6 %collective-permute-start.3 = (bf16[384,1024]{1,0:T(8,128)(2,1)S(1)}, bf16[384,1024]{1,0:T(8,128)(2,1)S(1)}, u32[]{:S(2)}, u32[]{:S(2)}) collective-permute-start(bf16[384,1024]{1,0:T(8,128)(2,1)S(1)} %collective-permute-done.2.refs_1_), channel_id=1, source_target_pairs={{0,1},{1,0},{2,3},{3,2},{4,5},{5,4},{6,7},{7,6},{8,15},{9,10},{10,... | collective-permute-start | bytes 2359304 | tf_op jit(solution)/shard_map/ppermute | solution.py:471
  30.8 0.0 copy-start.4
  30.9 0.6 copy-done.4
  31.5 1.3 %local_state.1 = (bf16[6,128,128]{2,1,0:T(8,128)(2,1)S(1)}, bf16[6,128,128]{2,1,0:T(8,128)(2,1)S(1)}, f32[24,128]{1,0:T(8,128)S(1)}) custom-call(s32[1,16]{1,0:T(1,128)S(1)} %copy-done.4, bf16[128,1536]{1,0:T(8,128)(2,1)S(1)} %bitcast.48, bf16[128,1536]{1,0:T(8,128)(2,1)S(1)} %bitcast.52), custom_call_target="tpu_custom_call" | custom-call | flops 50000000 | bytes 1200000 | tf_op jit(solution)/shard_map/local_state/pallas_call | solution.py:186
  32.8 1.9 %collective-permute-start.6 = (bf16[6,128,128]{2,1,0:T(8,128)(2,1)S(1)}, bf16[6,128,128]{2,1,0:T(8,128)(2,1)S(1)}, u32[]{:S(2)}, u32[]{:S(2)}) collective-permute-start(bf16[6,128,128]{2,1,0:T(8,128)(2,1)S(1)} %get-tuple-element.38), channel_id=1, source_target_pairs={{0,8},{8,0},{1,9},{9,1},{2,10},{10,2},{3,11},{11,3},{4,12},{12,4},... | collective-permute-start | bytes 589832 | tf_op jit(solution)/shard_map/ppermute | solution.py:456
  34.8 5.4 %collective-permute-done.3.refs_2_ = bf16[384,1024]{1,0:T(8,128)(2,1)S(1)} collective-permute-done((bf16[384,1024]{1,0:T(8,128)(2,1)S(1)}, bf16[384,1024]{1,0:T(8,128)(2,1)S(1)}, u32[]{:S(2)}, u32[]{:S(2)}) %collective-permute-start.3) | collective-permute-done | bytes 786464 | tf_op jit(solution)/shard_map/ppermute | solution.py:471
  40.2 1.9 %collective-permute-start.4 = (bf16[384,1024]{1,0:T(8,128)(2,1)S(1)}, bf16[384,1024]{1,0:T(8,128)(2,1)S(1)}, u32[]{:S(2)}, u32[]{:S(2)}) collective-permute-start(bf16[384,1024]{1,0:T(8,128)(2,1)S(1)} %collective-permute-done.3.refs_2_), channel_id=1, source_target_pairs={{0,7},{1,2},{2,1},{3,4},{4,3},{5,6},{6,5},{7,0},{8,9},{9,8},{10,11... | collective-permute-start | bytes 2359304 | tf_op jit(solution)/shard_map/ppermute | solution.py:471
  42.1 0.1 fusion.3
  42.2 5.1 %collective-permute-start.7 = (bf16[6,128,128]{2,1,0:T(8,128)(2,1)S(1)}, bf16[6,128,128]{2,1,0:T(8,128)(2,1)S(1)}, u32[]{:S(2)}, u32[]{:S(2)}) collective-permute-start(bf16[6,128,128]{2,1,0:T(8,128)(2,1)S(1)} %fusion.3), channel_id=1, source_target_pairs={{0,16},{8,24},{16,32},{24,40},{32,48},{40,56},{48,64},{56,72},{64,... | collective-permute-start | bytes 589832 | tf_op jit(solution)/shard_map/ppermute | solution.py:462
  47.4 7.7 %collective-permute-start = (bf16[128,1024]{1,0:T(8,128)(2,1)S(1)}, bf16[128,1024]{1,0:T(8,128)(2,1)S(1)}, u32[]{:S(2)}, u32[]{:S(2)}) collective-permute-start(bf16[128,1024]{1,0:T(8,128)(2,1)S(1)} %copy-done.6), channel_id=1, source_target_pairs={{0,8},{8,0},{1,9},{9,1},{2,10},{10,2},{3,11},{11,3},{4,12},{12,4},... | collective-permute-start | bytes 786440 | tf_op jit(solution)/shard_map/ppermute | solution.py:456
  55.1 0.0 copy-start.3
  55.1 0.1 add_convert_fusion.1
  55.2 3.2 %collective-permute-start.9 = (bf16[6,128,128]{2,1,0:T(8,128)(2,1)S(1)}, bf16[6,128,128]{2,1,0:T(8,128)(2,1)S(1)}, u32[]{:S(2)}, u32[]{:S(2)}) collective-permute-start(bf16[6,128,128]{2,1,0:T(8,128)(2,1)S(1)} %add_convert_fusion.1), channel_id=1, source_target_pairs={{0,48},{8,56},{16,64},{24,72},{32,80},{40,88},{48,96},{56,104},{64... | collective-permute-start | bytes 589832 | tf_op jit(solution)/shard_map/ppermute | solution.py:462
  58.4 4.2 %collective-permute-start.8 = (bf16[6,128,128]{2,1,0:T(8,128)(2,1)S(1)}, bf16[6,128,128]{2,1,0:T(8,128)(2,1)S(1)}, u32[]{:S(2)}, u32[]{:S(2)}) collective-permute-start(bf16[6,128,128]{2,1,0:T(8,128)(2,1)S(1)} %add_convert_fusion.1), channel_id=1, source_target_pairs={{0,16},{8,24},{16,32},{24,40},{32,48},{40,56},{48,64},{56,72},{64,... | collective-permute-start | bytes 589832 | tf_op jit(solution)/shard_map/ppermute | solution.py:462
  62.7 1.2 %share_part.1 = (f32[1536,128]{1,0:T(8,128)S(1)}, bf16[1536,128]{1,0:T(8,128)(2,1)S(1)}) custom-call(bf16[128,1024]{1,0:T(8,128)(2,1)S(1)} %copy-done.3, bf16[128,1024]{1,0:T(8,128)(2,1)S(1)} %collective-permute-done.cot_got_ref, bf16[384,1024]{1,0:T(8,128)(2,1)S(1)} %constant_dynamic-update-slice_fusion.refs_0_, ...), custom_call_target="tpu_custom_call" | custom-call | flops 700000000 | bytes 4500000 | tf_op jit(solution)/shard_map/share_part/pallas_call | solution.py:288
  63.9 0.5 share_end.1
  64.4 5.3 %collective-permute-start.5 = (bf16[1536,128]{1,0:T(8,128)(2,1)S(1)}, bf16[1536,128]{1,0:T(8,128)(2,1)S(1)}, u32[]{:S(2)}, u32[]{:S(2)}) collective-permute-start(bf16[1536,128]{1,0:T(8,128)(2,1)S(1)} %get-tuple-element.35), channel_id=1, source_target_pairs={{0,8},{8,0},{1,9},{9,1},{2,10},{10,2},{3,11},{11,3},{4,12},{12,4},... | collective-permute-start | bytes 1179656 | tf_op jit(solution)/shard_map/ppermute | solution.py:456
  69.8 0.0 copy-start.5
  69.8 0.0 copy-start
  69.8 0.2 fusion.5
  70.0 1.9 %collective-permute-start.10 = (bf16[6,128,128]{2,1,0:T(8,128)(2,1)S(1)}, bf16[6,128,128]{2,1,0:T(8,128)(2,1)S(1)}, u32[]{:S(2)}, u32[]{:S(2)}) collective-permute-start(bf16[6,128,128]{2,1,0:T(8,128)(2,1)S(1)} %get-tuple-element.56), channel_id=1, source_target_pairs={{0,8},{8,0},{1,9},{9,1},{2,10},{10,2},{3,11},{11,3},{4,12},{12,4},... | collective-permute-start | bytes 589832 | tf_op jit(solution)/shard_map/ppermute | solution.py:456
  72.0 2.5 %inside_part.1 = (bf16[12,128,128]{2,1,0:T(8,128)(2,1)S(1)}, f32[128,1536]{1,0:T(8,128)S(1)}) custom-call(s32[1,16]{1,0:T(1,128)S(1)} %copy-done.4, bf16[128,1536]{1,0:T(8,128)(2,1)S(1)} %bitcast.44, bf16[128,1536]{1,0:T(8,128)(2,1)S(1)} %bitcast.49, bf16[128,1536]{1,0:T(8,128)(2,1)S(1)} %bitcast.53), custom_call_target="tpu_custom_call" | custom-call | flops 100000000 | bytes 2400000 | tf_op jit(solution)/shard_map/inside_part/pallas_call | solution.py:216
  74.5 1.0 mixed_part.1
  75.5 2.2 %grad_mixed_part.1 = (bf16[128,1536]{1,0:T(8,128)(2,1)S(1)}, bf16[6,128,128]{2,1,0:T(8,128)(2,1)S(1)}, bf16[6,128,128]{2,1,0:T(8,128)(2,1)S(1)}) custom-call(s32[1,16]{1,0:T(1,128)S(1)} %copy-done.4, f32[1536,128]{1,0:T(8,128)S(1)} %get-tuple-element.34.own_ref, bf16[1536,128]{1,0:T(8,128)(2,1)S(1)} %collective-permute-done.5.got_ref, ...), custom_call_target="tpu_custom_call" | custom-call | flops 60000000 | bytes 4000000 | tf_op jit(solution)/shard_map/grad_mixed_part/pallas_call | solution.py:347
  77.7 2.4 %collective-permute-start.13 = (bf16[6,128,128]{2,1,0:T(8,128)(2,1)S(1)}, bf16[6,128,128]{2,1,0:T(8,128)(2,1)S(1)}, u32[]{:S(2)}, u32[]{:S(2)}) collective-permute-start(bf16[6,128,128]{2,1,0:T(8,128)(2,1)S(1)} %get-tuple-element.48), channel_id=1, source_target_pairs={{0,8},{8,0},{1,9},{9,1},{2,10},{10,2},{3,11},{11,3},{4,12},{12,4},... | collective-permute-start | bytes 589832 | tf_op jit(solution)/shard_map/ppermute | solution.py:456
  80.1 1.0 collective-permute-done.13
  81.2 0.1 fusion.9
  81.2 2.8 %collective-permute-start.14 = (bf16[6,128,128]{2,1,0:T(8,128)(2,1)S(1)}, bf16[6,128,128]{2,1,0:T(8,128)(2,1)S(1)}, u32[]{:S(2)}, u32[]{:S(2)}) collective-permute-start(bf16[6,128,128]{2,1,0:T(8,128)(2,1)S(1)} %fusion.9), channel_id=1, source_target_pairs={{16,0},{24,8},{32,16},{40,24},{48,32},{56,40},{64,48},{72,56},{80,... | collective-permute-start | bytes 589832 | tf_op jit(solution)/shard_map/ppermute | solution.py:462
  84.1 2.3 %collective-permute-start.11 = (bf16[128,1536]{1,0:T(8,128)(2,1)S(1)}, bf16[128,1536]{1,0:T(8,128)(2,1)S(1)}, u32[]{:S(2)}, u32[]{:S(2)}) collective-permute-start(bf16[128,1536]{1,0:T(8,128)(2,1)S(1)} %get-tuple-element.45.scaled_ref), channel_id=1, source_target_pairs={{0,8},{8,0},{1,9},{9,1},{2,10},{10,2},{3,11},{11,3},{4,12},{12,4},... | collective-permute-start | bytes 1179656 | tf_op jit(solution)/shard_map/ppermute | solution.py:456
  86.4 6.3 %collective-permute-done.14 = bf16[6,128,128]{2,1,0:T(8,128)(2,1)S(1)} collective-permute-done((bf16[6,128,128]{2,1,0:T(8,128)(2,1)S(1)}, bf16[6,128,128]{2,1,0:T(8,128)(2,1)S(1)}, u32[]{:S(2)}, u32[]{:S(2)}) %collective-permute-start.14) | collective-permute-done | bytes 196640 | tf_op jit(solution)/shard_map/ppermute | solution.py:462
  92.7 0.1 add_convert_fusion
  92.8 1.9 %collective-permute-start.16 = (bf16[6,128,128]{2,1,0:T(8,128)(2,1)S(1)}, bf16[6,128,128]{2,1,0:T(8,128)(2,1)S(1)}, u32[]{:S(2)}, u32[]{:S(2)}) collective-permute-start(bf16[6,128,128]{2,1,0:T(8,128)(2,1)S(1)} %add_convert_fusion), channel_id=1, source_target_pairs={{48,0},{56,8},{64,16},{72,24},{80,32},{88,40},{96,48},{104,56},{11... | collective-permute-start | bytes 589832 | tf_op jit(solution)/shard_map/ppermute | solution.py:462
  94.7 1.9 %collective-permute-start.15 = (bf16[6,128,128]{2,1,0:T(8,128)(2,1)S(1)}, bf16[6,128,128]{2,1,0:T(8,128)(2,1)S(1)}, u32[]{:S(2)}, u32[]{:S(2)}) collective-permute-start(bf16[6,128,128]{2,1,0:T(8,128)(2,1)S(1)} %add_convert_fusion), channel_id=1, source_target_pairs={{16,0},{24,8},{32,16},{40,24},{48,32},{56,40},{64,48},{72,56},{80,... | collective-permute-start | bytes 589832 | tf_op jit(solution)/shard_map/ppermute | solution.py:462
  96.6 1.2 %output_part.1 = (bf16[128,1024]{1,0:T(8,128)(2,1)S(1)}, bf16[128,1024]{1,0:T(8,128)(2,1)S(1)}) custom-call(bf16[128,1536]{1,0:T(8,128)(2,1)S(1)} %get-tuple-element.45.scaled_ref, bf16[128,1536]{1,0:T(8,128)(2,1)S(1)} %collective-permute-done.11.scaled_got_ref, bf16[384,1024]{1,0:T(8,128)(2,1)S(1)} %constant_dynamic-update-slice_fusion.refs_0_, ...), custom_call_target="tpu_custom_call" | custom-call | flops 810000000 | bytes 5000000 | tf_op jit(solution)/shard_map/output_part/pallas_call | solution.py:373
  97.9 3.1 %collective-permute-start.12 = (bf16[128,1024]{1,0:T(8,128)(2,1)S(1)}, bf16[128,1024]{1,0:T(8,128)(2,1)S(1)}, u32[]{:S(2)}, u32[]{:S(2)}) collective-permute-start(bf16[128,1024]{1,0:T(8,128)(2,1)S(1)} %get-tuple-element.47), channel_id=1, source_target_pairs={{0,8},{8,0},{1,9},{9,1},{2,10},{10,2},{3,11},{11,3},{4,12},{12,4},... | collective-permute-start | bytes 786440 | tf_op jit(solution)/shard_map/ppermute | solution.py:456
  100.9 1.1 collective-permute-done.16
  102.1 3.1 %collective-permute-done.15 = bf16[6,128,128]{2,1,0:T(8,128)(2,1)S(1)} collective-permute-done((bf16[6,128,128]{2,1,0:T(8,128)(2,1)S(1)}, bf16[6,128,128]{2,1,0:T(8,128)(2,1)S(1)}, u32[]{:S(2)}, u32[]{:S(2)}) %collective-permute-start.15) | collective-permute-done | bytes 196640 | tf_op jit(solution)/shard_map/ppermute | solution.py:462
  105.2 0.2 fusion.11
  105.4 3.9 %collective-permute-start.17 = (bf16[6,128,128]{2,1,0:T(8,128)(2,1)S(1)}, bf16[6,128,128]{2,1,0:T(8,128)(2,1)S(1)}, u32[]{:S(2)}, u32[]{:S(2)}) collective-permute-start(bf16[6,128,128]{2,1,0:T(8,128)(2,1)S(1)} %get-tuple-element.54), channel_id=1, source_target_pairs={{0,8},{8,0},{1,9},{9,1},{2,10},{10,2},{3,11},{11,3},{4,12},{12,4},... | collective-permute-start | bytes 589832 | tf_op jit(solution)/shard_map/ppermute | solution.py:456
  109.3 4.0 %grads_part.1 = (bf16[128,1536]{1,0:T(8,128)(2,1)}, f32[128,1536]{1,0:T(8,128)S(1)}, f32[128,1536]{1,0:T(8,128)S(1)}) custom-call(s32[1,16]{1,0:T(1,128)S(1)} %copy-done.4, bf16[128,1536]{1,0:T(8,128)(2,1)S(1)} %bitcast.47, bf16[128,1536]{1,0:T(8,128)(2,1)S(1)} %bitcast.50, bf16[128,1536]{1,0:T(8,128)(2,1)S(1)} %bitcast.54, ...), custom_call_target="tpu_custom_call" | custom-call | flops 250000000 | bytes 5000000 | tf_op jit(solution)/shard_map/grads_part/pallas_call | solution.py:409
  113.3 2.1 %last_part.1 = (bf16[128,1536]{1,0:T(8,128)(2,1)}, bf16[128,1536]{1,0:T(8,128)(2,1)}, bf16[128,2048]{1,0:T(8,128)(2,1)}) custom-call(s32[1,16]{1,0:T(1,128)S(1)} %copy-done.4, bf16[128,1536]{1,0:T(8,128)(2,1)S(1)} %bitcast.51, bf16[128,1536]{1,0:T(8,128)(2,1)S(1)} %bitcast.55, f32[128,1536]{1,0:T(8,128)S(1)} %get-tuple-element.43.dk_part_ref, ...), custom_call_target="tpu_custom_call" | custom-call | flops 100000000 | bytes 4500000 | tf_op jit(solution)/shard_map/last_part/pallas_call | solution.py:444
  (22 shorter events, 0.1 us)
Async XLA Ops:
  2.7 10.5 %collective-permute-start.1 = (bf16[192,1024]{1,0:T(8,128)(2,1)}, bf16[192,1024]{1,0:T(8,128)(2,1)S(1)}, u32[]{:S(2)}, u32[]{:S(2)}) collective-permute-start(bf16[192,1024]{1,0:T(8,128)(2,1)} %get-tuple-element.31), channel_id=1, source_target_pairs={{0,1},{1,0},{2,3},{3,2},{4,5},{5,4},{6,7},{7,6},{8,15},{9,10},{10,... | collective-permute-start | bytes 1179656 | tf_op jit(solution)/shard_map/ppermute | solution.py:471
  8.9 22.0 %copy-start.1 = (bf16[1,128,1536]{2,1,0:T(8,128)(2,1)S(1)}, bf16[1,128,1536]{2,1,0:T(8,128)(2,1)}, u32[]{:S(2)}) copy-start(bf16[1,128,1536]{2,1,0:T(8,128)(2,1)} %param.8) | copy-start | bytes 1179652
  8.9 22.0 %copy-start.2 = (bf16[1,128,1536]{2,1,0:T(8,128)(2,1)S(1)}, bf16[1,128,1536]{2,1,0:T(8,128)(2,1)}, u32[]{:S(2)}) copy-start(bf16[1,128,1536]{2,1,0:T(8,128)(2,1)} %param.9) | copy-start | bytes 1179652
  13.2 13.0 %collective-permute-start.2 = (bf16[384,1024]{1,0:T(8,128)(2,1)S(1)}, bf16[384,1024]{1,0:T(8,128)(2,1)S(1)}, u32[]{:S(2)}, u32[]{:S(2)}) collective-permute-start(bf16[384,1024]{1,0:T(8,128)(2,1)S(1)} %constant_dynamic-update-slice_fusion.refs_0_), channel_id=1, source_target_pairs={{0,7},{1,2},{2,1},{3,4},{4,3},{5,6},{6,5},{7,0},{8,9},{9,8},{10,11... | collective-permute-start | bytes 2359304 | tf_op jit(solution)/shard_map/ppermute | solution.py:471
  26.3 13.9 %collective-permute-start.3 = (bf16[384,1024]{1,0:T(8,128)(2,1)S(1)}, bf16[384,1024]{1,0:T(8,128)(2,1)S(1)}, u32[]{:S(2)}, u32[]{:S(2)}) collective-permute-start(bf16[384,1024]{1,0:T(8,128)(2,1)S(1)} %collective-permute-done.2.refs_1_), channel_id=1, source_target_pairs={{0,1},{1,0},{2,3},{3,2},{4,5},{5,4},{6,7},{7,6},{8,15},{9,10},{10,... | collective-permute-start | bytes 2359304 | tf_op jit(solution)/shard_map/ppermute | solution.py:471
  30.8 0.7 copy-start.4
  32.8 9.3 %collective-permute-start.6 = (bf16[6,128,128]{2,1,0:T(8,128)(2,1)S(1)}, bf16[6,128,128]{2,1,0:T(8,128)(2,1)S(1)}, u32[]{:S(2)}, u32[]{:S(2)}) collective-permute-start(bf16[6,128,128]{2,1,0:T(8,128)(2,1)S(1)} %get-tuple-element.38), channel_id=1, source_target_pairs={{0,8},{8,0},{1,9},{9,1},{2,10},{10,2},{3,11},{11,3},{4,12},{12,4},... | collective-permute-start | bytes 589832 | tf_op jit(solution)/shard_map/ppermute | solution.py:456
  40.2 23.7 %collective-permute-start.4 = (bf16[384,1024]{1,0:T(8,128)(2,1)S(1)}, bf16[384,1024]{1,0:T(8,128)(2,1)S(1)}, u32[]{:S(2)}, u32[]{:S(2)}) collective-permute-start(bf16[384,1024]{1,0:T(8,128)(2,1)S(1)} %collective-permute-done.3.refs_2_), channel_id=1, source_target_pairs={{0,7},{1,2},{2,1},{3,4},{4,3},{5,6},{6,5},{7,0},{8,9},{9,8},{10,11... | collective-permute-start | bytes 2359304 | tf_op jit(solution)/shard_map/ppermute | solution.py:471
  42.1 5.2 %copy-start.6 = (bf16[128,1024]{1,0:T(8,128)(2,1)S(1)}, bf16[128,1024]{1,0:T(8,128)(2,1)}, u32[]{:S(2)}) copy-start(bf16[128,1024]{1,0:T(8,128)(2,1)} %get-tuple-element.30) | copy-start | bytes 786436
  42.2 12.9 %collective-permute-start.7 = (bf16[6,128,128]{2,1,0:T(8,128)(2,1)S(1)}, bf16[6,128,128]{2,1,0:T(8,128)(2,1)S(1)}, u32[]{:S(2)}, u32[]{:S(2)}) collective-permute-start(bf16[6,128,128]{2,1,0:T(8,128)(2,1)S(1)} %fusion.3), channel_id=1, source_target_pairs={{0,16},{8,24},{16,32},{24,40},{32,48},{40,56},{48,64},{56,72},{64,... | collective-permute-start | bytes 589832 | tf_op jit(solution)/shard_map/ppermute | solution.py:462
  47.4 15.3 %collective-permute-start = (bf16[128,1024]{1,0:T(8,128)(2,1)S(1)}, bf16[128,1024]{1,0:T(8,128)(2,1)S(1)}, u32[]{:S(2)}, u32[]{:S(2)}) collective-permute-start(bf16[128,1024]{1,0:T(8,128)(2,1)S(1)} %copy-done.6), channel_id=1, source_target_pairs={{0,8},{8,0},{1,9},{9,1},{2,10},{10,2},{3,11},{11,3},{4,12},{12,4},... | collective-permute-start | bytes 786440 | tf_op jit(solution)/shard_map/ppermute | solution.py:456
  55.1 7.5 %copy-start.3 = (bf16[128,1024]{1,0:T(8,128)(2,1)S(1)}, bf16[128,1024]{1,0:T(8,128)(2,1)}, u32[]{:S(2)}) copy-start(bf16[128,1024]{1,0:T(8,128)(2,1)} %get-tuple-element.29.cot_keep_ref) | copy-start | bytes 786436
  55.2 14.5 %collective-permute-start.9 = (bf16[6,128,128]{2,1,0:T(8,128)(2,1)S(1)}, bf16[6,128,128]{2,1,0:T(8,128)(2,1)S(1)}, u32[]{:S(2)}, u32[]{:S(2)}) collective-permute-start(bf16[6,128,128]{2,1,0:T(8,128)(2,1)S(1)} %add_convert_fusion.1), channel_id=1, source_target_pairs={{0,48},{8,56},{16,64},{24,72},{32,80},{40,88},{48,96},{56,104},{64... | collective-permute-start | bytes 589832 | tf_op jit(solution)/shard_map/ppermute | solution.py:462
  58.4 11.4 %collective-permute-start.8 = (bf16[6,128,128]{2,1,0:T(8,128)(2,1)S(1)}, bf16[6,128,128]{2,1,0:T(8,128)(2,1)S(1)}, u32[]{:S(2)}, u32[]{:S(2)}) collective-permute-start(bf16[6,128,128]{2,1,0:T(8,128)(2,1)S(1)} %add_convert_fusion.1), channel_id=1, source_target_pairs={{0,16},{8,24},{16,32},{24,40},{32,48},{40,56},{48,64},{56,72},{64,... | collective-permute-start | bytes 589832 | tf_op jit(solution)/shard_map/ppermute | solution.py:462
  64.4 11.1 %collective-permute-start.5 = (bf16[1536,128]{1,0:T(8,128)(2,1)S(1)}, bf16[1536,128]{1,0:T(8,128)(2,1)S(1)}, u32[]{:S(2)}, u32[]{:S(2)}) collective-permute-start(bf16[1536,128]{1,0:T(8,128)(2,1)S(1)} %get-tuple-element.35), channel_id=1, source_target_pairs={{0,8},{8,0},{1,9},{9,1},{2,10},{10,2},{3,11},{11,3},{4,12},{12,4},... | collective-permute-start | bytes 1179656 | tf_op jit(solution)/shard_map/ppermute | solution.py:456
  69.8 2.2 %copy-start.5 = (f32[1536]{0:T(1024)S(1)}, f32[1536]{0:T(1024)}, u32[]{:S(2)}) copy-start(f32[1536]{0:T(1024)} %param.11) | copy-start | bytes 18436
  69.8 2.2 %copy-start = (bf16[1,128,1536]{2,1,0:T(8,128)(2,1)S(1)}, bf16[1,128,1536]{2,1,0:T(8,128)(2,1)}, u32[]{:S(2)}) copy-start(bf16[1,128,1536]{2,1,0:T(8,128)(2,1)} %param.7) | copy-start | bytes 1179652
  70.0 4.5 %collective-permute-start.10 = (bf16[6,128,128]{2,1,0:T(8,128)(2,1)S(1)}, bf16[6,128,128]{2,1,0:T(8,128)(2,1)S(1)}, u32[]{:S(2)}, u32[]{:S(2)}) collective-permute-start(bf16[6,128,128]{2,1,0:T(8,128)(2,1)S(1)} %get-tuple-element.56), channel_id=1, source_target_pairs={{0,8},{8,0},{1,9},{9,1},{2,10},{10,2},{3,11},{11,3},{4,12},{12,4},... | collective-permute-start | bytes 589832 | tf_op jit(solution)/shard_map/ppermute | solution.py:456
  77.7 3.5 %collective-permute-start.13 = (bf16[6,128,128]{2,1,0:T(8,128)(2,1)S(1)}, bf16[6,128,128]{2,1,0:T(8,128)(2,1)S(1)}, u32[]{:S(2)}, u32[]{:S(2)}) collective-permute-start(bf16[6,128,128]{2,1,0:T(8,128)(2,1)S(1)} %get-tuple-element.48), channel_id=1, source_target_pairs={{0,8},{8,0},{1,9},{9,1},{2,10},{10,2},{3,11},{11,3},{4,12},{12,4},... | collective-permute-start | bytes 589832 | tf_op jit(solution)/shard_map/ppermute | solution.py:456
  81.2 11.4 %collective-permute-start.14 = (bf16[6,128,128]{2,1,0:T(8,128)(2,1)S(1)}, bf16[6,128,128]{2,1,0:T(8,128)(2,1)S(1)}, u32[]{:S(2)}, u32[]{:S(2)}) collective-permute-start(bf16[6,128,128]{2,1,0:T(8,128)(2,1)S(1)} %fusion.9), channel_id=1, source_target_pairs={{16,0},{24,8},{32,16},{40,24},{48,32},{56,40},{64,48},{72,56},{80,... | collective-permute-start | bytes 589832 | tf_op jit(solution)/shard_map/ppermute | solution.py:462
  84.1 12.5 %collective-permute-start.11 = (bf16[128,1536]{1,0:T(8,128)(2,1)S(1)}, bf16[128,1536]{1,0:T(8,128)(2,1)S(1)}, u32[]{:S(2)}, u32[]{:S(2)}) collective-permute-start(bf16[128,1536]{1,0:T(8,128)(2,1)S(1)} %get-tuple-element.45.scaled_ref), channel_id=1, source_target_pairs={{0,8},{8,0},{1,9},{9,1},{2,10},{10,2},{3,11},{11,3},{4,12},{12,4},... | collective-permute-start | bytes 1179656 | tf_op jit(solution)/shard_map/ppermute | solution.py:456
  92.8 9.3 %collective-permute-start.16 = (bf16[6,128,128]{2,1,0:T(8,128)(2,1)S(1)}, bf16[6,128,128]{2,1,0:T(8,128)(2,1)S(1)}, u32[]{:S(2)}, u32[]{:S(2)}) collective-permute-start(bf16[6,128,128]{2,1,0:T(8,128)(2,1)S(1)} %add_convert_fusion), channel_id=1, source_target_pairs={{48,0},{56,8},{64,16},{72,24},{80,32},{88,40},{96,48},{104,56},{11... | collective-permute-start | bytes 589832 | tf_op jit(solution)/shard_map/ppermute | solution.py:462
  94.7 10.5 %collective-permute-start.15 = (bf16[6,128,128]{2,1,0:T(8,128)(2,1)S(1)}, bf16[6,128,128]{2,1,0:T(8,128)(2,1)S(1)}, u32[]{:S(2)}, u32[]{:S(2)}) collective-permute-start(bf16[6,128,128]{2,1,0:T(8,128)(2,1)S(1)} %add_convert_fusion), channel_id=1, source_target_pairs={{16,0},{24,8},{32,16},{40,24},{48,32},{56,40},{64,48},{72,56},{80,... | collective-permute-start | bytes 589832 | tf_op jit(solution)/shard_map/ppermute | solution.py:462
  97.9 15.5 %collective-permute-start.12 = (bf16[128,1024]{1,0:T(8,128)(2,1)S(1)}, bf16[128,1024]{1,0:T(8,128)(2,1)S(1)}, u32[]{:S(2)}, u32[]{:S(2)}) collective-permute-start(bf16[128,1024]{1,0:T(8,128)(2,1)S(1)} %get-tuple-element.47), channel_id=1, source_target_pairs={{0,8},{8,0},{1,9},{9,1},{2,10},{10,2},{3,11},{11,3},{4,12},{12,4},... | collective-permute-start | bytes 786440 | tf_op jit(solution)/shard_map/ppermute | solution.py:456
  105.4 7.9 %collective-permute-start.17 = (bf16[6,128,128]{2,1,0:T(8,128)(2,1)S(1)}, bf16[6,128,128]{2,1,0:T(8,128)(2,1)S(1)}, u32[]{:S(2)}, u32[]{:S(2)}) collective-permute-start(bf16[6,128,128]{2,1,0:T(8,128)(2,1)S(1)} %get-tuple-element.54), channel_id=1, source_target_pairs={{0,8},{8,0},{1,9},{9,1},{2,10},{10,2},{3,11},{11,3},{4,12},{12,4},... | collective-permute-start | bytes 589832 | tf_op jit(solution)/shard_map/ppermute | solution.py:456
